TPU v7x, 256 devices: a whole 4x4x8 slice. The times are simulated.
256 devices in a mesh: section: 8 (over x, z_hi), expert: 8 (over z_lo, core), tensor: 4 (over y).
Axes of the slice: x: 4, y: 4, z: 8 (z_hi: 2, z_lo: 4; z = z_hi * 4 + z_lo), core: 2. Of those that a mesh axis runs over, the one named last changes fastest.
Arguments:
- tokens: bfloat16 [512, 6144], P(('section', 'expert'), 'tensor'), may hold values from -6 to 6
- routes: int32 [512, 2], P(('section', 'expert')), may hold values from 0 to 7, all different within a row; in each aligned block of 8 rows (0 to 7, 8 to 15, ...) at most 4 rows name the same one
- router: float32 [6144, 8], replicated, may hold values from -0.18 to 0.18
- gate_proj: bfloat16 [8, 6144, 8192], P('expert', None, ('section', 'tensor')), may hold values from -0.078125 to 0.078125
- up_proj: bfloat16 [8, 6144, 8192], P('expert', None, ('section', 'tensor')), may hold values from -0.078125 to 0.078125
- down_proj: bfloat16 [8, 8192, 6144], P('expert', ('section', 'tensor')), may hold values from -0.125 to 0.125
- grad_out: bfloat16 [512, 6144], P(('section', 'expert'), 'tensor'), may hold values from -6 to 6
Outputs:
- moe_out: bfloat16 [512, 6144], P(('section', 'expert'), 'tensor')
- grad_tokens: bfloat16 [512, 6144], P(('section', 'expert'), 'tensor')
- grad_router: float32 [6144, 8], P('tensor')
Inputs may be any that keep to these rules, and one draw needn't show every extreme that they name: `routes`: each token names 2 different experts; in each aligned block of 8 tokens (the tokens of one group) no expert is named by more than 4 tokens, and in some blocks one expert is named by exactly 4.
All inputs are finite; a program needn't handle non-finite values.
Results may differ from a plain program's by a relative error of at most 0.02.
Values may be sent and summed in bfloat16 or wider, within the bound.
No kernel may reach another device: no remote copies, remote signals or barrier semaphores. Data moves between devices by JAX's collectives and lax.ppermute only.
A program may use at most 64 MiB of HBM per device.

v0:
```python
import jax
import jax.numpy as jnp
from jax import lax
from jax.sharding import PartitionSpec as P

precise = lax.Precision.HIGHEST


def route_table(routes, expert_count, capacity):
    flat_ids = routes.reshape(-1)
    expert_hot = (flat_ids[:, None] == jnp.arange(expert_count, dtype=jnp.int32)[None, :]).astype(
        jnp.float32
    )
    earlier = jnp.cumsum(expert_hot, axis=0) - expert_hot
    slot_ids = jnp.sum(earlier * expert_hot, axis=1).astype(jnp.int32)
    slot_hot = (slot_ids[:, None] == jnp.arange(capacity, dtype=jnp.int32)[None, :]).astype(
        jnp.float32
    )
    routing = expert_hot.T[:, None, :] * slot_hot.T[None, :, :]
    return routing.reshape(expert_count * capacity, flat_ids.shape[0])


def gate_weights(logits, routes):
    chosen = jnp.take_along_axis(logits, routes, axis=1)
    scores = jax.nn.sigmoid(chosen)
    totals = jnp.sum(scores, axis=1, keepdims=True)
    return (scores, scores / totals)


def expert_front(rows_x, gate_mat, up_mat):
    pre_gate = jnp.dot(rows_x, gate_mat, preferred_element_type=jnp.float32)
    pre_up = jnp.dot(rows_x, up_mat, preferred_element_type=jnp.float32)
    gate_sig = jax.nn.sigmoid(pre_gate)
    gate_act = pre_gate * gate_sig
    hidden = (gate_act * pre_up).astype(jnp.bfloat16)
    return (pre_gate, pre_up, gate_sig, gate_act, hidden)


def expert_grads(grad_hidden, pre_gate, pre_up, gate_sig, gate_act):
    grad_gate = (grad_hidden * pre_up * gate_sig * (1.0 + pre_gate * (1.0 - gate_sig))).astype(
        jnp.bfloat16
    )
    grad_up = (grad_hidden * gate_act).astype(jnp.bfloat16)
    return (grad_gate, grad_up)


def router_grads(grad_weight, scores, routes, expert_count):
    totals = scores[:, 0] + scores[:, 1]
    first = (grad_weight[:, 0] - grad_weight[:, 1]) * scores[:, 1] / (totals * totals)
    second = (grad_weight[:, 1] - grad_weight[:, 0]) * scores[:, 0] / (totals * totals)
    grad_scores = jnp.stack([first, second], axis=1)
    grad_chosen = grad_scores * scores * (1.0 - scores)
    expert_hot = (
        routes[:, :, None] == jnp.arange(expert_count, dtype=jnp.int32)[None, None, :]
    ).astype(jnp.float32)
    return jnp.sum(expert_hot * grad_chosen[:, :, None], axis=1)


def contract_last(left, right):
    return lax.dot_general(
        left, right, (((1,), (1,)), ((), ())), preferred_element_type=jnp.float32
    )


def on_device(tokens, routes, router, gate_proj, up_proj, down_proj, grad_out):
    tok_rows, quarter = tokens.shape
    tensor_count = lax.axis_size("tensor")
    expert_count = lax.axis_size("expert")
    top_count = routes.shape[1]
    capacity = 2 * tok_rows * top_count // expert_count
    block_rows = expert_count * capacity
    tensor_index = lax.axis_index("tensor")
    router_rows = lax.dynamic_slice_in_dim(router, tensor_index * quarter, quarter, 0)
    routing = route_table(routes, expert_count, capacity)
    gate_mat = gate_proj[0]
    up_mat = up_proj[0]
    down_mat = down_proj[0]
    send_x, send_dy = (tokens, grad_out)
    logits = lax.psum(jnp.dot(tokens.astype(jnp.float32), router_rows, precision=precise), "tensor")
    scores, weight = gate_weights(logits, routes)
    row_width = send_x.shape[1]
    x_sent = jnp.dot(
        routing, jnp.repeat(send_x.astype(jnp.float32), top_count, axis=0), precision=precise
    )
    x_sent = x_sent.astype(jnp.bfloat16).reshape(expert_count, capacity, row_width)
    scaled = jnp.repeat(send_dy.astype(jnp.float32), top_count, axis=0) * weight.reshape(-1, 1)
    dy_sent = (
        jnp.dot(routing, scaled, precision=precise)
        .astype(jnp.bfloat16)
        .reshape(expert_count, capacity, row_width)
    )

    def block_ids(count):
        return jnp.arange(count // block_rows, dtype=jnp.int32)

    def forward_block(hidden, block):
        section_at = block // tensor_count
        tensor_at = block % tensor_count
        hidden_rows = lax.dynamic_slice_in_dim(hidden, section_at * block_rows, block_rows, 0)
        columns = lax.dynamic_slice_in_dim(down_mat, tensor_at * quarter, quarter, 1)
        return jnp.dot(hidden_rows, columns, preferred_element_type=jnp.float32)

    def backward_block(grad_gate, grad_up, block):
        section_at = block // tensor_count
        tensor_at = block % tensor_count
        gate_rows = lax.dynamic_slice_in_dim(grad_gate, section_at * block_rows, block_rows, 0)
        up_rows = lax.dynamic_slice_in_dim(grad_up, section_at * block_rows, block_rows, 0)
        gate_part = lax.dynamic_slice_in_dim(gate_mat, tensor_at * quarter, quarter, 0)
        up_part = lax.dynamic_slice_in_dim(up_mat, tensor_at * quarter, quarter, 0)
        return contract_last(gate_rows, gate_part) + contract_last(up_rows, up_part)

    landed_x = lax.all_to_all(x_sent, "expert", split_axis=0, concat_axis=0, tiled=True)
    landed_x = lax.all_gather(landed_x, "tensor", axis=2, tiled=True)
    rows_x = lax.all_gather(landed_x.reshape(block_rows, -1), "section", axis=0, tiled=True)
    pre_gate, pre_up, gate_sig, gate_act, hidden = expert_front(rows_x, gate_mat, up_mat)
    summed_out = lax.psum_scatter(
        lax.map(
            lambda block: forward_block(hidden, block),
            block_ids(lax.axis_size(("section", "tensor")) * block_rows),
        )
        .reshape(lax.axis_size(("section", "tensor")) * block_rows, quarter)
        .astype(jnp.bfloat16),
        ("section", "tensor"),
        scatter_dimension=0,
        tiled=True,
    ).astype(jnp.float32)
    expert_out = lax.all_to_all(
        summed_out.reshape(expert_count, capacity, quarter).astype(jnp.bfloat16),
        "expert",
        split_axis=0,
        concat_axis=0,
        tiled=True,
    ).astype(jnp.float32)
    landed_dy = lax.all_to_all(dy_sent, "expert", split_axis=0, concat_axis=0, tiled=True)
    landed_dy = lax.all_gather(landed_dy, "tensor", axis=2, tiled=True)
    rows_dy = lax.all_gather(landed_dy.reshape(block_rows, -1), "section", axis=0, tiled=True)
    grad_hidden = contract_last(rows_dy, down_mat)
    grad_gate, grad_up = expert_grads(grad_hidden, pre_gate, pre_up, gate_sig, gate_act)
    summed_grad = lax.psum_scatter(
        lax.map(
            lambda block: backward_block(grad_gate, grad_up, block),
            block_ids(lax.axis_size(("section", "tensor")) * block_rows),
        )
        .reshape(lax.axis_size(("section", "tensor")) * block_rows, quarter)
        .astype(jnp.bfloat16),
        ("section", "tensor"),
        scatter_dimension=0,
        tiled=True,
    ).astype(jnp.float32)
    expert_grad = lax.all_to_all(
        summed_grad.reshape(expert_count, capacity, quarter).astype(jnp.bfloat16),
        "expert",
        split_axis=0,
        concat_axis=0,
        tiled=True,
    ).astype(jnp.float32)
    out_route = jnp.dot(
        routing.T, expert_out.reshape(block_rows, quarter), precision=precise
    ).reshape(tok_rows, top_count, quarter)
    grad_route = jnp.dot(
        routing.T, expert_grad.reshape(block_rows, quarter), precision=precise
    ).reshape(tok_rows, top_count, quarter)
    moe_out = jnp.sum(weight[:, :, None] * out_route, axis=1).astype(jnp.bfloat16)
    weight_part = jnp.sum(grad_out.astype(jnp.float32)[:, None, :] * out_route, axis=2)
    grad_weight = lax.psum(weight_part, "tensor")
    grad_logits = router_grads(grad_weight, scores, routes, expert_count)
    grad_tokens = (
        jnp.sum(grad_route, axis=1) + jnp.dot(grad_logits, router_rows.T, precision=precise)
    ).astype(jnp.bfloat16)
    router_part = jnp.dot(tokens.astype(jnp.float32).T, grad_logits, precision=precise)
    grad_router = lax.psum(router_part, ("section", "expert"))
    return (moe_out, grad_tokens, grad_router)


def solution(mesh):
    return jax.shard_map(
        on_device,
        mesh=mesh,
        in_specs=(
            P(("section", "expert"), "tensor"),
            P(("section", "expert"), None),
            P(),
            P("expert", None, ("section", "tensor")),
            P("expert", None, ("section", "tensor")),
            P("expert", ("section", "tensor"), None),
            P(("section", "expert"), "tensor"),
        ),
        out_specs=(
            P(("section", "expert"), "tensor"),
            P(("section", "expert"), "tensor"),
            P("tensor", None),
        ),
        check_vma=False,
    )
```

profile of v0, /device:TPU:1, one launch (start us, length us, event | category | flops | bytes accessed | tf_op | source)
XLA Modules:
  0.0 1151.5 jit_solution(11186698686855565210)
XLA Ops:
  9.6 12.7 %all_to_all.20 = bf16[8,4,1536]{2,1,0:T(4,128)(2,1)S(1)} all-to-all(bf16[8,4,1536]{2,1,0:T(4,128)(2,1)S(1)} %reshape.192), channel_id=1, replica_groups=mesh['section'=8,'expert'=8,'tensor'=4] {'expert'}, dimensions={0} | all-to-all | bytes 196608 | tf_op jit(solution)/shard_map/all_to_all | solution.py:112
  22.3 11.4 all_gather.12
  36.3 7.0 psum.21
  44.8 19.7 %all_to_all.21 = bf16[8,4,1536]{2,1,0:T(4,128)(2,1)S(1)} all-to-all(bf16[8,4,1536]{2,1,0:T(4,128)(2,1)S(1)} %reshape.195), channel_id=1, replica_groups=mesh['section'=8,'expert'=8,'tensor'=4] {'expert'}, dimensions={0} | all-to-all | bytes 196608 | tf_op jit(solution)/shard_map/all_to_all | solution.py:134
  64.5 10.7 all_gather.14
  76.1 53.4 %all-gather.3.cloned.1.call-done = bf16[256,6144]{1,0:T(8,128)(2,1)} async-done(((bf16[32,6144]{1,0:T(8,128)(2,1)}), bf16[256,6144]{1,0:T(8,128)(2,1)}) %all-gather.3.cloned.1.call-update) | async-done | bytes 3145744 | tf_op jit(solution)/shard_map/all_gather | solution.py:114
  129.5 4.7 fusion.29
  134.2 1.7 fusion.31
  135.9 83.3 %all-gather.5.cloned.1.call-done = bf16[256,6144]{1,0:T(8,128)(2,1)} async-done(((bf16[32,6144]{1,0:T(8,128)(2,1)}), bf16[256,6144]{1,0:T(8,128)(2,1)}) %all-gather.5.cloned.1.call-update) | async-done | bytes 3145744 | tf_op jit(solution)/shard_map/all_gather | solution.py:136
  219.2 4.6 multiply_convert_fusion
  224.1 147.5 %while.24 = (s32[]{:T(128)}, bf16[32,32,1536]{2,1,0:T(8,128)(2,1)S(1)}, s32[32]{0:T(128)S(1)}, bf16[256,256]{1,0:T(8,128)(2,1)}, bf16[256,6144]{1,0:T(8,128)(2,1...) while((s32[]{:T(128)}, ...), condition=%wide.region_5.6_spmd, body=%wide.region_4.5_spmd.sunk | while | flops 25165852 | bytes 999876 | solution.py:117
  371.6 1.7 copy-done.2
  373.7 198.6 %while.25 = (s32[]{:T(128)}, bf16[32,32,1536]{2,1,0:T(8,128)(2,1)S(1)}, s32[32]{0:T(128)S(1)}, bf16[256,256]{1,0:T(8,128)(2,1)}, bf16[6144,256]{1,0:T(8,128)(2,1...) while((s32[]{:T(128)}, ...), condition=%wide.region_9.10_spmd, body=%wide.region_8.9_spmd.sunk | while | flops 50380828 | bytes 2195932 | solution.py:140
  397.1 1.5 fusion.64
  403.3 1.5 fusion.64
  420.4 1.5 fusion.63
  428.1 1.5 fusion.64
  446.7 1.5 fusion.64
  451.5 1.5 fusion.63
  459.2 1.5 fusion.64
  471.6 1.5 fusion.64
  533.6 1.5 fusion.64
  546.0 1.5 fusion.64
  572.4 1.7 copy-done.1
  574.1 51.4 %reduce-scatter.3.cloned.1.call-done = bf16[32,1536]{1,0:T(8,128)(2,1)} async-done(((bf16[1024,1536]{1,0:T(8,128)(2,1)}), bf16[32,1536]{1,0:T(8,128)(2,1)}) %reduce-scatter.3.cloned.1.call-update) | async-done | bytes 98320 | tf_op jit(solution)/shard_map/reduce_scatter | solution.py:116
  625.5 1.5 convert_element_type.89
  627.1 6.6 all-to-all-start.1
  633.7 250.7 %reduce-scatter.5.cloned.1.call-done = bf16[32,1536]{1,0:T(8,128)(2,1)} async-done(((bf16[1024,1536]{1,0:T(8,128)(2,1)}), bf16[32,1536]{1,0:T(8,128)(2,1)}) %reduce-scatter.5.cloned.1.call-update) | async-done | bytes 98320 | tf_op jit(solution)/shard_map/reduce_scatter | solution.py:139
  884.4 1.6 convert_element_type.97
  886.0 6.6 all-to-all-start.3
  893.4 6.8 psum.22
  900.5 243.5 %psum.23 = f32[1536,8]{0,1:T(8,128)} all-reduce(f32[1536,8]{0,1:T(8,128)S(1)} %convolution_bitcast_fusion.1), channel_id=1, replica_groups=mesh['section'=8,'expert'=8,'tensor'=4] {'section','expert'}, use_global_device_ids=true, to_apply=%region_15.16 | all-reduce | flops 12288 | bytes 98304 | tf_op jit(solution)/shard_map/psum | solution.py:171
  (218 shorter events, 172.9 us)
Async XLA Ops:
  7.2 28.3 %copy-start = (f32[6144,8]{0,1:T(8,128)S(1)}, f32[6144,8]{0,1:T(8,128)}, u32[]{:S(2)}) copy-start(f32[6144,8]{0,1:T(8,128)} %param.13) | copy-start | bytes 589828
  7.2 122.3 %all-gather.3.cloned.1.call-start = ((), (), s32[]{:S(2)}) async-start(), calls=%async_computation.6 | async-start | bytes 3538944 | tf_op jit(solution)/shard_map/all_gather | solution.py:114
  9.6 34.5 %copy-start.5 = (bf16[8,1536]{1,0:T(8,128)(2,1)S(1)}, bf16[8,1536]{1,0:T(8,128)(2,1)}, u32[]{:S(2)}) copy-start(bf16[8,1536]{1,0:T(8,128)(2,1)} %param.17) | copy-start | bytes 73732
  9.6 34.5 %copy-start.6 = (s32[8,2]{0,1:T(2,128)S(1)}, s32[8,2]{0,1:T(2,128)}, u32[]{:S(2)}) copy-start(s32[8,2]{0,1:T(2,128)} %param.12) | copy-start | bytes 196
  34.6 184.6 %all-gather.5.cloned.1.call-start = ((), (), s32[]{:S(2)}) async-start(), calls=%async_computation.8 | async-start | bytes 3538944 | tf_op jit(solution)/shard_map/all_gather | solution.py:136
  76.0 549.5 %reduce-scatter.3.cloned.1.call-start = ((), (), s32[]{:S(2)}) async-start(), calls=%async_computation.7 | async-start | bytes 3244032 | tf_op jit(solution)/shard_map/reduce_scatter | solution.py:116
  76.1 58.1 %copy-start.3 = (bf16[1,6144,256]{2,1,0:T(8,128)(2,1)S(1)}, bf16[1,6144,256]{2,1,0:T(8,128)(2,1)}, u32[]{:S(2)}) copy-start(bf16[1,6144,256]{2,1,0:T(8,128)(2,1)} %param.14) | copy-start | bytes 9437188
  129.5 4.7 copy-start.7
  371.6 1.7 copy-start.2
  373.3 511.1 %reduce-scatter.5.cloned.1.call-start = ((), (), s32[]{:S(2)}) async-start(), calls=%async_computation.9 | async-start | bytes 3244032 | tf_op jit(solution)/shard_map/reduce_scatter | solution.py:139
  572.4 1.7 copy-start.1
  572.4 327.9 %copy-start.4 = (bf16[8,1536]{1,0:T(8,128)(2,1)S(1)}, bf16[8,1536]{1,0:T(8,128)(2,1)}, u32[]{:S(2)}) copy-start(bf16[8,1536]{1,0:T(8,128)(2,1)} %param.11) | copy-start | bytes 73732
  627.1 258.9 %all-to-all-start.1 = ((bf16[8,4,1536]{2,1,0:T(4,128)(2,1)}), bf16[8,4,1536]{2,1,0:T(4,128)(2,1)S(1)}, u32[]{:S(2)}, u32[]{:S(2)}) async-start(bf16[8,4,1536]{2,1,0:T(4,128)(2,1)} %convert_element_type.89), calls=%async_computation.2 | async-start | bytes 196608 | tf_op jit(solution)/shard_map/all_to_all | solution.py:127
  886.0 258.0 %all-to-all-start.3 = ((bf16[8,4,1536]{2,1,0:T(4,128)(2,1)}), bf16[8,4,1536]{2,1,0:T(4,128)(2,1)S(1)}, u32[]{:S(2)}, u32[]{:S(2)}) async-start(bf16[8,4,1536]{2,1,0:T(4,128)(2,1)} %convert_element_type.97), calls=%async_computation.5 | async-start | bytes 196608 | tf_op jit(solution)/shard_map/all_to_all | solution.py:150
Sparse Core Ops, SparseCore 0:
  34.7 94.7 all-gather.2
  132.1 87.0 all-gather.4
  373.4 252.0 reduce-scatter.2
  631.6 252.7 reduce-scatter.4
where the time goes:
time: 1160 us; the launch traced here: 1150 us
  waiting for transfers between devices  439 us (38%)
  blocking collectives  312 us (27%)
  loops' own time  169 us (15%)
  matrix products  154 us (13%)
  local copies, waits for them, and re-layouts  50 us (4%)
  between operations  14 us (1%)
  starting transfers between devices  13.3 us (1%)
    reduce_scatter x1, waiting for transfers between devices, on_device(): lax.psum_scatter(lax.map(lambda block: backward_block(grad_gate, grad_up,...  251 us
    psum x1, blocking collectives, on_device(): grad_router = lax.psum(router_part, ('section', 'expert'))  244 us
    dot_general x65, matrix products, contract_last(): lax.dot_general(left, right, (((1,), (1,)), ((), ())), preferred_element_...  99.8 us
    another operation x1, loops' own time, on_device(): lax.map(lambda block: backward_block(grad_gate, grad_up, block), block_id...  84.7 us
    another operation x1, loops' own time, on_device(): lax.map(lambda block: forward_block(hidden, block), block_ids(lax.axis_si...  83.9 us
    all_gather x1, waiting for transfers between devices, on_device(): lax.all_gather(landed_dy.reshape(block_rows, -1), 'section', axis=0, tile...  83.3 us
    all_gather x1, waiting for transfers between devices, on_device(): lax.all_gather(landed_x.reshape(block_rows, -1), 'section', axis=0, tiled...  53.4 us
    reduce_scatter x1, waiting for transfers between devices, on_device(): lax.psum_scatter(lax.map(lambda block: forward_block(hidden, block), bloc...  51.4 us
  transfers between devices with their start and end apart: 6, of which 4 were waited for; matrix products, arithmetic and copies ran while one was open for 11% of the time, Pallas kernels for 0%

commit v1 on v0

v1 whole, which is shorter than its diff:
```python
import jax
import jax.numpy as jnp
from jax import lax
from jax.experimental import pallas as pl
from jax.experimental.pallas import tpu as pltpu
from jax.sharding import Mesh
from jax.sharding import PartitionSpec as P

F32 = jnp.float32
BF16 = jnp.bfloat16
ZAX = ("zh", "zl", "c")
EXP = ("zl", "c")
ALL = ("x", "zh", "zl", "c")
RING = 4
OFFS = (0, -1, 1, 2)
N_EXP = 8
CAP = 4
SLOTS = N_EXP * CAP
LANES = 128


def dot(a, b):
    return jnp.dot(a, b, preferred_element_type=F32)


def dot_t(a, b):
    return lax.dot_general(a, b, (((1,), (1,)), ((), ())), preferred_element_type=F32)


def shift(a, axis, n):
    return lax.ppermute(a, axis, [(i, (i + n) % RING) for i in range(RING)])


def sds(shape, dtype):
    return jax.ShapeDtypeStruct(shape, dtype)


VMEM = pl.BlockSpec(memory_space=pltpu.VMEM)
SMEM = pl.BlockSpec(memory_space=pltpu.SMEM)


def local(body, outs, *args, smem=0, limit=16, alias=None):
    return pl.pallas_call(
        body,
        out_shape=outs,
        in_specs=[SMEM] * smem + [VMEM] * (len(args) - smem),
        out_specs=jax.tree.map(lambda _: VMEM, outs),
        input_output_aliases=alias or {},
        compiler_params=pltpu.CompilerParams(vmem_limit_bytes=limit << 20),
    )(*args)


def ring_gather(a, axis):
    half = a.shape[0] // 2
    left = shift(a, axis, 1)
    right = shift(a, axis, -1)
    return a, left, right, shift(left[:half], axis, 1), shift(right[half:], axis, -1)


def add_body(right, up, left, down, right_out, left_out):
    half = up.shape[0]
    right_out[:half] = (right[:half].astype(F32) + up[...].astype(F32)).astype(BF16)
    right_out[half:] = right[half:]
    left_out[:half] = left[:half]
    left_out[half:] = (left[half:].astype(F32) + down[...].astype(F32)).astype(BF16)


def ring_reduce(own, left, right, far_t, far_b, axis):
    up = shift(far_t, axis, 1)
    down = shift(far_b, axis, -1)
    like = sds(right.shape, BF16)
    right, left = local(add_body, (like, like), right, up, left, down)
    return own, shift(right, axis, 1), shift(left, axis, -1)


def split3(a):
    hi = a.astype(BF16)
    rest = a - hi.astype(F32)
    mid = rest.astype(BF16)
    low = (rest - mid.astype(F32)).astype(BF16)
    return hi, mid, low


def rows_body(own, left, right, far, rows_out, meta_out):
    n, width = own.shape
    for i, r in enumerate((own, left, right, far)):
        rows_out[i * n : (i + 1) * n] = r[:, : width - LANES]
        meta_out[i * n : (i + 1) * n] = r[:, width - LANES :]


def lanes_body(parts, out):
    n, rows, width = parts.shape
    for i in range(n):
        out[:, i * width : (i + 1) * width] = parts[i]


def front_body(
    at, x0, x1, x2, x3t, x3b, d0, d1, d2, d3t, d3b, meta, gate, up, down, router,
    hidden_out, gg_out, gu_out, tl_out, gate_out,
):
    y_at, e_at = at[0], at[1]
    quarter = x0.shape[1]
    pre_gate = pre_up = logits3 = None
    for i, off in enumerate(OFFS):
        q = pl.multiple_of(((y_at + (off + RING)) % RING) * quarter, quarter)
        a = (x0[...], x1[...], x2[...])[i] if i < 3 else jnp.concatenate([x3t[...], x3b[...]], 0)
        rows = pl.ds(q, quarter)
        g, u, r = dot(a, gate[rows]), dot(a, up[rows]), dot(a, router[rows])
        pre_gate = g if i == 0 else pre_gate + g
        pre_up = u if i == 0 else pre_up + u
        logits3 = r if i == 0 else logits3 + r
    raw = None
    for k in range(RING):
        cols = slice(k * quarter, (k + 1) * quarter)
        a = jnp.concatenate([d0[:, cols], d1[:, cols], d2[:, cols], d3t[:, cols], d3b[:, cols]], 0)
        g = dot_t(a, down[:, cols])
        raw = g if k == 0 else raw + g
    lane = lax.broadcasted_iota(jnp.int32, logits3.shape, 1)
    inside = lane < 3 * N_EXP
    expert = lane % N_EXP
    code = meta[...].astype(F32).astype(jnp.int32)
    other = code // CAP
    hot_own = (expert == e_at) & inside
    hot_other = (expert == other) & inside
    logit_own = jnp.sum(jnp.where(hot_own, logits3, 0.0), 1, keepdims=True)
    logit_other = jnp.sum(jnp.where(hot_other, logits3, 0.0), 1, keepdims=True)
    score_own = jax.nn.sigmoid(logit_own)
    score_other = jax.nn.sigmoid(logit_other)
    total = score_own + score_other
    weight = score_own / total
    both = score_own * score_other / (total * total)
    c_own = both * (1.0 - score_own)
    c_other = both * (1.0 - score_other)
    gate_sig = jax.nn.sigmoid(pre_gate)
    gate_act = pre_gate * gate_sig
    hidden = gate_act * pre_up
    grad_weight = jnp.sum(hidden * raw, 1, keepdims=True)
    hidden_out[...] = (weight * hidden).astype(BF16)
    grad_hidden = weight * raw
    gg_out[...] = (
        grad_hidden * pre_up * gate_sig * (1.0 + pre_gate * (1.0 - gate_sig))
    ).astype(BF16)
    gu_out[...] = (grad_hidden * gate_act).astype(BF16)
    wide = lane < 4 * N_EXP
    to_logits = jnp.where((expert == e_at) & wide, grad_weight * c_own, 0.0) - jnp.where(
        (expert == other) & wide, grad_weight * c_other, 0.0
    )
    high = to_logits.astype(BF16).astype(F32)
    tl_out[...] = jnp.where((lane // N_EXP) % 2 == 0, high, to_logits - high).astype(BF16)
    gate_out[...] = jnp.where(lane == 0, grad_weight, jnp.where(lane == 1, c_own, 0.0))


def back_body(
    at, hidden, gg, gu, tl, gate, up, down, router,
    m0, m1, m2, m3t, m3b, g0, g1, g2, g3t, g3b,
):
    y_at = at[0]
    quarter = m0.shape[1]
    own = g0.shape[0]
    for i in (3, 1, 2, 0):
        q = pl.multiple_of(((y_at + (OFFS[i] + RING)) % RING) * quarter, quarter)
        v = dot(hidden[...], down[:, pl.ds(q, quarter)]).astype(BF16)
        if i == 3:
            half = m3t.shape[0]
            m3t[...] = v[:half]
            m3b[...] = v[half:]
        else:
            (m0, m1, m2)[i][...] = v
    step = 512
    for k in range(RING * quarter // step):
        at_k = slice(k * step, (k + 1) * step)
        v = dot_t(gg[...], gate[at_k]) + dot_t(gu[...], up[at_k]) + dot_t(tl[...], router[at_k])
        v = v.astype(BF16)
        g0[:, at_k] = v[:own]
        g1[:, at_k] = v[own : 2 * own]
        g2[:, at_k] = v[2 * own : 3 * own]
        g3t[:, at_k] = v[3 * own : 3 * own + own // 2]
        g3b[:, at_k] = v[3 * own + own // 2 :]


def sum_rows_body(a, b, c, o0, o1, o2, o3):
    n = o0.shape[0]
    for i, o in enumerate((o0, o1, o2, o3)):
        s = slice(i * n, (i + 1) * n)
        o[...] = (a[s].astype(F32) + b[s].astype(F32) + c[s].astype(F32)).astype(BF16)


def sum_lanes_body(a, b, c, out):
    n, rows, width = out.shape
    for i in range(n):
        s = slice(i * width, (i + 1) * width)
        out[i] = (a[:, s].astype(F32) + b[:, s].astype(F32) + c[:, s].astype(F32)).astype(BF16)


def on_device(tokens, routes, router, gate_proj, up_proj, down_proj, grad_out):
    rows, quarter = tokens.shape
    y_at = lax.axis_index("y")
    x_at = lax.axis_index("x")
    e_at = lax.axis_index(EXP)
    at = jnp.stack([y_at, e_at]).astype(jnp.int32)
    gate, up, down = gate_proj[0], up_proj[0], down_proj[0]
    width = RING * quarter

    flat = routes.reshape(-1)
    ids = jnp.arange(flat.shape[0], dtype=jnp.int32)
    same = (flat[:, None] == flat[None, :]) & (ids[None, :] < ids[:, None])
    slot = jnp.sum(same.astype(jnp.int32), axis=1)
    code = (flat * CAP + slot).reshape(rows, 2)
    lanes = jnp.arange(SLOTS, dtype=jnp.int32)
    hot = (code[:, :, None] == lanes[None, None, :]).astype(F32)
    pick_b = jnp.sum(hot, axis=1).astype(BF16)
    meta = jnp.sum(hot * code[:, ::-1, None].astype(F32), axis=(0, 1))

    def pack(a):
        return lax.dot_general(
            pick_b, a, (((0,), (0,)), ((), ())), preferred_element_type=F32
        ).astype(BF16)

    packed = jnp.concatenate(
        [pack(tokens), jnp.broadcast_to(meta[:, None], (SLOTS, LANES)).astype(BF16), pack(grad_out)], 1
    ).reshape(N_EXP, CAP, -1)
    got = lax.all_to_all(jnp.concatenate([packed, packed], 0), ZAX, 0, 0, tiled=True)
    got = got.reshape(2 * SLOTS, -1)
    got_x, got_dy = got[:, : quarter + LANES], got[:, quarter + LANES :]
    n_own = got.shape[0]
    n_rows = RING * n_own

    got_dy = lax.all_to_all(
        jnp.broadcast_to(got_dy, (RING, n_own, quarter)), "y", 0, 0, tiled=True
    )
    pieces = [got_x] + [shift(got_x, "x", n) for n in (1, -1, 2)]
    row_x, meta_all = local(
        rows_body, (sds((n_rows, quarter), BF16), sds((n_rows, LANES), BF16)), *pieces
    )
    row_dy = local(lanes_body, sds((n_own, width), BF16), got_dy)
    full_x = ring_gather(row_x, "y")
    full_dy = ring_gather(row_dy, "x")

    parts = split3(router)
    pad = jnp.zeros((width, LANES - 3 * N_EXP), BF16)
    router_in = jnp.concatenate([*parts, pad], 1)
    pad = jnp.zeros((width, LANES - 4 * N_EXP), BF16)
    router_out = jnp.concatenate([parts[0], parts[0], parts[1], parts[1], pad], 1)

    n_ff = gate.shape[1]
    act = sds((n_rows, n_ff), BF16)
    hidden, grad_gate, grad_up, to_logits, gates = local(
        front_body,
        (act, act, act, sds((n_rows, LANES), BF16), sds((n_rows, LANES), F32)),
        at, *full_x, *full_dy, meta_all, gate, up, down, router_in, smem=1,
    )
    far = sds((n_rows // 2, quarter), BF16)
    near = sds((n_rows, quarter), BF16)
    g_far = sds((n_own // 2, width), BF16)
    g_near = sds((n_own, width), BF16)
    parts = local(
        back_body,
        (near, near, near, far, far, g_near, g_near, g_near, g_far, g_far),
        at, hidden, grad_gate, grad_up, to_logits, gate, up, down, router_out, smem=1,
    )

    grad_weight, c_own = gates[:, 0], gates[:, 1:2]
    spots = (x_at + jnp.array(OFFS, dtype=jnp.int32) + RING) % RING
    place = (spots[:, None] == jnp.arange(RING, dtype=jnp.int32)[None, :]).astype(F32)
    gw_abs = jnp.sum(place[:, :, None] * grad_weight.reshape(RING, 1, n_own), 0).reshape(1, n_rows)
    n_shards = 2 * RING * RING
    gw_all = lax.all_to_all(
        jnp.broadcast_to(gw_abs, (n_shards, n_rows)).reshape(n_shards, 2, n_rows // 2),
        ("x", "zh", "y"), 0, 0, tiled=True,
    )
    gw_sum = jnp.sum(gw_all, 0)[None]
    gw_exp = lax.all_to_all(
        jnp.broadcast_to(gw_sum, (N_EXP, 2, n_rows // 2)), EXP, 0, 0, tiled=True
    ).reshape(N_EXP, n_rows // CAP, CAP)
    gw_group = gw_exp.transpose(1, 0, 2).reshape(RING, n_own // CAP, SLOTS)
    gw_group = jnp.sum(place[:, :, None, None] * gw_group[None], 1).reshape(n_rows // CAP, 1, SLOTS)
    gw_group = jnp.broadcast_to(gw_group, (n_rows // CAP, CAP, SLOTS)).reshape(n_rows, SLOTS)
    own_code = e_at * CAP + jnp.arange(n_rows, dtype=jnp.int32)[:, None] % CAP
    meta_int = meta_all[:, :1].astype(jnp.int32)
    pair_hot = (lanes[None, :] == own_code).astype(F32) - (lanes[None, :] == meta_int).astype(F32)
    grad_logit = c_own * jnp.sum(gw_group * pair_hot, 1, keepdims=True)
    gl_parts = jnp.concatenate(split3(grad_logit), 1)
    column = lax.dot_general(
        gl_parts, row_x, (((0,), (0,)), ((), ())), preferred_element_type=F32
    )
    column = jnp.sum(column, 0).reshape(1, quarter // LANES, LANES)
    columns = lax.all_to_all(
        jnp.broadcast_to(column, (N_EXP, quarter // LANES, LANES)), EXP, 0, 0, tiled=True
    )
    grad_router = columns.reshape(N_EXP, quarter).T

    out_terms = ring_reduce(*parts[:5], "y")
    grad_terms = ring_reduce(*parts[5:], "x")
    piece = sds((n_own, quarter), BF16)
    out_x = local(sum_rows_body, (piece,) * RING, *out_terms)
    grad_y = local(sum_lanes_body, sds((RING, n_own, quarter), BF16), *grad_terms)
    out_got = [out_x[0]] + [shift(out_x[i], "x", OFFS[i]) for i in (1, 2, 3)]
    out_own = sum(a.astype(F32) for a in out_got).astype(BF16)
    grad_got = lax.all_to_all(grad_y, "y", 0, 0, tiled=True)
    grad_own = jnp.sum(grad_got.astype(F32), 0).astype(BF16)

    final = jnp.concatenate([out_own, grad_own], 1).reshape(2 * N_EXP, CAP, -1)
    final = lax.all_to_all(final, ZAX, 0, 0, tiled=True).reshape(2 * SLOTS, -1)
    both = dot(jnp.concatenate([pick_b, pick_b], 1), final).astype(BF16)
    return (both[:, :quarter], both[:, quarter:], grad_router)


def solution(mesh):
    fine = Mesh(mesh.devices.reshape(4, 2, 4, 2, 4), ("x", "zh", "zl", "c", "y"))
    return jax.shard_map(
        on_device,
        mesh=fine,
        in_specs=(
            P(ALL, "y"),
            P(ALL, None),
            P(),
            P(EXP, None, ("x", "zh", "y")),
            P(EXP, None, ("x", "zh", "y")),
            P(EXP, ("x", "zh", "y"), None),
            P(ALL, "y"),
        ),
        out_specs=(P(ALL, "y"), P(ALL, "y"), P("y", None)),
        check_vma=False,
    )
```

time: 1160 us -> 238 us (0.21)
  waiting for transfers between devices: 439 us -> 66.8 us
  blocking collectives: 312 us -> 24.7 us
  loops' own time: 169 us -> 0 us
  matrix products: 154 us -> 1.59 us
  starting transfers between devices: 13.3 us -> 56.9 us
  Pallas kernels: 0 us -> 16.9 us
  between operations: 14 us -> 1 us
    reduce_scatter x2 -> x0, waiting for transfers between devices: 302 us -> none  [the longest x1 251 us: on_device(): lax.psum_scatter(lax.map(lambda block: backward_block(grad_gate, grad_up,...]
    psum x3 -> x0, blocking collectives: 257 us -> none  [the longest x1 244 us: on_device(): grad_router = lax.psum(router_part, ('section', 'expert'))]
    another operation x2 -> x0, loops' own time: 169 us -> none  [the longest x1 84.7 us: on_device(): lax.map(lambda block: backward_block(grad_gate, grad_up, block), block_id...]
    dot_general x106 -> x4, matrix products: 154 us -> 1.59 us  [the longest x2 1.16 us: pack(): lax.dot_general(pick_b, a, (((0,), (0,)), ((), ())), preferred_element_ty...]
    all_gather x2 -> x0, waiting for transfers between devices: 137 us -> none  [the longest x1 83.3 us: on_device(): lax.all_gather(landed_dy.reshape(block_rows, -1), 'section', axis=0, tile...]
    dynamic_slice x64 -> x0, local copies, waits for them, and re-layouts: 38.1 us -> none  [on_device(): lax.map(lambda block: forward_block(hidden, block), block_ids(lax.axis_si...]
    all_to_all x2 -> x6, waiting for transfers between devices: 0.01 us -> 36.4 us  [the longest x1 13.9 us: on_device(): final = lax.all_to_all(final, ZAX, 0, 0, tiled=True).reshape(2 * SLOTS, -1)]
    ppermute x0 -> x22, waiting for transfers between devices: none -> 30.4 us  [shift(): return lax.ppermute(a, axis, [(i, (i + n) % RING) for i in range(RING)])]
  transfers between devices with their start and end apart: 6 -> 28, of which waited for: 4 -> 9; matrix products, arithmetic and copies ran while one was open for 11% -> 17% of each run, Pallas kernels for 0% -> 3%
where the time goes in v1:
time: 238 us; the launch traced here: 236 us
  waiting for transfers between devices  66.8 us (28%)
  starting transfers between devices  56.9 us (24%)
  local copies, waits for them, and re-layouts  56.1 us (24%)
  blocking collectives  24.7 us (10%)
  Pallas kernels  16.9 us (7%)
  other arithmetic  12.4 us (5%)
    ppermute x22, waiting for transfers between devices, shift(): return lax.ppermute(a, axis, [(i, (i + n) % RING) for i in range(RING)])  30.4 us
    unnamed x81, local copies, waits for them, and re-layouts  28.7 us
    ppermute x22, starting transfers between devices, shift(): return lax.ppermute(a, axis, [(i, (i + n) % RING) for i in range(RING)])  25.1 us
    all_to_all x1, blocking collectives, on_device(): lax.all_to_all(jnp.concatenate([packed, packed], 0), ZAX, 0, 0, tiled=True)  24.7 us
    pallas_call x8, Pallas kernels, local(): pl.pallas_call(body, out_shape=outs, in_specs=[SMEM] * smem + [VMEM] * (l...  16.9 us
    all_to_all x1, waiting for transfers between devices, on_device(): final = lax.all_to_all(final, ZAX, 0, 0, tiled=True).reshape(2 * SLOTS, -1)  13.9 us
    all_to_all x1, waiting for transfers between devices, on_device(): lax.all_to_all(jnp.broadcast_to(gw_abs, (n_shards, n_rows)).reshape(n_sha...  11.1 us
    all_to_all x1, starting transfers between devices, on_device(): lax.all_to_all(jnp.broadcast_to(gw_sum, (N_EXP, 2, n_rows // 2)), EXP, 0,...  9.27 us
  transfers between devices with their start and end apart: 28, of which 9 were waited for; matrix products, arithmetic and copies ran while one was open for 17% of the time, Pallas kernels for 3%

profile of v1, /device:TPU:1, one launch (start us, length us, event | category | flops | bytes accessed | tf_op | source)
XLA Modules:
  0.0 236.3 jit_solution(7616556617195620581)
XLA Ops:
  3.7 24.7 %all_to_all.35 = bf16[16,4,3200]{2,1,0:T(4,128)(2,1)S(1)} all-to-all(bf16[16,4,3200]{2,1,0:T(4,128)(2,1)S(1)} %pad_maximum_fusion), channel_id=1, replica_groups=mesh['x'=4,'zh'=2,'zl'=4,'c'=2,'y'=4] {'zh','zl','c'}, dimensions={0} | all-to-all | bytes 819200 | tf_op jit(solution)/shard_map/all_to_all | solution.py:222
  29.5 4.2 %all-to-all-start.1 = ((bf16[4,64,1536]{2,1,0:T(8,128)(2,1)}), bf16[4,64,1536]{2,1,0:T(8,128)(2,1)S(1)}, u32[]{:S(2)}, u32[]{:S(2)}) async-start(bf16[4,64,1536]{2,1,0:T(8,128)(2,1)} %broadcast_in_dim.25), calls=%async_computation.1 | async-start | bytes 1572864 | tf_op jit(solution)/shard_map/all_to_all | solution.py:228
  38.0 2.2 copy.81
  40.2 2.0 copy.82
  42.2 5.4 %collective-permute-done.2.far = bf16[64,1664]{1,0:T(8,128)(2,1)S(1)} collective-permute-done((bf16[64,1664]{1,0:T(8,128)(2,1)S(1)}, bf16[64,1664]{1,0:T(8,128)(2,1)S(1)}, u32[]{:S(2)}, u32[]{:S(2)}) %collective-permute-start.2) | collective-permute-done | bytes 213024 | tf_op jit(solution)/shard_map/ppermute | solution.py:31
  52.1 5.1 %subtract_convert_fusion.1 = (bf16[6144,8]{1,0:T(8,128)(2,1)}, bf16[6144,8]{1,0:T(8,128)(2,1)}) fusion(f32[6144,8]{1,0:T(8,128)} %copy.81, f32[6144,8]{1,0:T(8,128)} %copy.82), kind=kLoop, calls=%fused_computation.5 | loop fusion | flops 245760 | bytes 589824 | tf_op jit(solution)/shard_map/convert_element_type | solution.py:79
  58.7 9.1 %collective-permute-done.3.x1 = bf16[256,1536]{1,0:T(8,128)(2,1)S(1)} collective-permute-done((bf16[256,1536]{1,0:T(8,128)(2,1)S(1)}, bf16[256,1536]{1,0:T(8,128)(2,1)S(1)}, u32[]{:S(2)}, u32[]{:S(2)}) %collective-permute-start.3) | collective-permute-done | bytes 786464 | tf_op jit(solution)/shard_map/ppermute | solution.py:31
  70.4 2.7 %collective-permute-start.6 = (bf16[128,1536]{1,0:T(8,128)(2,1)}, bf16[128,1536]{1,0:T(8,128)(2,1)}, u32[]{:S(2)}, u32[]{:S(2)}) collective-permute-start(bf16[128,1536]{1,0:T(8,128)(2,1)} %slice.46), channel_id=1, source_target_pairs={{0,3},{1,0},{2,1},{3,2},{4,7},{5,4},{6,5},{7,6},{8,11},{9,8},{10,9... | collective-permute-start | bytes 1179656 | tf_op jit(solution)/shard_map/ppermute | solution.py:31
  74.8 1.8 slice.48
  77.2 4.1 %maximum_maximum_fusion.router = bf16[6144,128]{1,0:T(8,128)(2,1)} fusion(bf16[6144,8]{1,0:T(8,128)(2,1)} %get-tuple-element.58, bf16[6144,8]{1,0:T(8,128)(2,1)S(1)} %copy-done.35, bf16[6144,8]{1,0:T(8,128)(2,1)S(1)} %copy-done.36, bf16[128]{0:T(256)(128)(2,1)S(1)} %pad.8.clone), kind=kLoop, calls=%fused_computation.4 | loop fusion | flops 6291456 | bytes 1868032 | tf_op jit(solution)/shard_map/concatenate | solution.py:241
  82.7 9.1 %concatenate.25.router = bf16[6144,128]{1,0:T(8,128)(2,1)} concatenate(bf16[6144,8]{1,0:T(8,128)(2,1)} %copy.83, bf16[6144,8]{1,0:T(8,128)(2,1)} %copy.83, bf16[6144,8]{1,0:T(8,128)(2,1)} %get-tuple-element.57, bf16[6144,8]{1,0:T(8,128)(2,1)} %get-tuple-element.57, bf16[6144,96]{1,0:T(8,128)(2,1)} %broadcast_in_dim.27), dimensions={1} | concatenate | bytes 3145728 | tf_op jit(solution)/shard_map/concatenate | solution.py:243
  91.9 1.9 copy-done.2
  93.8 1.9 copy-done.4
  101.6 5.8 %shard_map.105 = (bf16[256,256]{1,0:T(8,128)(2,1)S(1)}, bf16[256,256]{1,0:T(8,128)(2,1)S(1)}, bf16[256,256]{1,0:T(8,128)(2,1)S(1)}, bf16[256,128]{1,0:T(8,128)(2,1)S(1)}, f32[256,128]{1,0:T(8,128)S(1)}) custom-call(s32[2]{0:T(128)S(1)} %pad_add_fusion.at, bf16[256,1536]{1,0:T(8,128)(2,1)S(1)} %copy-done.9, bf16[256,1536]{1,0:T(8,128)(2,1)S(1)} %copy-done.14, ...), custom_call_target="tpu_custom_call" | custom-call | tf_op jit(solution)/shard_map/pallas_call | solution.py:43
  107.4 4.9 %shard_map.106 = (bf16[256,1536]{1,0:T(8,128)(2,1)S(1)}, bf16[256,1536]{1,0:T(8,128)(2,1)S(1)}, bf16[256,1536]{1,0:T(8,128)(2,1)S(1)}, bf16[128,1536]{1,0:T(8,12...) custom-call(s32[2]{0:T(128)S(1)} %pad_add_fusion.at, ...), custom_call_target="tpu_custom_call" | custom-call | tf_op jit(solution)/shard_map/pallas_call | solution.py:43
  117.7 2.7 %collective-permute-start.12 = (bf16[128,1536]{1,0:T(8,128)(2,1)}, bf16[128,1536]{1,0:T(8,128)(2,1)S(1)}, u32[]{:S(2)}, u32[]{:S(2)}) collective-permute-start(bf16[128,1536]{1,0:T(8,128)(2,1)} %get-tuple-element.38), channel_id=1, source_target_pairs={{0,3},{1,0},{2,1},{3,2},{4,7},{5,4},{6,5},{7,6},{8,11},{9,8},{10,9... | collective-permute-start | bytes 1179656 | tf_op jit(solution)/shard_map/ppermute | solution.py:31
  120.9 2.2 collective-permute-start.19
  123.4 4.1 %collective-permute-done.11.up = bf16[128,1536]{1,0:T(8,128)(2,1)S(1)} collective-permute-done((bf16[128,1536]{1,0:T(8,128)(2,1)}, bf16[128,1536]{1,0:T(8,128)(2,1)S(1)}, u32[]{:S(2)}, u32[]{:S(2)}) %collective-permute-start.11) | collective-permute-done | bytes 393248 | tf_op jit(solution)/shard_map/ppermute | solution.py:31
  131.0 2.7 %collective-permute-start.14 = (bf16[256,1536]{1,0:T(8,128)(2,1)}, bf16[256,1536]{1,0:T(8,128)(2,1)S(1)}, u32[]{:S(2)}, u32[]{:S(2)}) collective-permute-start(bf16[256,1536]{1,0:T(8,128)(2,1)} %get-tuple-element.40), channel_id=1, source_target_pairs={{0,3},{1,0},{2,1},{3,2},{4,7},{5,4},{6,5},{7,6},{8,11},{9,8},{10,9... | collective-permute-start | bytes 2359304 | tf_op jit(solution)/shard_map/ppermute | solution.py:31
  134.5 4.0 %all-to-all-start.4 = ((f32[32,2,128]{2,1,0:T(2,128)}), f32[32,2,128]{2,1,0:T(2,128)S(1)}, u32[]{:S(2)}, u32[]{:S(2)}) async-start(f32[32,2,128]{2,1,0:T(2,128)} %broadcast_in_dim.29), calls=%async_computation.4 | async-start | bytes 65536 | tf_op jit(solution)/shard_map/all_to_all | solution.py:267
  138.5 11.1 %all-to-all-done.4 = f32[32,2,128]{2,1,0:T(2,128)S(1)} async-done(((f32[32,2,128]{2,1,0:T(2,128)}), f32[32,2,128]{2,1,0:T(2,128)S(1)}, u32[]{:S(2)}, u32[]{:S(2)}) %all-to-all-start.4) | async-done | bytes 32800 | tf_op jit(solution)/shard_map/all_to_all | solution.py:267
  150.3 9.3 %all-to-all-start.5 = ((f32[8,2,128]{2,1,0:T(2,128)}), f32[8,2,128]{2,1,0:T(2,128)S(1)}, u32[]{:S(2)}, u32[]{:S(2)}) async-start(f32[8,2,128]{2,1,0:T(2,128)} %broadcast_in_dim.30), calls=%async_computation.5 | async-start | bytes 16384 | tf_op jit(solution)/shard_map/all_to_all | solution.py:272
  167.0 2.3 collective-permute-start.21
  177.6 9.6 %collective-permute-done.20.b = bf16[64,6144]{1,0:T(8,128)(2,1)} collective-permute-done((bf16[64,6144]{1,0:T(8,128)(2,1)}, bf16[64,6144]{1,0:T(8,128)(2,1)}, u32[]{:S(2)}, u32[]{:S(2)}) %collective-permute-start.20) | collective-permute-done | bytes 786464 | tf_op jit(solution)/shard_map/ppermute | solution.py:31
  187.2 2.6 %shard_map.110 = bf16[4,64,1536]{2,1,0:T(8,128)(2,1)} custom-call(bf16[64,6144]{1,0:T(8,128)(2,1)S(1)} %copy-done.18, bf16[64,6144]{1,0:T(8,128)(2,1)} %collective-permute-done.20.b, bf16[64,6144]{1,0:T(8,128)(2,1)} %collective-permute-done.21.c), custom_call_target="tpu_custom_call" | custom-call | tf_op jit(solution)/shard_map/pallas_call | solution.py:43
  189.8 3.5 %all-to-all-start.2 = ((bf16[4,64,1536]{2,1,0:T(8,128)(2,1)}), bf16[4,64,1536]{2,1,0:T(8,128)(2,1)S(1)}, u32[]{:S(2)}, u32[]{:S(2)}) async-start(bf16[4,64,1536]{2,1,0:T(8,128)(2,1)} %shard_map.110), calls=%async_computation.2 | async-start | bytes 1572864 | tf_op jit(solution)/shard_map/all_to_all | solution.py:299
  193.6 2.1 collective-permute-done.16
  196.9 7.3 %all-to-all-done.2 = bf16[4,64,1536]{2,1,0:T(8,128)(2,1)S(1)} async-done(((bf16[4,64,1536]{2,1,0:T(8,128)(2,1)}), bf16[4,64,1536]{2,1,0:T(8,128)(2,1)S(1)}, u32[]{:S(2)}, u32[]{:S(2)}) %all-to-all-start.2) | async-done | bytes 786464 | tf_op jit(solution)/shard_map/all_to_all | solution.py:299
  204.9 6.7 %all-to-all-start.6 = ((f32[8,12,128]{2,1,0:T(8,128)}), f32[8,12,128]{2,1,0:T(8,128)S(1)}, u32[]{:S(2)}, u32[]{:S(2)}) async-start(f32[8,12,128]{2,1,0:T(8,128)} %broadcast_in_dim.67), calls=%async_computation.6 | async-start | bytes 131072 | tf_op jit(solution)/shard_map/all_to_all | solution.py:287
  212.6 4.0 %all-to-all-done.6 = f32[8,12,128]{2,1,0:T(8,128)S(1)} async-done(((f32[8,12,128]{2,1,0:T(8,128)}), f32[8,12,128]{2,1,0:T(8,128)S(1)}, u32[]{:S(2)}, u32[]{:S(2)}) %all-to-all-start.6) | async-done | bytes 49184 | tf_op jit(solution)/shard_map/all_to_all | solution.py:287
  216.6 4.2 %all-to-all-start.3 = ((bf16[16,4,3072]{2,1,0:T(4,128)(2,1)}), bf16[16,4,3072]{2,1,0:T(4,128)(2,1)S(1)}, u32[]{:S(2)}, u32[]{:S(2)}) async-start(bf16[16,4,3072]{2,1,0:T(4,128)(2,1)} %reshape.134), calls=%async_computation.3 | async-start | bytes 786432 | tf_op jit(solution)/shard_map/all_to_all | solution.py:303
  221.5 13.9 %all-to-all-done.3 = bf16[16,4,3072]{2,1,0:T(4,128)(2,1)S(1)} async-done(((bf16[16,4,3072]{2,1,0:T(4,128)(2,1)}), bf16[16,4,3072]{2,1,0:T(4,128)(2,1)S(1)}, u32[]{:S(2)}, u32[]{:S(2)}) %all-to-all-start.3) | async-done | bytes 393248 | tf_op jit(solution)/shard_map/all_to_all | solution.py:303
  (182 shorter events, 58.3 us)
Async XLA Ops:
  3.3 34.6 %copy-start.37 = (f32[6144,8]{0,1:T(8,128)S(1)}, f32[6144,8]{0,1:T(8,128)}, u32[]{:S(2)}) copy-start(f32[6144,8]{0,1:T(8,128)} %param.10) | copy-start | bytes 589828
  29.5 21.0 %all-to-all-start.1 = ((bf16[4,64,1536]{2,1,0:T(8,128)(2,1)}), bf16[4,64,1536]{2,1,0:T(8,128)(2,1)S(1)}, u32[]{:S(2)}, u32[]{:S(2)}) async-start(bf16[4,64,1536]{2,1,0:T(8,128)(2,1)} %broadcast_in_dim.25), calls=%async_computation.1 | async-start | bytes 1572864 | tf_op jit(solution)/shard_map/all_to_all | solution.py:228
  33.7 8.5 %collective-permute-start = (bf16[64,1664]{1,0:T(8,128)(2,1)S(1)}, bf16[64,1664]{1,0:T(8,128)(2,1)S(1)}, u32[]{:S(2)}, u32[]{:S(2)}) collective-permute-start(bf16[64,1664]{1,0:T(8,128)(2,1)S(1)} %slice.44.own), channel_id=1, source_target_pairs={{0,64},{64,128},{128,192},{192,0},{1,65},{65,129},{129,193},{193,1... | collective-permute-start | bytes 638984 | tf_op jit(solution)/shard_map/ppermute | solution.py:31
  35.0 7.2 %collective-permute-start.1 = (bf16[64,1664]{1,0:T(8,128)(2,1)S(1)}, bf16[64,1664]{1,0:T(8,128)(2,1)S(1)}, u32[]{:S(2)}, u32[]{:S(2)}) collective-permute-start(bf16[64,1664]{1,0:T(8,128)(2,1)S(1)} %slice.44.own), channel_id=1, source_target_pairs={{0,192},{64,0},{128,64},{192,128},{1,193},{65,1},{129,65},{193,129... | collective-permute-start | bytes 638984 | tf_op jit(solution)/shard_map/ppermute | solution.py:31
  36.4 11.2 %collective-permute-start.2 = (bf16[64,1664]{1,0:T(8,128)(2,1)S(1)}, bf16[64,1664]{1,0:T(8,128)(2,1)S(1)}, u32[]{:S(2)}, u32[]{:S(2)}) collective-permute-start(bf16[64,1664]{1,0:T(8,128)(2,1)S(1)} %slice.44.own), channel_id=1, source_target_pairs={{0,128},{64,192},{128,0},{192,64},{1,129},{65,193},{129,1},{193,65... | collective-permute-start | bytes 638984 | tf_op jit(solution)/shard_map/ppermute | solution.py:31
  47.7 20.1 %collective-permute-start.3 = (bf16[256,1536]{1,0:T(8,128)(2,1)S(1)}, bf16[256,1536]{1,0:T(8,128)(2,1)S(1)}, u32[]{:S(2)}, u32[]{:S(2)}) collective-permute-start(bf16[256,1536]{1,0:T(8,128)(2,1)S(1)} %get-tuple-element.28.x0), channel_id=1, source_target_pairs={{0,1},{1,2},{2,3},{3,0},{4,5},{5,6},{6,7},{7,4},{8,9},{9,10},{10,1... | collective-permute-start | bytes 2359304 | tf_op jit(solution)/shard_map/ppermute | solution.py:31
  49.2 19.4 %collective-permute-start.4 = (bf16[256,1536]{1,0:T(8,128)(2,1)S(1)}, bf16[256,1536]{1,0:T(8,128)(2,1)}, u32[]{:S(2)}, u32[]{:S(2)}) collective-permute-start(bf16[256,1536]{1,0:T(8,128)(2,1)S(1)} %get-tuple-element.28.x0), channel_id=1, source_target_pairs={{0,3},{1,0},{2,1},{3,2},{4,7},{5,4},{6,5},{7,6},{8,11},{9,8},{10,9... | collective-permute-start | bytes 2359304 | tf_op jit(solution)/shard_map/ppermute | solution.py:31
  50.6 22.5 %collective-permute-start.8 = (bf16[64,6144]{1,0:T(8,128)(2,1)S(1)}, bf16[64,6144]{1,0:T(8,128)(2,1)S(1)}, u32[]{:S(2)}, u32[]{:S(2)}) collective-permute-start(bf16[64,6144]{1,0:T(8,128)(2,1)S(1)} %shard_map.104.d0), channel_id=1, source_target_pairs={{0,192},{64,0},{128,64},{192,128},{1,193},{65,1},{129,65},{193,129... | collective-permute-start | bytes 2359304 | tf_op jit(solution)/shard_map/ppermute | solution.py:31
  52.0 22.8 %collective-permute-start.7 = (bf16[64,6144]{1,0:T(8,128)(2,1)S(1)}, bf16[64,6144]{1,0:T(8,128)(2,1)}, u32[]{:S(2)}, u32[]{:S(2)}) collective-permute-start(bf16[64,6144]{1,0:T(8,128)(2,1)S(1)} %shard_map.104.d0), channel_id=1, source_target_pairs={{0,64},{64,128},{128,192},{192,0},{1,65},{65,129},{129,193},{193,1... | collective-permute-start | bytes 2359304 | tf_op jit(solution)/shard_map/ppermute | solution.py:31
  68.6 23.2 %collective-permute-start.5 = (bf16[128,1536]{1,0:T(8,128)(2,1)}, bf16[128,1536]{1,0:T(8,128)(2,1)}, u32[]{:S(2)}, u32[]{:S(2)}) collective-permute-start(bf16[128,1536]{1,0:T(8,128)(2,1)} %slice.45), channel_id=1, source_target_pairs={{0,1},{1,2},{2,3},{3,0},{4,5},{5,6},{6,7},{7,4},{8,9},{9,10},{10,1... | collective-permute-start | bytes 1179656 | tf_op jit(solution)/shard_map/ppermute | solution.py:31
  70.4 21.5 %collective-permute-start.6 = (bf16[128,1536]{1,0:T(8,128)(2,1)}, bf16[128,1536]{1,0:T(8,128)(2,1)}, u32[]{:S(2)}, u32[]{:S(2)}) collective-permute-start(bf16[128,1536]{1,0:T(8,128)(2,1)} %slice.46), channel_id=1, source_target_pairs={{0,3},{1,0},{2,1},{3,2},{4,7},{5,4},{6,5},{7,6},{8,11},{9,8},{10,9... | collective-permute-start | bytes 1179656 | tf_op jit(solution)/shard_map/ppermute | solution.py:31
  74.0 17.9 %collective-permute-start.10 = (bf16[32,6144]{1,0:T(8,128)(2,1)}, bf16[32,6144]{1,0:T(8,128)(2,1)}, u32[]{:S(2)}, u32[]{:S(2)}) collective-permute-start(bf16[32,6144]{1,0:T(8,128)(2,1)} %slice.49), channel_id=1, source_target_pairs={{0,192},{64,0},{128,64},{192,128},{1,193},{65,1},{129,65},{193,129... | collective-permute-start | bytes 1179656 | tf_op jit(solution)/shard_map/ppermute | solution.py:31
  76.6 15.3 %collective-permute-start.9 = (bf16[32,6144]{1,0:T(8,128)(2,1)}, bf16[32,6144]{1,0:T(8,128)(2,1)}, u32[]{:S(2)}, u32[]{:S(2)}) collective-permute-start(bf16[32,6144]{1,0:T(8,128)(2,1)} %slice.48), channel_id=1, source_target_pairs={{0,64},{64,128},{128,192},{192,0},{1,65},{65,129},{129,193},{193,1... | collective-permute-start | bytes 1179656 | tf_op jit(solution)/shard_map/ppermute | solution.py:31
  117.7 9.8 %collective-permute-start.11 = (bf16[128,1536]{1,0:T(8,128)(2,1)}, bf16[128,1536]{1,0:T(8,128)(2,1)S(1)}, u32[]{:S(2)}, u32[]{:S(2)}) collective-permute-start(bf16[128,1536]{1,0:T(8,128)(2,1)} %get-tuple-element.36), channel_id=1, source_target_pairs={{0,1},{1,2},{2,3},{3,0},{4,5},{5,6},{6,7},{7,4},{8,9},{9,10},{10,1... | collective-permute-start | bytes 1179656 | tf_op jit(solution)/shard_map/ppermute | solution.py:31
  117.7 9.8 %collective-permute-start.12 = (bf16[128,1536]{1,0:T(8,128)(2,1)}, bf16[128,1536]{1,0:T(8,128)(2,1)S(1)}, u32[]{:S(2)}, u32[]{:S(2)}) collective-permute-start(bf16[128,1536]{1,0:T(8,128)(2,1)} %get-tuple-element.38), channel_id=1, source_target_pairs={{0,3},{1,0},{2,1},{3,2},{4,7},{5,4},{6,5},{7,6},{8,11},{9,8},{10,9... | collective-permute-start | bytes 1179656 | tf_op jit(solution)/shard_map/ppermute | solution.py:31
  120.4 39.2 %collective-permute-start.18 = (bf16[32,6144]{1,0:T(8,128)(2,1)}, bf16[32,6144]{1,0:T(8,128)(2,1)S(1)}, u32[]{:S(2)}, u32[]{:S(2)}) collective-permute-start(bf16[32,6144]{1,0:T(8,128)(2,1)} %get-tuple-element.47), channel_id=1, source_target_pairs={{0,64},{64,128},{128,192},{192,0},{1,65},{65,129},{129,193},{193,1... | collective-permute-start | bytes 1179656 | tf_op jit(solution)/shard_map/ppermute | solution.py:31
  120.9 39.3 %collective-permute-start.19 = (bf16[32,6144]{1,0:T(8,128)(2,1)}, bf16[32,6144]{1,0:T(8,128)(2,1)S(1)}, u32[]{:S(2)}, u32[]{:S(2)}) collective-permute-start(bf16[32,6144]{1,0:T(8,128)(2,1)} %get-tuple-element.49), channel_id=1, source_target_pairs={{0,192},{64,0},{128,64},{192,128},{1,193},{65,1},{129,65},{193,129... | collective-permute-start | bytes 1179656 | tf_op jit(solution)/shard_map/ppermute | solution.py:31
  129.7 43.4 %copy-start.20 = (bf16[256,1536]{1,0:T(8,128)(2,1)S(1)}, bf16[256,1536]{1,0:T(8,128)(2,1)}, u32[]{:S(2)}) copy-start(bf16[256,1536]{1,0:T(8,128)(2,1)} %copy-done.19) | copy-start | bytes 2359300
  131.0 41.2 %collective-permute-start.13 = (bf16[256,1536]{1,0:T(8,128)(2,1)}, bf16[256,1536]{1,0:T(8,128)(2,1)S(1)}, u32[]{:S(2)}, u32[]{:S(2)}) collective-permute-start(bf16[256,1536]{1,0:T(8,128)(2,1)} %get-tuple-element.39), channel_id=1, source_target_pairs={{0,1},{1,2},{2,3},{3,0},{4,5},{5,6},{6,7},{7,4},{8,9},{9,10},{10,1... | collective-permute-start | bytes 2359304 | tf_op jit(solution)/shard_map/ppermute | solution.py:31
  131.0 41.2 %collective-permute-start.14 = (bf16[256,1536]{1,0:T(8,128)(2,1)}, bf16[256,1536]{1,0:T(8,128)(2,1)S(1)}, u32[]{:S(2)}, u32[]{:S(2)}) collective-permute-start(bf16[256,1536]{1,0:T(8,128)(2,1)} %get-tuple-element.40), channel_id=1, source_target_pairs={{0,3},{1,0},{2,1},{3,2},{4,7},{5,4},{6,5},{7,6},{8,11},{9,8},{10,9... | collective-permute-start | bytes 2359304 | tf_op jit(solution)/shard_map/ppermute | solution.py:31
  134.5 15.1 %all-to-all-start.4 = ((f32[32,2,128]{2,1,0:T(2,128)}), f32[32,2,128]{2,1,0:T(2,128)S(1)}, u32[]{:S(2)}, u32[]{:S(2)}) async-start(f32[32,2,128]{2,1,0:T(2,128)} %broadcast_in_dim.29), calls=%async_computation.4 | async-start | bytes 65536 | tf_op jit(solution)/shard_map/all_to_all | solution.py:267
  150.3 19.3 %all-to-all-start.5 = ((f32[8,2,128]{2,1,0:T(2,128)}), f32[8,2,128]{2,1,0:T(2,128)S(1)}, u32[]{:S(2)}, u32[]{:S(2)}) async-start(f32[8,2,128]{2,1,0:T(2,128)} %broadcast_in_dim.30), calls=%async_computation.5 | async-start | bytes 16384 | tf_op jit(solution)/shard_map/all_to_all | solution.py:272
  165.3 21.9 %copy-start.18 = (bf16[64,6144]{1,0:T(8,128)(2,1)S(1)}, bf16[64,6144]{1,0:T(8,128)(2,1)}, u32[]{:S(2)}) copy-start(bf16[64,6144]{1,0:T(8,128)(2,1)} %copy-done.17) | copy-start | bytes 2359300
  166.6 20.6 %collective-permute-start.20 = (bf16[64,6144]{1,0:T(8,128)(2,1)}, bf16[64,6144]{1,0:T(8,128)(2,1)}, u32[]{:S(2)}, u32[]{:S(2)}) collective-permute-start(bf16[64,6144]{1,0:T(8,128)(2,1)} %get-tuple-element.50), channel_id=1, source_target_pairs={{0,64},{64,128},{128,192},{192,0},{1,65},{65,129},{129,193},{193,1... | collective-permute-start | bytes 2359304 | tf_op jit(solution)/shard_map/ppermute | solution.py:31
  167.0 20.3 %collective-permute-start.21 = (bf16[64,6144]{1,0:T(8,128)(2,1)}, bf16[64,6144]{1,0:T(8,128)(2,1)}, u32[]{:S(2)}, u32[]{:S(2)}) collective-permute-start(bf16[64,6144]{1,0:T(8,128)(2,1)} %get-tuple-element.51), channel_id=1, source_target_pairs={{0,192},{64,0},{128,64},{192,128},{1,193},{65,1},{129,65},{193,129... | collective-permute-start | bytes 2359304 | tf_op jit(solution)/shard_map/ppermute | solution.py:31
  174.3 19.1 %copy-start.10 = (bf16[256,1536]{1,0:T(8,128)(2,1)S(1)}, bf16[256,1536]{1,0:T(8,128)(2,1)}, u32[]{:S(2)}) copy-start(bf16[256,1536]{1,0:T(8,128)(2,1)} %copy-done.8) | copy-start | bytes 2359300
  175.2 18.3 %collective-permute-start.15 = (bf16[64,1536]{1,0:T(8,128)(2,1)}, bf16[64,1536]{1,0:T(8,128)(2,1)}, u32[]{:S(2)}, u32[]{:S(2)}) collective-permute-start(bf16[64,1536]{1,0:T(8,128)(2,1)} %get-tuple-element.42), channel_id=1, source_target_pairs={{0,192},{64,0},{128,64},{192,128},{1,193},{65,1},{129,65},{193,129... | collective-permute-start | bytes 589832 | tf_op jit(solution)/shard_map/ppermute | solution.py:31
  175.2 20.5 %collective-permute-start.16 = (bf16[64,1536]{1,0:T(8,128)(2,1)}, bf16[64,1536]{1,0:T(8,128)(2,1)}, u32[]{:S(2)}, u32[]{:S(2)}) collective-permute-start(bf16[64,1536]{1,0:T(8,128)(2,1)} %get-tuple-element.43), channel_id=1, source_target_pairs={{0,64},{64,128},{128,192},{192,0},{1,65},{65,129},{129,193},{193,1... | collective-permute-start | bytes 589832 | tf_op jit(solution)/shard_map/ppermute | solution.py:31
  176.7 19.0 %collective-permute-start.17 = (bf16[64,1536]{1,0:T(8,128)(2,1)}, bf16[64,1536]{1,0:T(8,128)(2,1)}, u32[]{:S(2)}, u32[]{:S(2)}) collective-permute-start(bf16[64,1536]{1,0:T(8,128)(2,1)} %get-tuple-element.44), channel_id=1, source_target_pairs={{0,128},{64,192},{128,0},{192,64},{1,129},{65,193},{129,1},{193,65... | collective-permute-start | bytes 589832 | tf_op jit(solution)/shard_map/ppermute | solution.py:31
  189.8 14.4 %all-to-all-start.2 = ((bf16[4,64,1536]{2,1,0:T(8,128)(2,1)}), bf16[4,64,1536]{2,1,0:T(8,128)(2,1)S(1)}, u32[]{:S(2)}, u32[]{:S(2)}) async-start(bf16[4,64,1536]{2,1,0:T(8,128)(2,1)} %shard_map.110), calls=%async_computation.2 | async-start | bytes 1572864 | tf_op jit(solution)/shard_map/all_to_all | solution.py:299
  204.9 11.8 %all-to-all-start.6 = ((f32[8,12,128]{2,1,0:T(8,128)}), f32[8,12,128]{2,1,0:T(8,128)S(1)}, u32[]{:S(2)}, u32[]{:S(2)}) async-start(f32[8,12,128]{2,1,0:T(8,128)} %broadcast_in_dim.67), calls=%async_computation.6 | async-start | bytes 131072 | tf_op jit(solution)/shard_map/all_to_all | solution.py:287
  216.6 18.7 %all-to-all-start.3 = ((bf16[16,4,3072]{2,1,0:T(4,128)(2,1)}), bf16[16,4,3072]{2,1,0:T(4,128)(2,1)S(1)}, u32[]{:S(2)}, u32[]{:S(2)}) async-start(bf16[16,4,3072]{2,1,0:T(4,128)(2,1)} %reshape.134), calls=%async_computation.3 | async-start | bytes 786432 | tf_op jit(solution)/shard_map/all_to_all | solution.py:303
  (35 other events, 141.1 us)

commit v2 on v1

v2 whole, which is shorter than its diff:
```python
import jax
import jax.numpy as jnp
from jax import lax
from jax.experimental import pallas as pl
from jax.experimental.pallas import tpu as pltpu
from jax.sharding import Mesh
from jax.sharding import PartitionSpec as P

F32 = jnp.float32
BF16 = jnp.bfloat16
ZAX = ("zh", "zl", "c")
EXP = ("zl", "c")
ALL = ("x", "zh", "zl", "c")
RING = 4
OFFS = (0, -1, 1, 2)
N_EXP = 8
CAP = 4
SLOTS = N_EXP * CAP
LANES = 128


def dot(a, b):
    return jnp.dot(a, b, preferred_element_type=F32)


def dot_t(a, b):
    return lax.dot_general(a, b, (((1,), (1,)), ((), ())), preferred_element_type=F32)


def shift(a, axis, n):
    return lax.ppermute(a, axis, [(i, (i + n) % RING) for i in range(RING)])


def sds(shape, dtype):
    return jax.ShapeDtypeStruct(shape, dtype)


VMEM = pl.BlockSpec(memory_space=pltpu.VMEM)
SMEM = pl.BlockSpec(memory_space=pltpu.SMEM)
ANY = pl.BlockSpec(memory_space=pl.ANY)


def kernel(body, outs, *args, specs, out_specs=None, scratch=(), limit=16):
    return pl.pallas_call(
        body,
        out_shape=outs,
        in_specs=list(specs),
        out_specs=out_specs or jax.tree.map(lambda _: VMEM, outs),
        scratch_shapes=list(scratch),
        compiler_params=pltpu.CompilerParams(vmem_limit_bytes=limit << 20),
    )(*args)


def spot(at, off):
    return (at + (off + RING)) % RING


def rows_body(own, left, right, far, top_out, bot_out, meta_out):
    n, width = own.shape
    for i, r in enumerate((own, left, right, far)):
        s = slice((i % 2) * n, (i % 2 + 1) * n)
        (top_out, bot_out)[i // 2][s] = r[:, : width - LANES]
        meta_out[i * n : (i + 1) * n] = r[:, width - LANES :]


def expert_body(
    at, x0t, x0b, x1t, x1b, x2t, x2b, x3t, x3b, dys, meta, gate, up, down, router,
    m0, m1, m2, m3t, m3b, g0, g1, g2, g3t, g3b, gw_out, gates_out,
    xb, db, gb, ub, wb, mb, rp, hb, ggb, gub, tlb, mo, go, sx, sd, sm, sg, su, sw, so,
):
    x_at, y_at, e_at = at[0], at[1], at[2]
    n = dys.shape[1]
    quarter = dys.shape[2]
    n_rows = RING * n
    half = n_rows // 2
    copies_x, copies_d, copies_m, copies_g, copies_u, copies_w = [], [], [], [], [], []

    def copy(src, dst, sem):
        c = pltpu.make_async_copy(src, dst, sem)
        c.start()
        return c

    def cols(i):
        return slice(i * quarter, (i + 1) * quarter)

    def row_at(i):
        return pl.ds(pl.multiple_of(spot(x_at, OFFS[i]) * n, n), n)

    for i in range(RING):
        pair = ((x0t, x0b), (x1t, x1b), (x2t, x2b), (x3t, x3b))[i]
        q = pl.ds(pl.multiple_of(spot(y_at, OFFS[i]) * quarter, quarter), quarter)
        for r in range(RING):
            src = pair[r // 2].at[(r % 2) * n : (r % 2 + 1) * n]
            copies_x.append(copy(src, xb.at[i, row_at(r), :], sx.at[i * RING + r]))
        copies_g.append(copy(gate.at[q], gb.at[i], sg.at[i]))
        copies_u.append(copy(up.at[q], ub.at[i], su.at[i]))
    for r in range(RING):
        copies_m.append(copy(meta.at[r * n : (r + 1) * n], mb.at[row_at(r), :], sm.at[r]))
    for i in range(RING):
        q = pl.ds(pl.multiple_of(spot(y_at, OFFS[i]) * quarter, quarter), quarter)
        for r in range(RING):
            src = dys.at[r * RING + spot(y_at, OFFS[i])]
            copies_d.append(copy(src, db.at[i, r * n : (r + 1) * n], sd.at[i * RING + r]))
        copies_w.append(copy(down.at[:, q], wb.at[i], sw.at[i]))

    for i in range(RING):
        q = pl.ds(pl.multiple_of(spot(y_at, OFFS[i]) * quarter, quarter), quarter)
        r0 = router[:, q]
        r1 = r0 - r0.astype(BF16).astype(F32)
        r2 = r1 - r1.astype(BF16).astype(F32)
        rp[i] = jnp.concatenate([r0, r1, r2, jnp.zeros_like(r0)], 0).astype(BF16)

    pre_gate = pre_up = logits3 = raw = None
    for i in range(RING):
        for r in range(RING):
            copies_x[i * RING + r].wait()
        copies_g[i].wait()
        copies_u[i].wait()
        a = xb[i]
        g, u, l = dot(a, gb[i]), dot(a, ub[i]), dot_t(a, rp[i])
        pre_gate = g if i == 0 else pre_gate + g
        pre_up = u if i == 0 else pre_up + u
        logits3 = l if i == 0 else logits3 + l
    for i in range(RING):
        for r in range(RING):
            copies_d[i * RING + r].wait()
        copies_w[i].wait()
        g = dot_t(db[i], wb[i])
        raw = g if i == 0 else raw + g
    for c in copies_m:
        c.wait()

    lane = lax.broadcasted_iota(jnp.int32, logits3.shape, 1)
    expert = lane % N_EXP
    code = mb[:, :1].astype(F32).astype(jnp.int32)
    other = code // CAP
    hot_own = expert == e_at
    hot_other = expert == other
    score_own = jax.nn.sigmoid(jnp.sum(jnp.where(hot_own, logits3, 0.0), 1, keepdims=True))
    score_other = jax.nn.sigmoid(jnp.sum(jnp.where(hot_other, logits3, 0.0), 1, keepdims=True))
    total = score_own + score_other
    weight = score_own / total
    both = score_own * score_other / (total * total)
    c_own = both * (1.0 - score_own)
    c_other = both * (1.0 - score_other)
    gate_sig = jax.nn.sigmoid(pre_gate)
    gate_act = pre_gate * gate_sig
    hidden = gate_act * pre_up
    product = hidden * raw
    grad_weight = jnp.sum(product, 1, keepdims=True)
    hb[...] = (weight * hidden).astype(BF16)
    grad_hidden = weight * raw
    ggb[...] = (
        grad_hidden * pre_up * gate_sig * (1.0 + pre_gate * (1.0 - gate_sig))
    ).astype(BF16)
    gub[...] = (grad_hidden * gate_act).astype(BF16)
    to_logits = jnp.where(hot_own, grad_weight * c_own, 0.0) - jnp.where(
        hot_other, grad_weight * c_other, 0.0
    )
    high = to_logits.astype(BF16).astype(F32)
    tlb[...] = jnp.where(lane < 2 * N_EXP, high, to_logits - high).astype(BF16)
    wide = lax.broadcasted_iota(jnp.int32, gates_out.shape, 1)
    gates_out[...] = jnp.where(wide == 0, c_own, code.astype(F32))
    ones = jnp.ones((8, product.shape[1]), F32)
    sums = lax.dot_general(
        ones, product, (((1,), (1,)), ((), ())),
        preferred_element_type=F32, precision=lax.Precision.HIGHEST,
    )
    for k in range(gw_out.shape[0] // 8):
        gw_out[k * 8 : (k + 1) * 8] = sums

    outs = []

    def send(src, dst):
        outs.append(copy(src, dst, so.at[len(outs)]))

    for i in (3, 1, 2, 0):
        mo[i] = dot(hb[...], wb[i]).astype(BF16)
        if i == 3:
            send(mo.at[i, :half], m3t)
            send(mo.at[i, half:], m3b)
        else:
            send(mo.at[i], (m0, m1, m2)[i])
    for i in range(RING):
        r4 = jnp.concatenate([rp[i][: 2 * N_EXP], rp[i][: 2 * N_EXP]], 0)
        v = dot_t(ggb[...], gb[i]) + dot_t(gub[...], ub[i]) + dot(tlb[...], r4)
        go[i] = v.astype(BF16)
        q = pl.ds(pl.multiple_of(spot(y_at, OFFS[i]) * quarter, quarter), quarter)
        for j, dst in ((1, g1), (2, g2), (0, g0)):
            send(go.at[i, row_at(j), :], dst.at[:, q])
        start = pl.multiple_of(spot(x_at, 2) * n, n)
        send(go.at[i, pl.ds(start, n // 2), :], g3t.at[:, q])
        send(go.at[i, pl.ds(pl.multiple_of(start + n // 2, n // 2), n // 2), :], g3b.at[:, q])
    for c in outs:
        c.wait()


def exchange_body(gw_all, out):
    out[...] = jnp.broadcast_to(jnp.sum(gw_all[...], 0, keepdims=True), out.shape)


def column_body(at, gw, gates, top, bot, out, gl):
    x_at, zh_at, e_at = at[0], at[3], at[2]
    n_rows = gates.shape[0]
    n = n_rows // RING
    n_half = top.shape[1] // 2
    row = lax.broadcasted_iota(jnp.int32, (n_rows, n_rows), 0)
    col = lax.broadcasted_iota(jnp.int32, (n_rows, n_rows), 1)
    code = gates[:, 1:2].astype(jnp.int32)
    mate = (row // CAP) * CAP + code % CAP

    def fetch(mask):
        return lax.dot_general(
            mask.astype(F32), gw[...], (((1,), (1,)), ((), ())),
            preferred_element_type=F32, precision=lax.Precision.HIGHEST,
        )

    lane = lax.broadcasted_iota(jnp.int32, (n_rows, N_EXP), 1)
    diff = jnp.where(lane == e_at, fetch(row == col), 0.0) - jnp.where(
        lane == code // CAP, fetch(mate == col), 0.0
    )
    gl[...] = jnp.broadcast_to(gates[:, :1] * jnp.sum(diff, 1, keepdims=True), gl.shape)
    feat = pl.ds(pl.multiple_of(zh_at * n_half, n_half), n_half)
    acc = None
    for i in range(RING):
        a = (top, bot)[i // 2][(i % 2) * n : (i % 2 + 1) * n, feat].astype(F32)
        g = gl[pl.ds(pl.multiple_of(spot(x_at, OFFS[i]) * n, n), n), :1]
        s = jnp.sum(a * g, 0, keepdims=True)
        acc = s if i == 0 else acc + s
    q = n_half // 2
    high = acc.astype(BF16).astype(F32)
    low = acc - high
    four = jnp.concatenate([high[:, :q], high[:, q:], low[:, :q], low[:, q:]], 0)
    block = jnp.concatenate([four, four], 0)
    for k in range(out.shape[0] // 16):
        out[k * 16 : (k + 1) * 16] = jnp.concatenate([block, block], 0).astype(BF16)


def add_body(right, up, left, down, right_out, left_out):
    right_out[...] = (right[...].astype(F32) + up[...].astype(F32)).astype(BF16)
    left_out[...] = (left[...].astype(F32) + down[...].astype(F32)).astype(BF16)


def ring_reduce(own, left, right, far_t, far_b, axis):
    up = shift(far_t, axis, 1)
    down = shift(far_b, axis, -1)
    half, width = far_t.shape
    steps = 4
    top = pl.BlockSpec((half, width // steps), lambda j: (0, j))
    bottom = pl.BlockSpec((half, width // steps), lambda j: (1, j))
    like = sds(right.shape, BF16)
    right, left = pl.pallas_call(
        add_body,
        grid=(steps,),
        out_shape=(like, like),
        in_specs=[top, top, bottom, top],
        out_specs=(top, bottom),
        input_output_aliases={0: 0, 2: 1},
        compiler_params=pltpu.CompilerParams(vmem_limit_bytes=16 << 20),
    )(right, up, left, down)
    return own, shift(right, axis, 1), shift(left, axis, -1)


def sum_rows_body(at, a, b, c, o0, o1, o2, o3):
    n = o0.shape[0]
    for i, o in enumerate((o0, o1, o2, o3)):
        s = pl.ds(pl.multiple_of(spot(at[0], OFFS[i]) * n, n), n)
        o[...] = (a[s].astype(F32) + b[s].astype(F32) + c[s].astype(F32)).astype(BF16)


def sum_rows(at, a, b, c):
    rows, width = a.shape
    steps = 4
    full = pl.BlockSpec((rows, width // steps), lambda j: (0, j))
    part = pl.BlockSpec((rows // RING, width // steps), lambda j: (0, j))
    return pl.pallas_call(
        sum_rows_body,
        grid=(steps,),
        out_shape=(sds((rows // RING, width), BF16),) * RING,
        in_specs=[SMEM] + [full] * 3,
        out_specs=(part,) * RING,
        compiler_params=pltpu.CompilerParams(vmem_limit_bytes=16 << 20),
    )(at, a, b, c)


def sum_lanes_body(a, b, c, out):
    out[0] = (a[...].astype(F32) + b[...].astype(F32) + c[...].astype(F32)).astype(BF16)


def sum_lanes(a, b, c):
    rows, width = a.shape
    part = pl.BlockSpec((rows, width // RING), lambda j: (0, j))
    return pl.pallas_call(
        sum_lanes_body,
        grid=(RING,),
        out_shape=sds((RING, rows, width // RING), BF16),
        in_specs=[part] * 3,
        out_specs=pl.BlockSpec((1, rows, width // RING), lambda j: (j, 0, 0)),
        compiler_params=pltpu.CompilerParams(vmem_limit_bytes=16 << 20),
    )(a, b, c)


def last_body(a0, a1, a2, a3, g, column, out):
    width = a0.shape[1]
    total = a0[...].astype(F32) + a1[...].astype(F32) + (a2[...].astype(F32) + a3[...].astype(F32))
    out[:, :width] = total.astype(BF16)
    total = g[0].astype(F32) + g[1].astype(F32) + (g[2].astype(F32) + g[3].astype(F32))
    out[:, width : 2 * width] = total.astype(BF16)
    out[:, 2 * width :] = column[...]


def combine_body(pick, got, moe_out, gt_out, gr_out):
    width = moe_out.shape[1]
    two = pick[...]
    moe_out[...] = dot(two, got[:, :width]).astype(BF16)
    gt_out[...] = dot(two, got[:, width : 2 * width]).astype(BF16)
    tail = got[:, 2 * width :]
    q = tail.shape[1]
    n_got = got.shape[0]
    e = lax.broadcasted_iota(jnp.int32, (N_EXP, n_got), 0)
    r = lax.broadcasted_iota(jnp.int32, (N_EXP, n_got), 1)
    for zh in range(2):
        for c in range(2):
            base = (zh * N_EXP + e) * CAP + c
            high, low = ((r == base + k).astype(F32).astype(BF16) for k in (0, 2))
            parts = dot(high, tail) + dot(low, tail)
            gr_out[:, (zh * 2 + c) * q : (zh * 2 + c + 1) * q] = parts


def on_device(tokens, routes, router, gate_proj, up_proj, down_proj, grad_out):
    rows, quarter = tokens.shape
    at = jnp.stack(
        [lax.axis_index("x"), lax.axis_index("y"), lax.axis_index(EXP), lax.axis_index("zh")]
    ).astype(jnp.int32)
    gate, up, down = gate_proj[0], up_proj[0], down_proj[0]
    width = RING * quarter
    n_ff = gate.shape[1]

    flat = routes.reshape(-1)
    ids = jnp.arange(flat.shape[0], dtype=jnp.int32)
    same = (flat[:, None] == flat[None, :]) & (ids[None, :] < ids[:, None])
    slot = jnp.sum(same.astype(jnp.int32), axis=1)
    code = (flat * CAP + slot).reshape(rows, 2)
    lanes = jnp.arange(SLOTS, dtype=jnp.int32)
    hot = (code[:, :, None] == lanes[None, None, :]).astype(F32)
    pick_b = jnp.sum(hot, axis=1).astype(BF16)
    meta = jnp.sum(hot * code[:, ::-1, None].astype(F32), axis=(0, 1))

    def pack(a):
        return lax.dot_general(
            pick_b, a, (((0,), (0,)), ((), ())), preferred_element_type=F32
        ).astype(BF16)

    def to_owner(a):
        a = a.reshape(N_EXP, CAP, -1)
        a = lax.all_to_all(jnp.concatenate([a, a], 0), ZAX, 0, 0, tiled=True)
        return a.reshape(2 * SLOTS, -1)

    meta = jnp.broadcast_to(meta[:, None], (SLOTS, LANES)).astype(BF16)
    got_x = to_owner(jnp.concatenate([pack(tokens), meta], 1))
    got_dy = to_owner(pack(grad_out))
    n_own = got_x.shape[0]
    n_rows = RING * n_own
    half = n_rows // 2

    all_dy = lax.all_gather(got_dy, ("x", "y"), axis=0)
    pieces = [got_x] + [shift(got_x, "x", n) for n in (1, -1, 2)]
    part = sds((half, quarter), BF16)
    top, bot, meta_all = kernel(
        rows_body, (part, part, sds((n_rows, LANES), BF16)), *pieces, specs=[VMEM] * 4
    )
    left_t = shift(top, "y", 1)
    right_b = shift(bot, "y", -1)
    left_b = shift(bot, "y", 1)
    right_t = shift(top, "y", -1)
    far_t = shift(left_t, "y", 1)
    far_b = shift(right_b, "y", -1)

    near = sds((n_rows, quarter), BF16)
    g_far = sds((n_own // 2, width), BF16)
    g_near = sds((n_own, width), BF16)
    n_shards = 2 * RING * RING
    sem = pltpu.SemaphoreType.DMA
    *parts, gw, gates = kernel(
        expert_body,
        (near, near, near, part, part, g_near, g_near, g_near, g_far, g_far,
         sds((n_shards, n_rows), F32), sds((n_rows, LANES), F32)),
        at, top, bot, left_t, left_b, right_t, right_b, far_t, far_b, all_dy, meta_all,
        gate, up, down, router.T,
        specs=[SMEM] + [ANY] * 13 + [VMEM],
        out_specs=(ANY,) * 10 + (VMEM, VMEM),
        scratch=[
            pltpu.VMEM((RING, n_rows, quarter), BF16), pltpu.VMEM((RING, n_rows, quarter), BF16),
            pltpu.VMEM((RING, quarter, n_ff), BF16), pltpu.VMEM((RING, quarter, n_ff), BF16),
            pltpu.VMEM((RING, n_ff, quarter), BF16), pltpu.VMEM((n_rows, LANES), BF16),
            pltpu.VMEM((RING, 4 * N_EXP, quarter), BF16),
            pltpu.VMEM((n_rows, n_ff), BF16), pltpu.VMEM((n_rows, n_ff), BF16),
            pltpu.VMEM((n_rows, n_ff), BF16), pltpu.VMEM((n_rows, 4 * N_EXP), BF16),
            pltpu.VMEM((RING, n_rows, quarter), BF16), pltpu.VMEM((RING, n_rows, quarter), BF16),
            sem((RING * RING,)), sem((RING * RING,)), sem((RING,)), sem((RING,)), sem((RING,)),
            sem((RING,)), sem((5 + 5 * RING,)),
        ],
        limit=44,
    )

    gw_all = lax.all_to_all(
        gw.reshape(n_shards, 2, n_rows // 2), ("x", "zh", "y"), 0, 0, tiled=True
    )
    gw_exp = lax.all_to_all(
        kernel(exchange_body, sds((N_EXP, 2, n_rows // 2), F32), gw_all, specs=[VMEM]),
        EXP, 0, 0, tiled=True,
    ).reshape(N_EXP, n_rows)
    column = kernel(
        column_body, sds((n_own, quarter // 4), BF16), at, gw_exp, gates, top, bot,
        specs=[SMEM] + [VMEM] * 4, scratch=[pltpu.VMEM((n_rows, LANES), F32)],
    )

    out_terms = ring_reduce(*parts[:5], "y")
    grad_terms = ring_reduce(*parts[5:], "x")
    out_x = sum_rows(at, *out_terms)
    grad_got = lax.all_to_all(sum_lanes(*grad_terms), "y", 0, 0, tiled=True)
    out_got = [out_x[0]] + [shift(out_x[i], "x", OFFS[i]) for i in (1, 2, 3)]
    final = kernel(
        last_body, sds((n_own, 2 * quarter + quarter // 4), BF16), *out_got, grad_got, column,
        specs=[VMEM] * 6,
    )
    final = lax.all_to_all(final.reshape(2 * N_EXP, CAP, -1), ZAX, 0, 0, tiled=True)
    res = sds((rows, quarter), BF16)
    moe_out, grad_tokens, grad_router = kernel(
        combine_body, (res, res, sds((N_EXP, quarter), F32)),
        jnp.concatenate([pick_b, pick_b], 1), final.reshape(2 * SLOTS, -1), specs=[VMEM] * 2,
    )
    return (moe_out, grad_tokens, grad_router.T)


def solution(mesh):
    fine = Mesh(mesh.devices.reshape(4, 2, 4, 2, 4), ("x", "zh", "zl", "c", "y"))
    return jax.shard_map(
        on_device,
        mesh=fine,
        in_specs=(
            P(ALL, "y"),
            P(ALL, None),
            P(),
            P(EXP, None, ("x", "zh", "y")),
            P(EXP, None, ("x", "zh", "y")),
            P(EXP, ("x", "zh", "y"), None),
            P(ALL, "y"),
        ),
        out_specs=(P(ALL, "y"), P(ALL, "y"), P("y", None)),
        check_vma=False,
    )
```

time: 238 us -> 227 us (0.954)
  local copies, waits for them, and re-layouts: 56.1 us -> 11.6 us
  blocking collectives: 24.7 us -> 48.8 us
  Pallas kernels: 16.9 us -> 34.7 us
  between operations: 1 us -> 14.2 us
  starting transfers between devices: 56.9 us -> 43.8 us
  other arithmetic: 12.4 us -> 0.73 us
  waiting for transfers between devices: 66.8 us -> 70.8 us
    all_to_all x1 -> x3, blocking collectives: 24.7 us -> 48.8 us  [the longest x2 33.5 us: to_owner(): a = lax.all_to_all(jnp.concatenate([a, a], 0), ZAX, 0, 0, tiled=True)]
    ppermute x22 -> x20, waiting for transfers between devices: 30.4 us -> 53.9 us  [shift(): return lax.ppermute(a, axis, [(i, (i + n) % RING) for i in range(RING)])]
    all_to_all x6 -> x3, waiting for transfers between devices: 36.4 us -> 16.8 us  [the longest x1 15.5 us: on_device(): lax.all_to_all(final.reshape(2 * N_EXP, CAP, -1), ZAX, 0, 0, tiled=True)]
    unnamed x81 -> x26, local copies, waits for them, and re-layouts: 28.7 us -> 9.26 us
    pallas_call x8 -> x10, Pallas kernels: 16.9 us -> 34.7 us  [the longest x6 21.9 us: kernel(): pl.pallas_call(body, out_shape=outs, in_specs=list(specs), out_specs=out_...]
    all_to_all x6 -> x3, starting transfers between devices: 31.8 us -> 18.5 us  [the longest x1 8.53 us: on_device(): lax.all_to_all(kernel(exchange_body, sds((N_EXP, 2, n_rows // 2), F32), g...]
    concatenate x2 -> x0, local copies, waits for them, and re-layouts: 9.18 us -> none  [the longest x1 9.1 us: on_device(): jnp.concatenate([parts[0], parts[0], parts[1], parts[1], pad], 1)]
    convert_element_type x5 -> x0, other arithmetic: 6.37 us -> none  [the longest x2 5.05 us: split3(): mid = rest.astype(BF16)]
  transfers between devices with their start and end apart: 28 -> 24, of which waited for: 9 -> 13; matrix products, arithmetic and copies ran while one was open for 17% -> 1% of each run, Pallas kernels for 3% -> 7%
where the time goes in v2:
time: 227 us; the launch traced here: 226 us
  waiting for transfers between devices  70.8 us (31%)
  blocking collectives  48.8 us (21%)
  starting transfers between devices  43.8 us (19%)
  Pallas kernels  34.7 us (15%)
  between operations  14.2 us (6%)
  local copies, waits for them, and re-layouts  11.6 us (5%)
    ppermute x20, waiting for transfers between devices, shift(): return lax.ppermute(a, axis, [(i, (i + n) % RING) for i in range(RING)])  53.9 us
    all_to_all x2, blocking collectives, to_owner(): a = lax.all_to_all(jnp.concatenate([a, a], 0), ZAX, 0, 0, tiled=True)  33.5 us
    ppermute x20, starting transfers between devices, shift(): return lax.ppermute(a, axis, [(i, (i + n) % RING) for i in range(RING)])  25.3 us
    pallas_call x6, Pallas kernels, kernel(): pl.pallas_call(body, out_shape=outs, in_specs=list(specs), out_specs=out_...  21.9 us
    all_to_all x1, waiting for transfers between devices, on_device(): lax.all_to_all(final.reshape(2 * N_EXP, CAP, -1), ZAX, 0, 0, tiled=True)  15.5 us
    all_to_all x1, blocking collectives, on_device(): lax.all_to_all(gw.reshape(n_shards, 2, n_rows // 2), ('x', 'zh', 'y'), 0,...  15.4 us
    unnamed x26, local copies, waits for them, and re-layouts  9.26 us
    all_to_all x1, starting transfers between devices, on_device(): lax.all_to_all(kernel(exchange_body, sds((N_EXP, 2, n_rows // 2), F32), g...  8.53 us
  transfers between devices with their start and end apart: 24, of which 13 were waited for; matrix products, arithmetic and copies ran while one was open for 1% of the time, Pallas kernels for 7%

profile of v2, /device:TPU:1, one launch (start us, length us, event | category | flops | bytes accessed | tf_op | source)
XLA Modules:
  0.0 225.7 jit_solution(17987821695003973371)
XLA Ops:
  9.1 20.1 %all_to_all.30 = bf16[16,4,1536]{2,1,0:T(4,128)(2,1)S(1)} all-to-all(bf16[16,4,1536]{2,1,0:T(4,128)(2,1)S(1)} %pad_maximum_fusion.1), channel_id=1, replica_groups=mesh['x'=4,'zh'=2,'zl'=4,'c'=2,'y'=4] {'zh','zl','c'}, dimensions={0} | all-to-all | bytes 393216 | tf_op jit(solution)/shard_map/all_to_all | solution.py:356
  31.2 13.4 %all_to_all.31 = bf16[16,4,1664]{2,1,0:T(4,128)(2,1)S(1)} all-to-all(bf16[16,4,1664]{2,1,0:T(4,128)(2,1)S(1)} %pad_maximum_fusion), channel_id=1, replica_groups=mesh['x'=4,'zh'=2,'zl'=4,'c'=2,'y'=4] {'zh','zl','c'}, dimensions={0} | all-to-all | bytes 425984 | tf_op jit(solution)/shard_map/all_to_all | solution.py:356
  44.6 2.8 %collective-permute-start.2 = (bf16[64,1664]{1,0:T(8,128)(2,1)S(1)}, bf16[64,1664]{1,0:T(8,128)(2,1)S(1)}, u32[]{:S(2)}, u32[]{:S(2)}) collective-permute-start(bf16[64,1664]{1,0:T(8,128)(2,1)S(1)} %reshape.42.own), channel_id=1, source_target_pairs={{0,128},{64,192},{128,0},{192,64},{1,129},{65,193},{129,1},{193,65... | collective-permute-start | bytes 638984 | tf_op jit(solution)/shard_map/ppermute | solution.py:31
  48.9 5.8 %collective-permute-done.2.far = bf16[64,1664]{1,0:T(8,128)(2,1)S(1)} collective-permute-done((bf16[64,1664]{1,0:T(8,128)(2,1)S(1)}, bf16[64,1664]{1,0:T(8,128)(2,1)S(1)}, u32[]{:S(2)}, u32[]{:S(2)}) %collective-permute-start.2) | collective-permute-done | bytes 213024 | tf_op jit(solution)/shard_map/ppermute | solution.py:31
  54.7 4.2 %collective-permute-done.1.right = bf16[64,1664]{1,0:T(8,128)(2,1)S(1)} collective-permute-done((bf16[64,1664]{1,0:T(8,128)(2,1)S(1)}, bf16[64,1664]{1,0:T(8,128)(2,1)S(1)}, u32[]{:S(2)}, u32[]{:S(2)}) %collective-permute-start.1) | collective-permute-done | bytes 213024 | tf_op jit(solution)/shard_map/ppermute | solution.py:31
  60.8 1.9 collective-permute-start.6
  62.7 1.1 collective-permute-start.5
  64.2 8.4 %collective-permute-done.3.x1t = bf16[128,1536]{1,0:T(8,128)(2,1)S(1)} collective-permute-done((bf16[128,1536]{1,0:T(8,128)(2,1)S(1)}, bf16[128,1536]{1,0:T(8,128)(2,1)S(1)}, u32[]{:S(2)}, u32[]{:S(2)}) %collective-permute-start.3) | collective-permute-done | bytes 393248 | tf_op jit(solution)/shard_map/ppermute | solution.py:31
  72.7 1.0 collective-permute-done.6.x2b
  73.7 3.5 %collective-permute-start.8 = (bf16[128,1536]{1,0:T(8,128)(2,1)S(1)}, bf16[128,1536]{1,0:T(8,128)(2,1)S(1)}, u32[]{:S(2)}, u32[]{:S(2)}) collective-permute-start(bf16[128,1536]{1,0:T(8,128)(2,1)S(1)} %collective-permute-done.6.x2b), channel_id=1, source_target_pairs={{0,3},{1,0},{2,1},{3,2},{4,7},{5,4},{6,5},{7,6},{8,11},{9,8},{10,9... | collective-permute-start | bytes 1179656 | tf_op jit(solution)/shard_map/ppermute | solution.py:31
  77.3 13.3 %collective-permute-done.5.x2t = bf16[128,1536]{1,0:T(8,128)(2,1)S(1)} collective-permute-done((bf16[128,1536]{1,0:T(8,128)(2,1)S(1)}, bf16[128,1536]{1,0:T(8,128)(2,1)S(1)}, u32[]{:S(2)}, u32[]{:S(2)}) %collective-permute-start.5) | collective-permute-done | bytes 393248 | tf_op jit(solution)/shard_map/ppermute | solution.py:31
  92.1 8.9 %collective-permute-done.7.x3t = bf16[128,1536]{1,0:T(8,128)(2,1)S(1)} collective-permute-done((bf16[128,1536]{1,0:T(8,128)(2,1)S(1)}, bf16[128,1536]{1,0:T(8,128)(2,1)S(1)}, u32[]{:S(2)}, u32[]{:S(2)}) %collective-permute-start.7) | collective-permute-done | bytes 393248 | tf_op jit(solution)/shard_map/ppermute | solution.py:31
  107.3 18.6 %shard_map.95 = (bf16[256,1536]{1,0:T(8,128)(2,1)S(1)}, bf16[256,1536]{1,0:T(8,128)(2,1)}, bf16[256,1536]{1,0:T(8,128)(2,1)}, bf16[128,1536]{1,0:T(8,128)(2,1)S(...) custom-call(s32[4]{0:T(128)S(1)} %pad_add_fusion.at, ...), custom_call_target="tpu_custom_call" | custom-call | tf_op jit(solution)/shard_map/pallas_call | solution.py:44
  126.6 2.1 collective-permute-start.17
  128.7 2.7 %collective-permute-start.10 = (bf16[128,1536]{1,0:T(8,128)(2,1)S(1)}, bf16[128,1536]{1,0:T(8,128)(2,1)S(1)}, u32[]{:S(2)}, u32[]{:S(2)}) collective-permute-start(bf16[128,1536]{1,0:T(8,128)(2,1)S(1)} %get-tuple-element.36), channel_id=1, source_target_pairs={{0,3},{1,0},{2,1},{3,2},{4,7},{5,4},{6,5},{7,6},{8,11},{9,8},{10,9... | collective-permute-start | bytes 1179656 | tf_op jit(solution)/shard_map/ppermute | solution.py:31
  131.4 5.2 %collective-permute-done.16.up = bf16[32,6144]{1,0:T(8,128)(2,1)S(1)} collective-permute-done((bf16[32,6144]{1,0:T(8,128)(2,1)S(1)}, bf16[32,6144]{1,0:T(8,128)(2,1)S(1)}, u32[]{:S(2)}, u32[]{:S(2)}) %collective-permute-start.16) | collective-permute-done | bytes 393248 | tf_op jit(solution)/shard_map/ppermute | solution.py:31
  136.5 3.3 %shard_map.98 = (bf16[64,6144]{1,0:T(8,128)(2,1)}, bf16[64,6144]{1,0:T(8,128)(2,1)}) custom-call(bf16[64,6144]{1,0:T(8,128)(2,1)} %get-tuple-element.44.right, bf16[32,6144]{1,0:T(8,128)(2,1)S(1)} %collective-permute-done.16.up, bf16[64,6144]{1,0:T(8,128)(2,1)} %get-tuple-element.46.left, ...), custom_call_target="tpu_custom_call", output_to_operand_aliasing={{0}: (0, {}), {1}: (2, {})} | custom-call | tf_op jit(solution)/shard_map/pallas_call | solution.py:252
  139.9 2.7 %collective-permute-start.19 = (bf16[64,6144]{1,0:T(8,128)(2,1)}, bf16[64,6144]{1,0:T(8,128)(2,1)}, u32[]{:S(2)}, u32[]{:S(2)}) collective-permute-start(bf16[64,6144]{1,0:T(8,128)(2,1)} %get-tuple-element.49), channel_id=1, source_target_pairs={{0,192},{64,0},{128,64},{192,128},{1,193},{65,1},{129,65},{193,129... | collective-permute-start | bytes 2359304 | tf_op jit(solution)/shard_map/ppermute | solution.py:31
  142.6 3.4 %shard_map.96 = (bf16[256,1536]{1,0:T(8,128)(2,1)}, bf16[256,1536]{1,0:T(8,128)(2,1)}) custom-call(bf16[256,1536]{1,0:T(8,128)(2,1)} %get-tuple-element.33.right, bf16[128,1536]{1,0:T(8,128)(2,1)S(1)} %collective-permute-done.9.up, bf16[256,1536]{1,0:T(8,128)(2,1)} %get-tuple-element.35.left, ...), custom_call_target="tpu_custom_call", output_to_operand_aliasing={{0}: (0, {}), {1}: (2, {})} | custom-call | tf_op jit(solution)/shard_map/pallas_call | solution.py:252
  146.0 2.7 %collective-permute-start.12 = (bf16[256,1536]{1,0:T(8,128)(2,1)}, bf16[256,1536]{1,0:T(8,128)(2,1)}, u32[]{:S(2)}, u32[]{:S(2)}) collective-permute-start(bf16[256,1536]{1,0:T(8,128)(2,1)} %get-tuple-element.38), channel_id=1, source_target_pairs={{0,3},{1,0},{2,1},{3,2},{4,7},{5,4},{6,5},{7,6},{8,11},{9,8},{10,9... | collective-permute-start | bytes 2359304 | tf_op jit(solution)/shard_map/ppermute | solution.py:31
  148.6 15.4 %all_to_all.32.gw_all = f32[32,2,128]{2,1,0:T(2,128)S(1)} all-to-all(f32[32,2,128]{2,1,0:T(2,128)S(1)} %reshape.44), channel_id=1, replica_groups=mesh['x'=4,'zh'=2,'zl'=4,'c'=2,'y'=4] {'x','zh','y'}, dimensions={0} | all-to-all | bytes 65536 | tf_op jit(solution)/shard_map/all_to_all | solution.py:406
  164.7 8.5 %all-to-all-start.4 = ((f32[8,2,128]{2,1,0:T(2,128)}), f32[8,2,128]{2,1,0:T(2,128)S(1)}, u32[]{:S(2)}, u32[]{:S(2)}) async-start(f32[8,2,128]{2,1,0:T(2,128)} %shard_map.100), calls=%async_computation.4 | async-start | bytes 16384 | tf_op jit(solution)/shard_map/all_to_all | solution.py:409
  173.2 3.6 %shard_map.99 = bf16[4,64,1536]{2,1,0:T(8,128)(2,1)} custom-call(bf16[64,6144]{1,0:T(8,128)(2,1)S(1)} %get-tuple-element.43.a, bf16[64,6144]{1,0:T(8,128)(2,1)} %collective-permute-done.18.b, bf16[64,6144]{1,0:T(8,128)(2,1)} %collective-permute-done.19.c), custom_call_target="tpu_custom_call" | custom-call | tf_op jit(solution)/shard_map/pallas_call | solution.py:293
  176.8 1.3 all-to-all-done.4
  178.1 3.5 %all-to-all-start.2 = ((bf16[4,64,1536]{2,1,0:T(8,128)(2,1)}), bf16[4,64,1536]{2,1,0:T(8,128)(2,1)S(1)}, u32[]{:S(2)}, u32[]{:S(2)}) async-start(bf16[4,64,1536]{2,1,0:T(8,128)(2,1)} %shard_map.99), calls=%async_computation.2 | async-start | bytes 1572864 | tf_op jit(solution)/shard_map/all_to_all | solution.py:421
  181.6 2.4 %shard_map.97 = (bf16[64,1536]{1,0:T(8,128)(2,1)S(1)}, bf16[64,1536]{1,0:T(8,128)(2,1)S(1)}, bf16[64,1536]{1,0:T(8,128)(2,1)S(1)}, bf16[64,1536]{1,0:T(8,128)(2,1)S(1)}) custom-call(s32[4]{0:T(128)S(1)} %pad_add_fusion.at, bf16[256,1536]{1,0:T(8,128)(2,1)S(1)} %get-tuple-element.32.a, bf16[256,1536]{1,0:T(8,128)(2,1)S(1)} %collective-permute-done.11.b, ...), custom_call_target="tpu_custom_call" | custom-call | tf_op jit(solution)/shard_map/pallas_call | solution.py:276
  186.6 1.6 shard_map.101.column
  188.1 1.7 collective-permute-done.13.a1
  189.9 2.9 %collective-permute-done.14.a2 = bf16[64,1536]{1,0:T(8,128)(2,1)S(1)} collective-permute-done((bf16[64,1536]{1,0:T(8,128)(2,1)S(1)}, bf16[64,1536]{1,0:T(8,128)(2,1)S(1)}, u32[]{:S(2)}, u32[]{:S(2)}) %collective-permute-start.14) | collective-permute-done | bytes 196640 | tf_op jit(solution)/shard_map/ppermute | solution.py:31
  192.7 2.0 collective-permute-done.15.a3
  195.8 6.5 %all-to-all-start.5 = ((bf16[16,4,3456]{2,1,0:T(4,128)(2,1)}), bf16[16,4,3456]{2,1,0:T(4,128)(2,1)S(1)}, u32[]{:S(2)}, u32[]{:S(2)}) async-start(bf16[16,4,3456]{2,1,0:T(4,128)(2,1)} %reshape.46), calls=%async_computation.5 | async-start | bytes 884736 | tf_op jit(solution)/shard_map/all_to_all | solution.py:427
  202.4 15.5 %all-to-all-done.5 = bf16[16,4,3456]{2,1,0:T(4,128)(2,1)S(1)} async-done(((bf16[16,4,3456]{2,1,0:T(4,128)(2,1)}), bf16[16,4,3456]{2,1,0:T(4,128)(2,1)S(1)}, u32[]{:S(2)}, u32[]{:S(2)}) %all-to-all-start.5) | async-done | bytes 442400 | tf_op jit(solution)/shard_map/all_to_all | solution.py:427
  (80 shorter events, 21.6 us)
Async XLA Ops:
  7.2 1.6 copy-start
  7.2 95.3 %copy-start.9 = (f32[6144,8]{0,1:T(8,128)S(1)}, f32[6144,8]{0,1:T(8,128)}, u32[]{:S(2)}) copy-start(f32[6144,8]{0,1:T(8,128)} %param.9) | copy-start | bytes 589828
  7.2 95.3 %all-gather.2.cloned.1.call-start = ((), (), s32[]{:S(2)}) async-start(), calls=%async_computation.6 | async-start | bytes 3342336 | tf_op jit(solution)/shard_map/all_gather | solution.py:366
  44.6 10.1 %collective-permute-start.2 = (bf16[64,1664]{1,0:T(8,128)(2,1)S(1)}, bf16[64,1664]{1,0:T(8,128)(2,1)S(1)}, u32[]{:S(2)}, u32[]{:S(2)}) collective-permute-start(bf16[64,1664]{1,0:T(8,128)(2,1)S(1)} %reshape.42.own), channel_id=1, source_target_pairs={{0,128},{64,192},{128,0},{192,64},{1,129},{65,193},{129,1},{193,65... | collective-permute-start | bytes 638984 | tf_op jit(solution)/shard_map/ppermute | solution.py:31
  47.5 11.5 %collective-permute-start.1 = (bf16[64,1664]{1,0:T(8,128)(2,1)S(1)}, bf16[64,1664]{1,0:T(8,128)(2,1)S(1)}, u32[]{:S(2)}, u32[]{:S(2)}) collective-permute-start(bf16[64,1664]{1,0:T(8,128)(2,1)S(1)} %reshape.42.own), channel_id=1, source_target_pairs={{0,192},{64,0},{128,64},{192,128},{1,193},{65,1},{129,65},{193,129... | collective-permute-start | bytes 638984 | tf_op jit(solution)/shard_map/ppermute | solution.py:31
  48.3 11.0 %collective-permute-start = (bf16[64,1664]{1,0:T(8,128)(2,1)S(1)}, bf16[64,1664]{1,0:T(8,128)(2,1)S(1)}, u32[]{:S(2)}, u32[]{:S(2)}) collective-permute-start(bf16[64,1664]{1,0:T(8,128)(2,1)S(1)} %reshape.42.own), channel_id=1, source_target_pairs={{0,64},{64,128},{128,192},{192,0},{1,65},{65,129},{129,193},{193,1... | collective-permute-start | bytes 638984 | tf_op jit(solution)/shard_map/ppermute | solution.py:31
  60.0 12.6 %collective-permute-start.3 = (bf16[128,1536]{1,0:T(8,128)(2,1)S(1)}, bf16[128,1536]{1,0:T(8,128)(2,1)S(1)}, u32[]{:S(2)}, u32[]{:S(2)}) collective-permute-start(bf16[128,1536]{1,0:T(8,128)(2,1)S(1)} %get-tuple-element.29.x0t.top), channel_id=1, source_target_pairs={{0,1},{1,2},{2,3},{3,0},{4,5},{5,6},{6,7},{7,4},{8,9},{9,10},{10,1... | collective-permute-start | bytes 1179656 | tf_op jit(solution)/shard_map/ppermute | solution.py:31
  60.8 12.9 %collective-permute-start.6 = (bf16[128,1536]{1,0:T(8,128)(2,1)S(1)}, bf16[128,1536]{1,0:T(8,128)(2,1)S(1)}, u32[]{:S(2)}, u32[]{:S(2)}) collective-permute-start(bf16[128,1536]{1,0:T(8,128)(2,1)S(1)} %get-tuple-element.30.x0b.bot), channel_id=1, source_target_pairs={{0,3},{1,0},{2,1},{3,2},{4,7},{5,4},{6,5},{7,6},{8,11},{9,8},{10,9... | collective-permute-start | bytes 1179656 | tf_op jit(solution)/shard_map/ppermute | solution.py:31
  62.7 27.8 %collective-permute-start.5 = (bf16[128,1536]{1,0:T(8,128)(2,1)S(1)}, bf16[128,1536]{1,0:T(8,128)(2,1)S(1)}, u32[]{:S(2)}, u32[]{:S(2)}) collective-permute-start(bf16[128,1536]{1,0:T(8,128)(2,1)S(1)} %get-tuple-element.29.x0t.top), channel_id=1, source_target_pairs={{0,3},{1,0},{2,1},{3,2},{4,7},{5,4},{6,5},{7,6},{8,11},{9,8},{10,9... | collective-permute-start | bytes 1179656 | tf_op jit(solution)/shard_map/ppermute | solution.py:31
  63.8 27.5 %collective-permute-start.4 = (bf16[128,1536]{1,0:T(8,128)(2,1)S(1)}, bf16[128,1536]{1,0:T(8,128)(2,1)S(1)}, u32[]{:S(2)}, u32[]{:S(2)}) collective-permute-start(bf16[128,1536]{1,0:T(8,128)(2,1)S(1)} %get-tuple-element.30.x0b.bot), channel_id=1, source_target_pairs={{0,1},{1,2},{2,3},{3,0},{4,5},{5,6},{6,7},{7,4},{8,9},{9,10},{10,1... | collective-permute-start | bytes 1179656 | tf_op jit(solution)/shard_map/ppermute | solution.py:31
  72.6 28.4 %collective-permute-start.7 = (bf16[128,1536]{1,0:T(8,128)(2,1)S(1)}, bf16[128,1536]{1,0:T(8,128)(2,1)S(1)}, u32[]{:S(2)}, u32[]{:S(2)}) collective-permute-start(bf16[128,1536]{1,0:T(8,128)(2,1)S(1)} %collective-permute-done.3.x1t), channel_id=1, source_target_pairs={{0,1},{1,2},{2,3},{3,0},{4,5},{5,6},{6,7},{7,4},{8,9},{9,10},{10,1... | collective-permute-start | bytes 1179656 | tf_op jit(solution)/shard_map/ppermute | solution.py:31
  73.7 28.1 %collective-permute-start.8 = (bf16[128,1536]{1,0:T(8,128)(2,1)S(1)}, bf16[128,1536]{1,0:T(8,128)(2,1)S(1)}, u32[]{:S(2)}, u32[]{:S(2)}) collective-permute-start(bf16[128,1536]{1,0:T(8,128)(2,1)S(1)} %collective-permute-done.6.x2b), channel_id=1, source_target_pairs={{0,3},{1,0},{2,1},{3,2},{4,7},{5,4},{6,5},{7,6},{8,11},{9,8},{10,9... | collective-permute-start | bytes 1179656 | tf_op jit(solution)/shard_map/ppermute | solution.py:31
  91.3 0.8 copy-start.3
  102.5 1.0 copy-start.2
  103.5 1.0 copy-start.4
  104.5 1.0 copy-start.6
  105.5 1.0 copy-start.8
  106.5 0.8 copy-start.11
  125.9 10.6 %collective-permute-start.16 = (bf16[32,6144]{1,0:T(8,128)(2,1)S(1)}, bf16[32,6144]{1,0:T(8,128)(2,1)S(1)}, u32[]{:S(2)}, u32[]{:S(2)}) collective-permute-start(bf16[32,6144]{1,0:T(8,128)(2,1)S(1)} %get-tuple-element.45), channel_id=1, source_target_pairs={{0,64},{64,128},{128,192},{192,0},{1,65},{65,129},{129,193},{193,1... | collective-permute-start | bytes 1179656 | tf_op jit(solution)/shard_map/ppermute | solution.py:31
  126.6 9.9 %collective-permute-start.17 = (bf16[32,6144]{1,0:T(8,128)(2,1)S(1)}, bf16[32,6144]{1,0:T(8,128)(2,1)S(1)}, u32[]{:S(2)}, u32[]{:S(2)}) collective-permute-start(bf16[32,6144]{1,0:T(8,128)(2,1)S(1)} %get-tuple-element.47), channel_id=1, source_target_pairs={{0,192},{64,0},{128,64},{192,128},{1,193},{65,1},{129,65},{193,129... | collective-permute-start | bytes 1179656 | tf_op jit(solution)/shard_map/ppermute | solution.py:31
  128.7 13.9 %collective-permute-start.9 = (bf16[128,1536]{1,0:T(8,128)(2,1)S(1)}, bf16[128,1536]{1,0:T(8,128)(2,1)S(1)}, u32[]{:S(2)}, u32[]{:S(2)}) collective-permute-start(bf16[128,1536]{1,0:T(8,128)(2,1)S(1)} %get-tuple-element.34), channel_id=1, source_target_pairs={{0,1},{1,2},{2,3},{3,0},{4,5},{5,6},{6,7},{7,4},{8,9},{9,10},{10,1... | collective-permute-start | bytes 1179656 | tf_op jit(solution)/shard_map/ppermute | solution.py:31
  128.7 13.9 %collective-permute-start.10 = (bf16[128,1536]{1,0:T(8,128)(2,1)S(1)}, bf16[128,1536]{1,0:T(8,128)(2,1)S(1)}, u32[]{:S(2)}, u32[]{:S(2)}) collective-permute-start(bf16[128,1536]{1,0:T(8,128)(2,1)S(1)} %get-tuple-element.36), channel_id=1, source_target_pairs={{0,3},{1,0},{2,1},{3,2},{4,7},{5,4},{6,5},{7,6},{8,11},{9,8},{10,9... | collective-permute-start | bytes 1179656 | tf_op jit(solution)/shard_map/ppermute | solution.py:31
  139.9 33.3 %collective-permute-start.18 = (bf16[64,6144]{1,0:T(8,128)(2,1)}, bf16[64,6144]{1,0:T(8,128)(2,1)}, u32[]{:S(2)}, u32[]{:S(2)}) collective-permute-start(bf16[64,6144]{1,0:T(8,128)(2,1)} %get-tuple-element.48), channel_id=1, source_target_pairs={{0,64},{64,128},{128,192},{192,0},{1,65},{65,129},{129,193},{193,1... | collective-permute-start | bytes 2359304 | tf_op jit(solution)/shard_map/ppermute | solution.py:31
  139.9 33.3 %collective-permute-start.19 = (bf16[64,6144]{1,0:T(8,128)(2,1)}, bf16[64,6144]{1,0:T(8,128)(2,1)}, u32[]{:S(2)}, u32[]{:S(2)}) collective-permute-start(bf16[64,6144]{1,0:T(8,128)(2,1)} %get-tuple-element.49), channel_id=1, source_target_pairs={{0,192},{64,0},{128,64},{192,128},{1,193},{65,1},{129,65},{193,129... | collective-permute-start | bytes 2359304 | tf_op jit(solution)/shard_map/ppermute | solution.py:31
  146.0 35.7 %collective-permute-start.11 = (bf16[256,1536]{1,0:T(8,128)(2,1)}, bf16[256,1536]{1,0:T(8,128)(2,1)S(1)}, u32[]{:S(2)}, u32[]{:S(2)}) collective-permute-start(bf16[256,1536]{1,0:T(8,128)(2,1)} %get-tuple-element.37), channel_id=1, source_target_pairs={{0,1},{1,2},{2,3},{3,0},{4,5},{5,6},{6,7},{7,4},{8,9},{9,10},{10,1... | collective-permute-start | bytes 2359304 | tf_op jit(solution)/shard_map/ppermute | solution.py:31
  146.0 35.7 %collective-permute-start.12 = (bf16[256,1536]{1,0:T(8,128)(2,1)}, bf16[256,1536]{1,0:T(8,128)(2,1)}, u32[]{:S(2)}, u32[]{:S(2)}) collective-permute-start(bf16[256,1536]{1,0:T(8,128)(2,1)} %get-tuple-element.38), channel_id=1, source_target_pairs={{0,3},{1,0},{2,1},{3,2},{4,7},{5,4},{6,5},{7,6},{8,11},{9,8},{10,9... | collective-permute-start | bytes 2359304 | tf_op jit(solution)/shard_map/ppermute | solution.py:31
  164.7 13.5 %all-to-all-start.4 = ((f32[8,2,128]{2,1,0:T(2,128)}), f32[8,2,128]{2,1,0:T(2,128)S(1)}, u32[]{:S(2)}, u32[]{:S(2)}) async-start(f32[8,2,128]{2,1,0:T(2,128)} %shard_map.100), calls=%async_computation.4 | async-start | bytes 16384 | tf_op jit(solution)/shard_map/all_to_all | solution.py:409
  178.1 16.7 %all-to-all-start.2 = ((bf16[4,64,1536]{2,1,0:T(8,128)(2,1)}), bf16[4,64,1536]{2,1,0:T(8,128)(2,1)S(1)}, u32[]{:S(2)}, u32[]{:S(2)}) async-start(bf16[4,64,1536]{2,1,0:T(8,128)(2,1)} %shard_map.99), calls=%async_computation.2 | async-start | bytes 1572864 | tf_op jit(solution)/shard_map/all_to_all | solution.py:421
  184.1 5.8 %collective-permute-start.13 = (bf16[64,1536]{1,0:T(8,128)(2,1)S(1)}, bf16[64,1536]{1,0:T(8,128)(2,1)S(1)}, u32[]{:S(2)}, u32[]{:S(2)}) collective-permute-start(bf16[64,1536]{1,0:T(8,128)(2,1)S(1)} %get-tuple-element.40), channel_id=1, source_target_pairs={{0,192},{64,0},{128,64},{192,128},{1,193},{65,1},{129,65},{193,129... | collective-permute-start | bytes 589832 | tf_op jit(solution)/shard_map/ppermute | solution.py:31
  185.0 7.7 %collective-permute-start.14 = (bf16[64,1536]{1,0:T(8,128)(2,1)S(1)}, bf16[64,1536]{1,0:T(8,128)(2,1)S(1)}, u32[]{:S(2)}, u32[]{:S(2)}) collective-permute-start(bf16[64,1536]{1,0:T(8,128)(2,1)S(1)} %get-tuple-element.41), channel_id=1, source_target_pairs={{0,64},{64,128},{128,192},{192,0},{1,65},{65,129},{129,193},{193,1... | collective-permute-start | bytes 589832 | tf_op jit(solution)/shard_map/ppermute | solution.py:31
  185.6 9.2 %collective-permute-start.15 = (bf16[64,1536]{1,0:T(8,128)(2,1)S(1)}, bf16[64,1536]{1,0:T(8,128)(2,1)S(1)}, u32[]{:S(2)}, u32[]{:S(2)}) collective-permute-start(bf16[64,1536]{1,0:T(8,128)(2,1)S(1)} %get-tuple-element.42), channel_id=1, source_target_pairs={{0,128},{64,192},{128,0},{192,64},{1,129},{65,193},{129,1},{193,65... | collective-permute-start | bytes 589832 | tf_op jit(solution)/shard_map/ppermute | solution.py:31
  195.8 22.1 %all-to-all-start.5 = ((bf16[16,4,3456]{2,1,0:T(4,128)(2,1)}), bf16[16,4,3456]{2,1,0:T(4,128)(2,1)S(1)}, u32[]{:S(2)}, u32[]{:S(2)}) async-start(bf16[16,4,3456]{2,1,0:T(4,128)(2,1)} %reshape.46), calls=%async_computation.5 | async-start | bytes 884736 | tf_op jit(solution)/shard_map/all_to_all | solution.py:427
  (4 other events, 2.9 us)
Sparse Core Ops, SparseCore 0:
  30.1 66.0 all-gather.1

commit v3 on v2

v3 whole, which is shorter than its diff:
```python
import jax
import jax.numpy as jnp
from jax import lax
from jax.experimental import pallas as pl
from jax.experimental.pallas import tpu as pltpu
from jax.sharding import Mesh
from jax.sharding import PartitionSpec as P

F32 = jnp.float32
BF16 = jnp.bfloat16
ZAX = ("zh", "zl", "c")
EXP = ("zl", "c")
ALL = ("x", "zh", "zl", "c")
RING = 4
OFFS = (0, -1, 1, 2)
N_EXP = 8
CAP = 4
SLOTS = N_EXP * CAP
LANES = 128


def dot(a, b):
    return jnp.dot(a, b, preferred_element_type=F32)


def dot_t(a, b):
    return lax.dot_general(a, b, (((1,), (1,)), ((), ())), preferred_element_type=F32)


def shift(a, axis, n):
    return lax.ppermute(a, axis, [(i, (i + n) % RING) for i in range(RING)])


def sds(shape, dtype):
    return jax.ShapeDtypeStruct(shape, dtype)


VMEM = pl.BlockSpec(memory_space=pltpu.VMEM)
SMEM = pl.BlockSpec(memory_space=pltpu.SMEM)
HBM = pl.BlockSpec(memory_space=pltpu.HBM)


def kernel(body, outs, *args, specs, out_specs=None, scratch=(), limit=16):
    return pl.pallas_call(
        body,
        out_shape=outs,
        in_specs=list(specs),
        out_specs=out_specs or jax.tree.map(lambda _: VMEM, outs),
        scratch_shapes=list(scratch),
        compiler_params=pltpu.CompilerParams(vmem_limit_bytes=limit << 20),
    )(*args)


def spot(at, off):
    return (at + (off + RING)) % RING


def split_body(got, x_out, dy_out):
    width = x_out.shape[1]
    x_out[...] = got[:, :width]
    dy = got[:, width:]
    for i in range(RING):
        dy_out[i] = dy


def rows_body(own, left, right, far, top_out, bot_out, meta_out):
    n, width = own.shape
    for i, r in enumerate((own, left, right, far)):
        s = slice((i % 2) * n, (i % 2 + 1) * n)
        (top_out, bot_out)[i // 2][s] = r[:, : width - LANES]
        meta_out[i * n : (i + 1) * n] = r[:, width - LANES :]


def lanes_body(parts, top_out, bot_out):
    width = parts.shape[2]
    for i in range(RING):
        (top_out, bot_out)[i // 2][:, (i % 2) * width : (i % 2 + 1) * width] = parts[i]


def expert_body(
    at, x0t, x0b, x1t, x1b, x2t, x2b, x3t, x3b, d0t, d0b, d1t, d1b, d2t, d2b, d3t, d3b,
    meta, gate, up, down, router,
    m0, m1, m2, m3t, m3b, g0, g1, g2, g3t, g3b,
    gw_out, gates_out,
    rp, hb, ggb, gub, tlb, pb, mo, go, so,
):
    x_at, y_at, e_at = at[0], at[1], at[2]
    half, quarter = x0t.shape
    n = d0t.shape[0]
    n_rows = 2 * half

    def quarter_at(i):
        return pl.ds(pl.multiple_of(spot(y_at, OFFS[i]) * quarter, quarter), quarter)

    for k in range(RING):
        r0 = router[:, k * quarter : (k + 1) * quarter]
        r1 = r0 - r0.astype(BF16).astype(F32)
        r2 = r1 - r1.astype(BF16).astype(F32)
        rp[k] = jnp.concatenate([r0, r1, r2, jnp.zeros_like(r0)], 0).astype(BF16)

    pre_gate = pre_up = logits3 = raw = None
    for i in range(RING):
        pair = ((x0t, x0b), (x1t, x1b), (x2t, x2b), (x3t, x3b))[i]
        a = jnp.concatenate([pair[0][...], pair[1][...]], 0)
        q = quarter_at(i)
        g, u, l = dot(a, gate[q]), dot(a, up[q]), dot_t(a, rp[spot(y_at, OFFS[i])])
        pre_gate = g if i == 0 else pre_gate + g
        pre_up = u if i == 0 else pre_up + u
        logits3 = l if i == 0 else logits3 + l
    for k in range(RING):
        group = ((d0t, d1t, d2t, d3t), (d0b, d1b, d2b, d3b))[k // 2]
        s = slice((k % 2) * quarter, (k % 2 + 1) * quarter)
        a = jnp.concatenate([d[:, s] for d in group], 0)
        g = dot_t(a, down[:, k * quarter : (k + 1) * quarter])
        raw = g if k == 0 else raw + g

    lane = lax.broadcasted_iota(jnp.int32, logits3.shape, 1)
    expert = lane % N_EXP
    code = meta[:, :1].astype(F32).astype(jnp.int32)
    other = code // CAP
    hot_own = expert == e_at
    hot_other = expert == other
    score_own = jax.nn.sigmoid(jnp.sum(jnp.where(hot_own, logits3, 0.0), 1, keepdims=True))
    score_other = jax.nn.sigmoid(jnp.sum(jnp.where(hot_other, logits3, 0.0), 1, keepdims=True))
    total = score_own + score_other
    weight = score_own / total
    both = score_own * score_other / (total * total)
    c_own = both * (1.0 - score_own)
    c_other = both * (1.0 - score_other)
    gate_sig = jax.nn.sigmoid(pre_gate)
    gate_act = pre_gate * gate_sig
    hidden = gate_act * pre_up
    product = hidden * raw
    grad_weight = jnp.sum(product, 1, keepdims=True)
    hb[...] = (weight * hidden).astype(BF16)
    grad_hidden = weight * raw
    ggb[...] = (
        grad_hidden * pre_up * gate_sig * (1.0 + pre_gate * (1.0 - gate_sig))
    ).astype(BF16)
    gub[...] = (grad_hidden * gate_act).astype(BF16)
    to_logits = jnp.where(hot_own, grad_weight * c_own, 0.0) - jnp.where(
        hot_other, grad_weight * c_other, 0.0
    )
    high = to_logits.astype(BF16).astype(F32)
    tlb[...] = jnp.where(lane < 2 * N_EXP, high, to_logits - high).astype(BF16)
    wide = lax.broadcasted_iota(jnp.int32, gates_out.shape, 1)
    gates_out[...] = jnp.where(wide == 0, c_own, code.astype(F32))
    for i in range(RING):
        row = pl.ds(pl.multiple_of(spot(x_at, OFFS[i]) * n, n), n)
        pb[row, :] = product[i * n : (i + 1) * n]
    ones = jnp.ones((8, product.shape[1]), F32)
    sums = lax.dot_general(
        ones, pb[...], (((1,), (1,)), ((), ())),
        preferred_element_type=F32, precision=lax.Precision.HIGHEST,
    )
    for k in range(2):
        w = gw_out.shape[2]
        piece = sums[:1, k * w : (k + 1) * w]
        gw_out[:, k, :] = jnp.broadcast_to(piece, (gw_out.shape[0], w))

    outs = []

    def send(src, dst):
        c = pltpu.make_async_copy(src, dst, so.at[len(outs)])
        c.start()
        outs.append(c)

    for i in (3, 1, 2, 0):
        mo[i] = dot(hb[...], down[:, quarter_at(i)]).astype(BF16)
        if i == 3:
            send(mo.at[i, :half], m3t)
            send(mo.at[i, half:], m3b)
        else:
            send(mo.at[i], (m0, m1, m2)[i])
    for k in range(RING):
        s = slice(k * quarter, (k + 1) * quarter)
        r4 = jnp.concatenate([rp[k][: 2 * N_EXP], rp[k][: 2 * N_EXP]], 0)
        v = dot_t(ggb[...], gate[s]) + dot_t(gub[...], up[s]) + dot(tlb[...], r4)
        t = slice((k % 2) * quarter, (k % 2 + 1) * quarter)
        go[k // 2, :, t] = v.astype(BF16)
        if k % 2:
            send(go.at[k // 2, 3 * n : 4 * n], (g3t, g3b)[k // 2])
            two = slice((k - 1) * quarter, (k + 1) * quarter)
            for i in (1, 2, 0):
                send(go.at[k // 2, i * n : (i + 1) * n], (g0, g1, g2)[i].at[:, two])
    for c in outs:
        c.wait()


def exchange_body(gw_all, out):
    out[...] = jnp.broadcast_to(jnp.sum(gw_all[...], 0, keepdims=True), out.shape)


def column_body(at, gw, gates, top, bot, out):
    x_at, zh_at, e_at = at[0], at[3], at[2]
    n_rows = gates.shape[0]
    n = n_rows // RING
    n_half = top.shape[1] // 2
    row = jnp.concatenate(
        [lax.broadcasted_iota(jnp.int32, (n, n_rows), 0) + spot(x_at, o) * n for o in OFFS], 0
    )
    col = lax.broadcasted_iota(jnp.int32, (n_rows, n_rows), 1)
    code = gates[:, 1:2].astype(jnp.int32)
    mate = (row // CAP) * CAP + code % CAP

    def fetch(mask):
        return lax.dot_general(
            mask.astype(F32), gw[...], (((1,), (1,)), ((), ())),
            preferred_element_type=F32, precision=lax.Precision.HIGHEST,
        )

    lane = lax.broadcasted_iota(jnp.int32, (n_rows, N_EXP), 1)
    diff = jnp.where(lane == e_at, fetch(row == col), 0.0) - jnp.where(
        lane == code // CAP, fetch(mate == col), 0.0
    )
    gl = gates[:, :1] * jnp.sum(diff, 1, keepdims=True)
    feat = pl.ds(pl.multiple_of(zh_at * n_half, n_half), n_half)
    acc = None
    for i in range(RING):
        a = (top, bot)[i // 2][(i % 2) * n : (i % 2 + 1) * n, feat].astype(F32)
        s = jnp.sum(a * gl[i * n : (i + 1) * n], 0, keepdims=True)
        acc = s if i == 0 else acc + s
    q = n_half // 2
    high = acc.astype(BF16).astype(F32)
    low = acc - high
    four = jnp.concatenate([high[:, :q], high[:, q:], low[:, :q], low[:, q:]], 0)
    block = jnp.concatenate([four, four], 0)
    for k in range(out.shape[0] // 16):
        out[k * 16 : (k + 1) * 16] = jnp.concatenate([block, block], 0).astype(BF16)


def add(a, b):
    return (a.astype(F32) + b.astype(F32)).astype(BF16)


def add_rows_body(right, up, left, down, right_out, left_out):
    half = up.shape[0]
    right_out[:half] = add(right[:half], up[...])
    right_out[half:] = right[half:]
    left_out[:half] = left[:half]
    left_out[half:] = add(left[half:], down[...])


def add_lanes_body(right, up, left, down, right_out, left_out):
    half = up.shape[1]
    right_out[:, :half] = add(right[:, :half], up[...])
    right_out[:, half:] = right[:, half:]
    left_out[:, :half] = left[:, :half]
    left_out[:, half:] = add(left[:, half:], down[...])


def ring_reduce(body, own, left, right, far_a, far_b, axis):
    up = shift(far_a, axis, 1)
    down = shift(far_b, axis, -1)
    like = sds(right.shape, BF16)
    right, left = kernel(body, (like, like), right, up, left, down, specs=[VMEM] * 4)
    return own, shift(right, axis, 1), shift(left, axis, -1)


def sum_rows_body(a, b, c, o0, o1, o2, o3):
    n = o0.shape[0]
    for i, o in enumerate((o0, o1, o2, o3)):
        s = slice(i * n, (i + 1) * n)
        o[...] = (a[s].astype(F32) + b[s].astype(F32) + c[s].astype(F32)).astype(BF16)


def sum_lanes_body(a, b, c, out):
    width = out.shape[2]
    for i in range(RING):
        s = slice(i * width, (i + 1) * width)
        out[i] = (a[:, s].astype(F32) + b[:, s].astype(F32) + c[:, s].astype(F32)).astype(BF16)


def last_body(a0, a1, a2, a3, g, column, out):
    width = a0.shape[1]
    total = a0[...].astype(F32) + a1[...].astype(F32) + (a2[...].astype(F32) + a3[...].astype(F32))
    out[:, :width] = total.astype(BF16)
    total = g[0].astype(F32) + g[1].astype(F32) + (g[2].astype(F32) + g[3].astype(F32))
    out[:, width : 2 * width] = total.astype(BF16)
    out[:, 2 * width :] = column[...]


def combine_body(pick, got, moe_out, gt_out, gr_out):
    width = moe_out.shape[1]
    two = pick[...]
    moe_out[...] = dot(two, got[:, :width]).astype(BF16)
    gt_out[...] = dot(two, got[:, width : 2 * width]).astype(BF16)
    tail = got[:, 2 * width :]
    q = tail.shape[1]
    n_got = got.shape[0]
    e = lax.broadcasted_iota(jnp.int32, (N_EXP, n_got), 0)
    r = lax.broadcasted_iota(jnp.int32, (N_EXP, n_got), 1)
    for zh in range(2):
        for c in range(2):
            base = (zh * N_EXP + e) * CAP + c
            high, low = ((r == base + k).astype(F32).astype(BF16) for k in (0, 2))
            parts = dot(high, tail) + dot(low, tail)
            gr_out[:, (zh * 2 + c) * q : (zh * 2 + c + 1) * q] = parts


def on_device(tokens, routes, router, gate_proj, up_proj, down_proj, grad_out):
    rows, quarter = tokens.shape
    at = jnp.stack(
        [lax.axis_index("x"), lax.axis_index("y"), lax.axis_index(EXP), lax.axis_index("zh")]
    ).astype(jnp.int32)
    gate, up, down = gate_proj[0], up_proj[0], down_proj[0]
    n_ff = gate.shape[1]

    at, routes = lax.optimization_barrier((at, routes))

    flat = routes.reshape(-1)
    ids = jnp.arange(flat.shape[0], dtype=jnp.int32)
    same = (flat[:, None] == flat[None, :]) & (ids[None, :] < ids[:, None])
    slot = jnp.sum(same.astype(jnp.int32), axis=1)
    code = (flat * CAP + slot).reshape(rows, 2)
    lanes = jnp.arange(SLOTS, dtype=jnp.int32)
    hot = (code[:, :, None] == lanes[None, None, :]).astype(F32)
    pick_b = jnp.sum(hot, axis=1).astype(BF16)
    meta = jnp.sum(hot * code[:, ::-1, None].astype(F32), axis=(0, 1))

    def pack(a):
        return lax.dot_general(
            pick_b, a, (((0,), (0,)), ((), ())), preferred_element_type=F32
        ).astype(BF16)

    meta = jnp.broadcast_to(meta[:, None], (SLOTS, LANES)).astype(BF16)
    packed = jnp.concatenate([pack(tokens), meta, pack(grad_out)], 1).reshape(N_EXP, CAP, -1)
    got = lax.all_to_all(jnp.concatenate([packed, packed], 0), ZAX, 0, 0, tiled=True)
    got = got.reshape(2 * SLOTS, -1)
    n_own = got.shape[0]
    n_rows = RING * n_own
    half = n_rows // 2
    got_x, got_dy = kernel(
        split_body,
        (sds((n_own, quarter + LANES), BF16), sds((RING, n_own, quarter), BF16)),
        got, specs=[VMEM],
    )

    got_dy = lax.all_to_all(got_dy, "y", 0, 0, tiled=True)
    pieces = [got_x] + [shift(got_x, "x", n) for n in (1, -1, 2)]
    part = sds((half, quarter), BF16)
    top, bot, meta_all = kernel(
        rows_body, (part, part, sds((n_rows, LANES), BF16)), *pieces, specs=[VMEM] * 4
    )
    g_part = sds((n_own, 2 * quarter), BF16)
    d_top, d_bot = kernel(lanes_body, (g_part, g_part), got_dy, specs=[VMEM])

    def ring_gather(a, b, axis):
        left_a = shift(a, axis, 1)
        right_b = shift(b, axis, -1)
        left_b = shift(b, axis, 1)
        right_a = shift(a, axis, -1)
        return a, b, left_a, left_b, right_a, right_b, shift(left_a, axis, 1), shift(right_b, axis, -1)

    full_x = ring_gather(top, bot, "y")
    full_dy = ring_gather(d_top, d_bot, "x")

    sem = pltpu.SemaphoreType.DMA
    n_shards = 2 * RING * RING
    near = sds((n_rows, quarter), BF16)
    g_near = sds((n_own, RING * quarter), BF16)
    *parts, gw, gates = kernel(
        expert_body,
        (near,) * 3 + (part,) * 2 + (g_near,) * 3 + (g_part,) * 2
        + (sds((n_shards, 2, n_rows // 2), F32), sds((n_rows, LANES), F32)),
        at, *full_x, *full_dy, meta_all, gate, up, down, router.T,
        specs=[SMEM] + [VMEM] * 21,
        out_specs=(HBM,) * 10 + (VMEM, VMEM),
        scratch=[
            pltpu.VMEM((RING, 4 * N_EXP, quarter), BF16),
            pltpu.VMEM((n_rows, n_ff), BF16), pltpu.VMEM((n_rows, n_ff), BF16),
            pltpu.VMEM((n_rows, n_ff), BF16), pltpu.VMEM((n_rows, 4 * N_EXP), BF16),
            pltpu.VMEM((n_rows, n_ff), F32),
            pltpu.VMEM((RING, n_rows, quarter), BF16), pltpu.VMEM((2, n_rows, 2 * quarter), BF16),
            sem((13,)),
        ],
        limit=26,
    )

    out_terms = ring_reduce(add_rows_body, *parts[:5], "y")
    grad_terms = ring_reduce(add_lanes_body, *parts[5:], "x")

    grad_y = kernel(
        sum_lanes_body, sds((RING, n_own, quarter), BF16), *grad_terms, specs=[VMEM] * 3
    )

    gw_all = lax.all_to_all(gw, ("x", "zh", "y"), 0, 0, tiled=True)
    gw_exp = lax.all_to_all(
        kernel(exchange_body, sds((N_EXP, 2, n_rows // 2), F32), gw_all, specs=[VMEM]),
        EXP, 0, 0, tiled=True,
    ).reshape(N_EXP, n_rows)
    column = kernel(
        column_body, sds((n_own, quarter // 4), BF16), at, gw_exp, gates, top, bot,
        specs=[SMEM] + [VMEM] * 4,
    )

    piece = sds((n_own, quarter), BF16)
    out_x = kernel(sum_rows_body, (piece,) * RING, *out_terms, specs=[VMEM] * 3)
    grad_got = lax.all_to_all(grad_y, "y", 0, 0, tiled=True)
    out_got = [out_x[0]] + [shift(out_x[i], "x", OFFS[i]) for i in (1, 2, 3)]
    final = kernel(
        last_body, sds((n_own, 2 * quarter + quarter // 4), BF16), *out_got, grad_got, column,
        specs=[VMEM] * 6,
    )
    final = lax.all_to_all(final.reshape(2 * N_EXP, CAP, -1), ZAX, 0, 0, tiled=True)
    res = sds((rows, quarter), BF16)
    moe_out, grad_tokens, grad_router = kernel(
        combine_body, (res, res, sds((N_EXP, quarter), F32)),
        jnp.concatenate([pick_b, pick_b], 1), final.reshape(2 * SLOTS, -1), specs=[VMEM] * 2,
    )
    return (moe_out, grad_tokens, grad_router.T)


def solution(mesh):
    fine = Mesh(mesh.devices.reshape(4, 2, 4, 2, 4), ("x", "zh", "zl", "c", "y"))
    return jax.shard_map(
        on_device,
        mesh=fine,
        in_specs=(
            P(ALL, "y"),
            P(ALL, None),
            P(),
            P(EXP, None, ("x", "zh", "y")),
            P(EXP, None, ("x", "zh", "y")),
            P(EXP, ("x", "zh", "y"), None),
            P(ALL, "y"),
        ),
        out_specs=(P(ALL, "y"), P(ALL, "y"), P("y", None)),
        check_vma=False,
    )
```

time: 227 us -> 193 us (0.85)
  waiting for transfers between devices: 70.8 us -> 57 us
  Pallas kernels: 34.7 us -> 21 us
  between operations: 14.2 us -> 0.82 us
  starting transfers between devices: 43.8 us -> 57.1 us
  blocking collectives: 48.8 us -> 41.1 us
    ppermute x20 -> x26, waiting for transfers between devices: 53.9 us -> 37.8 us  [shift(): return lax.ppermute(a, axis, [(i, (i + n) % RING) for i in range(RING)])]
    pallas_call x4 -> x0, Pallas kernels: 12.8 us -> none  [the longest x2 6.72 us: ring_reduce(): pl.pallas_call(add_body, grid=(steps,), out_shape=(like, like), in_specs=...]
    ppermute x20 -> x26, starting transfers between devices: 25.3 us -> 35.8 us  [shift(): return lax.ppermute(a, axis, [(i, (i + n) % RING) for i in range(RING)])]
    all_to_all x3 -> x2, blocking collectives: 48.8 us -> 41.1 us  [the longest x1 24.7 us: on_device(): lax.all_to_all(jnp.concatenate([packed, packed], 0), ZAX, 0, 0, tiled=True)]
    all_to_all x1 -> x2, starting transfers between devices: 3.49 us -> 7.68 us  [the longest x1 4.18 us: on_device(): got_dy = lax.all_to_all(got_dy, 'y', 0, 0, tiled=True)]
    unnamed x26 -> x23, local copies, waits for them, and re-layouts: 9.26 us -> 10.6 us
    pallas_call x6 -> x12, Pallas kernels: 21.9 us -> 21 us  [kernel(): pl.pallas_call(body, out_shape=outs, in_specs=list(specs), out_specs=out_...]
  transfers between devices with their start and end apart: 24 -> 30, of which waited for: 13 -> 16; matrix products, arithmetic and copies ran while one was open for 1% -> 0% of each run, Pallas kernels for 7% -> 5%
where the time goes in v3:
time: 193 us; the launch traced here: 192 us
  starting transfers between devices  57.1 us (30%)
  waiting for transfers between devices  57 us (30%)
  blocking collectives  41.1 us (21%)
  Pallas kernels  21 us (11%)
  local copies, waits for them, and re-layouts  13 us (7%)
    ppermute x26, waiting for transfers between devices, shift(): return lax.ppermute(a, axis, [(i, (i + n) % RING) for i in range(RING)])  37.8 us
    ppermute x26, starting transfers between devices, shift(): return lax.ppermute(a, axis, [(i, (i + n) % RING) for i in range(RING)])  35.8 us
    all_to_all x1, blocking collectives, on_device(): lax.all_to_all(jnp.concatenate([packed, packed], 0), ZAX, 0, 0, tiled=True)  24.7 us
    pallas_call x12, Pallas kernels, kernel(): pl.pallas_call(body, out_shape=outs, in_specs=list(specs), out_specs=out_...  21 us
    all_to_all x1, blocking collectives, on_device(): gw_all = lax.all_to_all(gw, ('x', 'zh', 'y'), 0, 0, tiled=True)  16.4 us
    all_to_all x1, waiting for transfers between devices, on_device(): lax.all_to_all(final.reshape(2 * N_EXP, CAP, -1), ZAX, 0, 0, tiled=True)  15.6 us
    unnamed x23, local copies, waits for them, and re-layouts  10.6 us
    all_to_all x1, starting transfers between devices, on_device(): lax.all_to_all(kernel(exchange_body, sds((N_EXP, 2, n_rows // 2), F32), g...  7.03 us
  transfers between devices with their start and end apart: 30, of which 16 were waited for; matrix products, arithmetic and copies ran while one was open for 0% of the time, Pallas kernels for 5%

profile of v3, /device:TPU:1, one launch (start us, length us, event | category | flops | bytes accessed | tf_op | source)
XLA Modules:
  0.0 191.8 jit_solution(12042943711734829183)
XLA Ops:
  3.8 24.7 %all_to_all.30 = bf16[16,4,3200]{2,1,0:T(4,128)(2,1)S(1)} all-to-all(bf16[16,4,3200]{2,1,0:T(4,128)(2,1)S(1)} %pad_maximum_fusion), channel_id=1, replica_groups=mesh['x'=4,'zh'=2,'zl'=4,'c'=2,'y'=4] {'zh','zl','c'}, dimensions={0} | all-to-all | bytes 819200 | tf_op jit(solution)/shard_map/all_to_all | solution.py:328
  29.5 2.7 %collective-permute-start.2 = (bf16[64,1664]{1,0:T(8,128)(2,1)S(1)}, bf16[64,1664]{1,0:T(8,128)(2,1)S(1)}, u32[]{:S(2)}, u32[]{:S(2)}) collective-permute-start(bf16[64,1664]{1,0:T(8,128)(2,1)S(1)} %get-tuple-element.37.own), channel_id=1, source_target_pairs={{0,128},{64,192},{128,0},{192,64},{1,129},{65,193},{129,1},{193,65... | collective-permute-start | bytes 638984 | tf_op jit(solution)/shard_map/ppermute | solution.py:31
  33.8 4.2 %all-to-all-start.1 = ((bf16[4,64,1536]{2,1,0:T(8,128)(2,1)}), bf16[4,64,1536]{2,1,0:T(8,128)(2,1)S(1)}, u32[]{:S(2)}, u32[]{:S(2)}) async-start(bf16[4,64,1536]{2,1,0:T(8,128)(2,1)} %get-tuple-element.40), calls=%async_computation.1 | async-start | bytes 1572864 | tf_op jit(solution)/shard_map/all_to_all | solution.py:339
  37.9 4.7 %collective-permute-done.1.right = bf16[64,1664]{1,0:T(8,128)(2,1)S(1)} collective-permute-done((bf16[64,1664]{1,0:T(8,128)(2,1)S(1)}, bf16[64,1664]{1,0:T(8,128)(2,1)S(1)}, u32[]{:S(2)}, u32[]{:S(2)}) %collective-permute-start.1) | collective-permute-done | bytes 213024 | tf_op jit(solution)/shard_map/ppermute | solution.py:31
  43.3 2.7 %collective-permute-start.5 = (bf16[128,1536]{1,0:T(8,128)(2,1)S(1)}, bf16[128,1536]{1,0:T(8,128)(2,1)S(1)}, u32[]{:S(2)}, u32[]{:S(2)}) collective-permute-start(bf16[128,1536]{1,0:T(8,128)(2,1)S(1)} %get-tuple-element.38.x0t.top), channel_id=1, source_target_pairs={{0,3},{1,0},{2,1},{3,2},{4,7},{5,4},{6,5},{7,6},{8,11},{9,8},{10,9... | collective-permute-start | bytes 1179656 | tf_op jit(solution)/shard_map/ppermute | solution.py:31
  46.1 2.7 %collective-permute-start.6 = (bf16[128,1536]{1,0:T(8,128)(2,1)S(1)}, bf16[128,1536]{1,0:T(8,128)(2,1)S(1)}, u32[]{:S(2)}, u32[]{:S(2)}) collective-permute-start(bf16[128,1536]{1,0:T(8,128)(2,1)S(1)} %get-tuple-element.39.x0b.bot), channel_id=1, source_target_pairs={{0,3},{1,0},{2,1},{3,2},{4,7},{5,4},{6,5},{7,6},{8,11},{9,8},{10,9... | collective-permute-start | bytes 1179656 | tf_op jit(solution)/shard_map/ppermute | solution.py:31
  50.1 2.1 %collective-permute-start.11 = (bf16[64,3072]{1,0:T(8,128)(2,1)S(1)}, bf16[64,3072]{1,0:T(8,128)(2,1)S(1)}, u32[]{:S(2)}, u32[]{:S(2)}) collective-permute-start(bf16[64,3072]{1,0:T(8,128)(2,1)S(1)} %get-tuple-element.41.d0t), channel_id=1, source_target_pairs={{0,192},{64,0},{128,64},{192,128},{1,193},{65,1},{129,65},{193,129... | collective-permute-start | bytes 1179656 | tf_op jit(solution)/shard_map/ppermute | solution.py:31
  52.3 4.7 %collective-permute-done.5.x2t = bf16[128,1536]{1,0:T(8,128)(2,1)S(1)} collective-permute-done((bf16[128,1536]{1,0:T(8,128)(2,1)S(1)}, bf16[128,1536]{1,0:T(8,128)(2,1)S(1)}, u32[]{:S(2)}, u32[]{:S(2)}) %collective-permute-start.5) | collective-permute-done | bytes 393248 | tf_op jit(solution)/shard_map/ppermute | solution.py:31
  58.8 2.1 %collective-permute-start.12 = (bf16[64,3072]{1,0:T(8,128)(2,1)S(1)}, bf16[64,3072]{1,0:T(8,128)(2,1)S(1)}, u32[]{:S(2)}, u32[]{:S(2)}) collective-permute-start(bf16[64,3072]{1,0:T(8,128)(2,1)S(1)} %get-tuple-element.42.d0b), channel_id=1, source_target_pairs={{0,192},{64,0},{128,64},{192,128},{1,193},{65,1},{129,65},{193,129... | collective-permute-start | bytes 1179656 | tf_op jit(solution)/shard_map/ppermute | solution.py:31
  60.8 4.6 %collective-permute-done.6.x2b = bf16[128,1536]{1,0:T(8,128)(2,1)S(1)} collective-permute-done((bf16[128,1536]{1,0:T(8,128)(2,1)S(1)}, bf16[128,1536]{1,0:T(8,128)(2,1)S(1)}, u32[]{:S(2)}, u32[]{:S(2)}) %collective-permute-start.6) | collective-permute-done | bytes 393248 | tf_op jit(solution)/shard_map/ppermute | solution.py:31
  71.8 2.2 %collective-permute-start.14 = (bf16[64,3072]{1,0:T(8,128)(2,1)S(1)}, bf16[64,3072]{1,0:T(8,128)(2,1)S(1)}, u32[]{:S(2)}, u32[]{:S(2)}) collective-permute-start(bf16[64,3072]{1,0:T(8,128)(2,1)S(1)} %collective-permute-done.12.d2b), channel_id=1, source_target_pairs={{0,192},{64,0},{128,64},{192,128},{1,193},{65,1},{129,65},{193,129... | collective-permute-start | bytes 1179656 | tf_op jit(solution)/shard_map/ppermute | solution.py:31
  74.1 2.1 %collective-permute-done.10.d1b = bf16[64,3072]{1,0:T(8,128)(2,1)S(1)} collective-permute-done((bf16[64,3072]{1,0:T(8,128)(2,1)S(1)}, bf16[64,3072]{1,0:T(8,128)(2,1)S(1)}, u32[]{:S(2)}, u32[]{:S(2)}) %collective-permute-start.10) | collective-permute-done | bytes 393248 | tf_op jit(solution)/shard_map/ppermute | solution.py:31
  76.1 2.8 %collective-permute-done.7.x3t = bf16[128,1536]{1,0:T(8,128)(2,1)S(1)} collective-permute-done((bf16[128,1536]{1,0:T(8,128)(2,1)S(1)}, bf16[128,1536]{1,0:T(8,128)(2,1)S(1)}, u32[]{:S(2)}, u32[]{:S(2)}) %collective-permute-start.7) | collective-permute-done | bytes 393248 | tf_op jit(solution)/shard_map/ppermute | solution.py:31
  78.9 5.6 %collective-permute-done.13.d3t = bf16[64,3072]{1,0:T(8,128)(2,1)S(1)} collective-permute-done((bf16[64,3072]{1,0:T(8,128)(2,1)S(1)}, bf16[64,3072]{1,0:T(8,128)(2,1)S(1)}, u32[]{:S(2)}, u32[]{:S(2)}) %collective-permute-start.13) | collective-permute-done | bytes 393248 | tf_op jit(solution)/shard_map/ppermute | solution.py:31
  84.6 1.9 copy-done.1
  86.4 1.9 copy-done.2
  88.3 1.9 copy-done.3
  93.1 10.1 %shard_map.97 = (bf16[256,1536]{1,0:T(8,128)(2,1)S(1)}, bf16[256,1536]{1,0:T(8,128)(2,1)S(1)}, bf16[256,1536]{1,0:T(8,128)(2,1)S(1)}, bf16[128,1536]{1,0:T(8,128...) custom-call(s32[4]{0:T(128)S(1)} %pad_add_fusion.at, ...), custom_call_target="tpu_custom_call" | custom-call | tf_op jit(solution)/shard_map/pallas_call | solution.py:44
  103.2 2.7 %collective-permute-start.23 = (bf16[64,3072]{1,0:T(8,128)(2,1)S(1)}, bf16[64,3072]{1,0:T(8,128)(2,1)S(1)}, u32[]{:S(2)}, u32[]{:S(2)}) collective-permute-start(bf16[64,3072]{1,0:T(8,128)(2,1)S(1)} %get-tuple-element.59), channel_id=1, source_target_pairs={{0,192},{64,0},{128,64},{192,128},{1,193},{65,1},{129,65},{193,129... | collective-permute-start | bytes 1179656 | tf_op jit(solution)/shard_map/ppermute | solution.py:31
  105.9 2.8 %collective-permute-start.15 = (bf16[128,1536]{1,0:T(8,128)(2,1)S(1)}, bf16[128,1536]{1,0:T(8,128)(2,1)S(1)}, u32[]{:S(2)}, u32[]{:S(2)}) collective-permute-start(bf16[128,1536]{1,0:T(8,128)(2,1)S(1)} %get-tuple-element.46), channel_id=1, source_target_pairs={{0,1},{1,2},{2,3},{3,0},{4,5},{5,6},{6,7},{7,4},{8,9},{9,10},{10,1... | collective-permute-start | bytes 1179656 | tf_op jit(solution)/shard_map/ppermute | solution.py:31
  109.7 3.3 %collective-permute-done.22.up = bf16[64,3072]{1,0:T(8,128)(2,1)S(1)} collective-permute-done((bf16[64,3072]{1,0:T(8,128)(2,1)S(1)}, bf16[64,3072]{1,0:T(8,128)(2,1)S(1)}, u32[]{:S(2)}, u32[]{:S(2)}) %collective-permute-start.22) | collective-permute-done | bytes 393248 | tf_op jit(solution)/shard_map/ppermute | solution.py:31
  114.3 2.7 %collective-permute-start.25 = (bf16[64,6144]{1,0:T(8,128)(2,1)}, bf16[64,6144]{1,0:T(8,128)(2,1)}, u32[]{:S(2)}, u32[]{:S(2)}) collective-permute-start(bf16[64,6144]{1,0:T(8,128)(2,1)} %get-tuple-element.61), channel_id=1, source_target_pairs={{0,192},{64,0},{128,64},{192,128},{1,193},{65,1},{129,65},{193,129... | collective-permute-start | bytes 2359304 | tf_op jit(solution)/shard_map/ppermute | solution.py:31
  118.6 3.1 %collective-permute-start.17 = (bf16[256,1536]{1,0:T(8,128)(2,1)}, bf16[256,1536]{1,0:T(8,128)(2,1)S(1)}, u32[]{:S(2)}, u32[]{:S(2)}) collective-permute-start(bf16[256,1536]{1,0:T(8,128)(2,1)} %get-tuple-element.49), channel_id=1, source_target_pairs={{0,1},{1,2},{2,3},{3,0},{4,5},{5,6},{6,7},{7,4},{8,9},{9,10},{10,1... | collective-permute-start | bytes 2359304 | tf_op jit(solution)/shard_map/ppermute | solution.py:31
  122.8 16.4 %all_to_all.31.gw_all = f32[32,2,128]{2,1,0:T(2,128)S(1)} all-to-all(f32[32,2,128]{2,1,0:T(2,128)S(1)} %get-tuple-element.62), channel_id=1, replica_groups=mesh['x'=4,'zh'=2,'zl'=4,'c'=2,'y'=4] {'x','zh','y'}, dimensions={0} | all-to-all | bytes 65536 | tf_op jit(solution)/shard_map/all_to_all | solution.py:387
  139.9 7.0 %all-to-all-start.4 = ((f32[8,2,128]{2,1,0:T(2,128)}), f32[8,2,128]{2,1,0:T(2,128)S(1)}, u32[]{:S(2)}, u32[]{:S(2)}) async-start(f32[8,2,128]{2,1,0:T(2,128)} %shard_map.102), calls=%async_computation.4 | async-start | bytes 16384 | tf_op jit(solution)/shard_map/all_to_all | solution.py:388
  146.9 2.5 %shard_map.101 = bf16[4,64,1536]{2,1,0:T(8,128)(2,1)} custom-call(bf16[64,6144]{1,0:T(8,128)(2,1)S(1)} %get-tuple-element.55.a, bf16[64,6144]{1,0:T(8,128)(2,1)} %collective-permute-done.24.b, bf16[64,6144]{1,0:T(8,128)(2,1)} %collective-permute-done.25.c), custom_call_target="tpu_custom_call" | custom-call | tf_op jit(solution)/shard_map/pallas_call | solution.py:44
  149.5 2.4 %all-to-all-done.4 = f32[8,2,128]{2,1,0:T(2,128)S(1)} async-done(((f32[8,2,128]{2,1,0:T(2,128)}), f32[8,2,128]{2,1,0:T(2,128)S(1)}, u32[]{:S(2)}, u32[]{:S(2)}) %all-to-all-start.4) | async-done | bytes 8224 | tf_op jit(solution)/shard_map/all_to_all | solution.py:388
  151.9 3.5 %all-to-all-start.2 = ((bf16[4,64,1536]{2,1,0:T(8,128)(2,1)}), bf16[4,64,1536]{2,1,0:T(8,128)(2,1)S(1)}, u32[]{:S(2)}, u32[]{:S(2)}) async-start(bf16[4,64,1536]{2,1,0:T(8,128)(2,1)} %shard_map.101), calls=%async_computation.2 | async-start | bytes 1572864 | tf_op jit(solution)/shard_map/all_to_all | solution.py:399
  160.9 1.7 collective-permute-done.19.a1
  162.6 3.4 %collective-permute-done.20.a2 = bf16[64,1536]{1,0:T(8,128)(2,1)S(1)} collective-permute-done((bf16[64,1536]{1,0:T(8,128)(2,1)S(1)}, bf16[64,1536]{1,0:T(8,128)(2,1)S(1)}, u32[]{:S(2)}, u32[]{:S(2)}) %collective-permute-start.20) | collective-permute-done | bytes 196640 | tf_op jit(solution)/shard_map/ppermute | solution.py:31
  168.7 6.5 %all-to-all-start.5 = ((bf16[16,4,3456]{2,1,0:T(4,128)(2,1)}), bf16[16,4,3456]{2,1,0:T(4,128)(2,1)S(1)}, u32[]{:S(2)}, u32[]{:S(2)}) async-start(bf16[16,4,3456]{2,1,0:T(4,128)(2,1)} %reshape.38), calls=%async_computation.5 | async-start | bytes 884736 | tf_op jit(solution)/shard_map/all_to_all | solution.py:405
  175.3 15.6 %all-to-all-done.5 = bf16[16,4,3456]{2,1,0:T(4,128)(2,1)S(1)} async-done(((bf16[16,4,3456]{2,1,0:T(4,128)(2,1)}), bf16[16,4,3456]{2,1,0:T(4,128)(2,1)S(1)}, u32[]{:S(2)}, u32[]{:S(2)}) %all-to-all-start.5) | async-done | bytes 442400 | tf_op jit(solution)/shard_map/all_to_all | solution.py:405
  (86 shorter events, 33.7 us)
Async XLA Ops:
  3.5 81.1 %copy-start.8 = (f32[6144,8]{0,1:T(8,128)S(1)}, f32[6144,8]{0,1:T(8,128)}, u32[]{:S(2)}) copy-start(f32[6144,8]{0,1:T(8,128)} %param.9) | copy-start | bytes 589828
  29.5 8.4 %collective-permute-start.2 = (bf16[64,1664]{1,0:T(8,128)(2,1)S(1)}, bf16[64,1664]{1,0:T(8,128)(2,1)S(1)}, u32[]{:S(2)}, u32[]{:S(2)}) collective-permute-start(bf16[64,1664]{1,0:T(8,128)(2,1)S(1)} %get-tuple-element.37.own), channel_id=1, source_target_pairs={{0,128},{64,192},{128,0},{192,64},{1,129},{65,193},{129,1},{193,65... | collective-permute-start | bytes 638984 | tf_op jit(solution)/shard_map/ppermute | solution.py:31
  32.3 10.4 %collective-permute-start.1 = (bf16[64,1664]{1,0:T(8,128)(2,1)S(1)}, bf16[64,1664]{1,0:T(8,128)(2,1)S(1)}, u32[]{:S(2)}, u32[]{:S(2)}) collective-permute-start(bf16[64,1664]{1,0:T(8,128)(2,1)S(1)} %get-tuple-element.37.own), channel_id=1, source_target_pairs={{0,192},{64,0},{128,64},{192,128},{1,193},{65,1},{129,65},{193,129... | collective-permute-start | bytes 638984 | tf_op jit(solution)/shard_map/ppermute | solution.py:31
  33.2 9.5 %collective-permute-start = (bf16[64,1664]{1,0:T(8,128)(2,1)S(1)}, bf16[64,1664]{1,0:T(8,128)(2,1)S(1)}, u32[]{:S(2)}, u32[]{:S(2)}) collective-permute-start(bf16[64,1664]{1,0:T(8,128)(2,1)S(1)} %get-tuple-element.37.own), channel_id=1, source_target_pairs={{0,64},{64,128},{128,192},{192,0},{1,65},{65,129},{129,193},{193,1... | collective-permute-start | bytes 638984 | tf_op jit(solution)/shard_map/ppermute | solution.py:31
  33.8 16.3 %all-to-all-start.1 = ((bf16[4,64,1536]{2,1,0:T(8,128)(2,1)}), bf16[4,64,1536]{2,1,0:T(8,128)(2,1)S(1)}, u32[]{:S(2)}, u32[]{:S(2)}) async-start(bf16[4,64,1536]{2,1,0:T(8,128)(2,1)} %get-tuple-element.40), calls=%async_computation.1 | async-start | bytes 1572864 | tf_op jit(solution)/shard_map/all_to_all | solution.py:339
  43.3 13.6 %collective-permute-start.5 = (bf16[128,1536]{1,0:T(8,128)(2,1)S(1)}, bf16[128,1536]{1,0:T(8,128)(2,1)S(1)}, u32[]{:S(2)}, u32[]{:S(2)}) collective-permute-start(bf16[128,1536]{1,0:T(8,128)(2,1)S(1)} %get-tuple-element.38.x0t.top), channel_id=1, source_target_pairs={{0,3},{1,0},{2,1},{3,2},{4,7},{5,4},{6,5},{7,6},{8,11},{9,8},{10,9... | collective-permute-start | bytes 1179656 | tf_op jit(solution)/shard_map/ppermute | solution.py:31
  46.1 12.7 %collective-permute-start.3 = (bf16[128,1536]{1,0:T(8,128)(2,1)S(1)}, bf16[128,1536]{1,0:T(8,128)(2,1)S(1)}, u32[]{:S(2)}, u32[]{:S(2)}) collective-permute-start(bf16[128,1536]{1,0:T(8,128)(2,1)S(1)} %get-tuple-element.38.x0t.top), channel_id=1, source_target_pairs={{0,1},{1,2},{2,3},{3,0},{4,5},{5,6},{6,7},{7,4},{8,9},{9,10},{10,1... | collective-permute-start | bytes 1179656 | tf_op jit(solution)/shard_map/ppermute | solution.py:31
  46.1 19.3 %collective-permute-start.6 = (bf16[128,1536]{1,0:T(8,128)(2,1)S(1)}, bf16[128,1536]{1,0:T(8,128)(2,1)S(1)}, u32[]{:S(2)}, u32[]{:S(2)}) collective-permute-start(bf16[128,1536]{1,0:T(8,128)(2,1)S(1)} %get-tuple-element.39.x0b.bot), channel_id=1, source_target_pairs={{0,3},{1,0},{2,1},{3,2},{4,7},{5,4},{6,5},{7,6},{8,11},{9,8},{10,9... | collective-permute-start | bytes 1179656 | tf_op jit(solution)/shard_map/ppermute | solution.py:31
  48.8 18.4 %collective-permute-start.4 = (bf16[128,1536]{1,0:T(8,128)(2,1)S(1)}, bf16[128,1536]{1,0:T(8,128)(2,1)S(1)}, u32[]{:S(2)}, u32[]{:S(2)}) collective-permute-start(bf16[128,1536]{1,0:T(8,128)(2,1)S(1)} %get-tuple-element.39.x0b.bot), channel_id=1, source_target_pairs={{0,1},{1,2},{2,3},{3,0},{4,5},{5,6},{6,7},{7,4},{8,9},{9,10},{10,1... | collective-permute-start | bytes 1179656 | tf_op jit(solution)/shard_map/ppermute | solution.py:31
  50.1 18.8 %collective-permute-start.11 = (bf16[64,3072]{1,0:T(8,128)(2,1)S(1)}, bf16[64,3072]{1,0:T(8,128)(2,1)S(1)}, u32[]{:S(2)}, u32[]{:S(2)}) collective-permute-start(bf16[64,3072]{1,0:T(8,128)(2,1)S(1)} %get-tuple-element.41.d0t), channel_id=1, source_target_pairs={{0,192},{64,0},{128,64},{192,128},{1,193},{65,1},{129,65},{193,129... | collective-permute-start | bytes 1179656 | tf_op jit(solution)/shard_map/ppermute | solution.py:31
  57.0 14.4 %collective-permute-start.9 = (bf16[64,3072]{1,0:T(8,128)(2,1)S(1)}, bf16[64,3072]{1,0:T(8,128)(2,1)S(1)}, u32[]{:S(2)}, u32[]{:S(2)}) collective-permute-start(bf16[64,3072]{1,0:T(8,128)(2,1)S(1)} %get-tuple-element.41.d0t), channel_id=1, source_target_pairs={{0,64},{64,128},{128,192},{192,0},{1,65},{65,129},{129,193},{193,1... | collective-permute-start | bytes 1179656 | tf_op jit(solution)/shard_map/ppermute | solution.py:31
  58.8 13.1 %collective-permute-start.12 = (bf16[64,3072]{1,0:T(8,128)(2,1)S(1)}, bf16[64,3072]{1,0:T(8,128)(2,1)S(1)}, u32[]{:S(2)}, u32[]{:S(2)}) collective-permute-start(bf16[64,3072]{1,0:T(8,128)(2,1)S(1)} %get-tuple-element.42.d0b), channel_id=1, source_target_pairs={{0,192},{64,0},{128,64},{192,128},{1,193},{65,1},{129,65},{193,129... | collective-permute-start | bytes 1179656 | tf_op jit(solution)/shard_map/ppermute | solution.py:31
  65.4 10.7 %collective-permute-start.10 = (bf16[64,3072]{1,0:T(8,128)(2,1)S(1)}, bf16[64,3072]{1,0:T(8,128)(2,1)S(1)}, u32[]{:S(2)}, u32[]{:S(2)}) collective-permute-start(bf16[64,3072]{1,0:T(8,128)(2,1)S(1)} %get-tuple-element.42.d0b), channel_id=1, source_target_pairs={{0,64},{64,128},{128,192},{192,0},{1,65},{65,129},{129,193},{193,1... | collective-permute-start | bytes 1179656 | tf_op jit(solution)/shard_map/ppermute | solution.py:31
  67.9 11.0 %collective-permute-start.7 = (bf16[128,1536]{1,0:T(8,128)(2,1)S(1)}, bf16[128,1536]{1,0:T(8,128)(2,1)S(1)}, u32[]{:S(2)}, u32[]{:S(2)}) collective-permute-start(bf16[128,1536]{1,0:T(8,128)(2,1)S(1)} %collective-permute-done.3.x1t), channel_id=1, source_target_pairs={{0,1},{1,2},{2,3},{3,0},{4,5},{5,6},{6,7},{7,4},{8,9},{9,10},{10,1... | collective-permute-start | bytes 1179656 | tf_op jit(solution)/shard_map/ppermute | solution.py:31
  68.9 10.0 %collective-permute-start.8 = (bf16[128,1536]{1,0:T(8,128)(2,1)S(1)}, bf16[128,1536]{1,0:T(8,128)(2,1)S(1)}, u32[]{:S(2)}, u32[]{:S(2)}) collective-permute-start(bf16[128,1536]{1,0:T(8,128)(2,1)S(1)} %collective-permute-done.6.x2b), channel_id=1, source_target_pairs={{0,3},{1,0},{2,1},{3,2},{4,7},{5,4},{6,5},{7,6},{8,11},{9,8},{10,9... | collective-permute-start | bytes 1179656 | tf_op jit(solution)/shard_map/ppermute | solution.py:31
  71.4 13.2 %collective-permute-start.13 = (bf16[64,3072]{1,0:T(8,128)(2,1)S(1)}, bf16[64,3072]{1,0:T(8,128)(2,1)S(1)}, u32[]{:S(2)}, u32[]{:S(2)}) collective-permute-start(bf16[64,3072]{1,0:T(8,128)(2,1)S(1)} %collective-permute-done.9.d1t), channel_id=1, source_target_pairs={{0,64},{64,128},{128,192},{192,0},{1,65},{65,129},{129,193},{193,1... | collective-permute-start | bytes 1179656 | tf_op jit(solution)/shard_map/ppermute | solution.py:31
  71.8 12.7 %collective-permute-start.14 = (bf16[64,3072]{1,0:T(8,128)(2,1)S(1)}, bf16[64,3072]{1,0:T(8,128)(2,1)S(1)}, u32[]{:S(2)}, u32[]{:S(2)}) collective-permute-start(bf16[64,3072]{1,0:T(8,128)(2,1)S(1)} %collective-permute-done.12.d2b), channel_id=1, source_target_pairs={{0,192},{64,0},{128,64},{192,128},{1,193},{65,1},{129,65},{193,129... | collective-permute-start | bytes 1179656 | tf_op jit(solution)/shard_map/ppermute | solution.py:31
  84.5 1.9 copy-start.1
  103.1 9.9 %collective-permute-start.22 = (bf16[64,3072]{1,0:T(8,128)(2,1)S(1)}, bf16[64,3072]{1,0:T(8,128)(2,1)S(1)}, u32[]{:S(2)}, u32[]{:S(2)}) collective-permute-start(bf16[64,3072]{1,0:T(8,128)(2,1)S(1)} %get-tuple-element.57), channel_id=1, source_target_pairs={{0,64},{64,128},{128,192},{192,0},{1,65},{65,129},{129,193},{193,1... | collective-permute-start | bytes 1179656 | tf_op jit(solution)/shard_map/ppermute | solution.py:31
  103.2 9.8 %collective-permute-start.23 = (bf16[64,3072]{1,0:T(8,128)(2,1)S(1)}, bf16[64,3072]{1,0:T(8,128)(2,1)S(1)}, u32[]{:S(2)}, u32[]{:S(2)}) collective-permute-start(bf16[64,3072]{1,0:T(8,128)(2,1)S(1)} %get-tuple-element.59), channel_id=1, source_target_pairs={{0,192},{64,0},{128,64},{192,128},{1,193},{65,1},{129,65},{193,129... | collective-permute-start | bytes 1179656 | tf_op jit(solution)/shard_map/ppermute | solution.py:31
  105.9 11.3 %collective-permute-start.15 = (bf16[128,1536]{1,0:T(8,128)(2,1)S(1)}, bf16[128,1536]{1,0:T(8,128)(2,1)S(1)}, u32[]{:S(2)}, u32[]{:S(2)}) collective-permute-start(bf16[128,1536]{1,0:T(8,128)(2,1)S(1)} %get-tuple-element.46), channel_id=1, source_target_pairs={{0,1},{1,2},{2,3},{3,0},{4,5},{5,6},{6,7},{7,4},{8,9},{9,10},{10,1... | collective-permute-start | bytes 1179656 | tf_op jit(solution)/shard_map/ppermute | solution.py:31
  108.7 8.6 %collective-permute-start.16 = (bf16[128,1536]{1,0:T(8,128)(2,1)S(1)}, bf16[128,1536]{1,0:T(8,128)(2,1)S(1)}, u32[]{:S(2)}, u32[]{:S(2)}) collective-permute-start(bf16[128,1536]{1,0:T(8,128)(2,1)S(1)} %get-tuple-element.48), channel_id=1, source_target_pairs={{0,3},{1,0},{2,1},{3,2},{4,7},{5,4},{6,5},{7,6},{8,11},{9,8},{10,9... | collective-permute-start | bytes 1179656 | tf_op jit(solution)/shard_map/ppermute | solution.py:31
  114.3 32.6 %collective-permute-start.24 = (bf16[64,6144]{1,0:T(8,128)(2,1)}, bf16[64,6144]{1,0:T(8,128)(2,1)}, u32[]{:S(2)}, u32[]{:S(2)}) collective-permute-start(bf16[64,6144]{1,0:T(8,128)(2,1)} %get-tuple-element.60), channel_id=1, source_target_pairs={{0,64},{64,128},{128,192},{192,0},{1,65},{65,129},{129,193},{193,1... | collective-permute-start | bytes 2359304 | tf_op jit(solution)/shard_map/ppermute | solution.py:31
  114.3 32.6 %collective-permute-start.25 = (bf16[64,6144]{1,0:T(8,128)(2,1)}, bf16[64,6144]{1,0:T(8,128)(2,1)}, u32[]{:S(2)}, u32[]{:S(2)}) collective-permute-start(bf16[64,6144]{1,0:T(8,128)(2,1)} %get-tuple-element.61), channel_id=1, source_target_pairs={{0,192},{64,0},{128,64},{192,128},{1,193},{65,1},{129,65},{193,129... | collective-permute-start | bytes 2359304 | tf_op jit(solution)/shard_map/ppermute | solution.py:31
  118.6 36.8 %collective-permute-start.17 = (bf16[256,1536]{1,0:T(8,128)(2,1)}, bf16[256,1536]{1,0:T(8,128)(2,1)S(1)}, u32[]{:S(2)}, u32[]{:S(2)}) collective-permute-start(bf16[256,1536]{1,0:T(8,128)(2,1)} %get-tuple-element.49), channel_id=1, source_target_pairs={{0,1},{1,2},{2,3},{3,0},{4,5},{5,6},{6,7},{7,4},{8,9},{9,10},{10,1... | collective-permute-start | bytes 2359304 | tf_op jit(solution)/shard_map/ppermute | solution.py:31
  121.6 33.7 %collective-permute-start.18 = (bf16[256,1536]{1,0:T(8,128)(2,1)}, bf16[256,1536]{1,0:T(8,128)(2,1)}, u32[]{:S(2)}, u32[]{:S(2)}) collective-permute-start(bf16[256,1536]{1,0:T(8,128)(2,1)} %get-tuple-element.50), channel_id=1, source_target_pairs={{0,3},{1,0},{2,1},{3,2},{4,7},{5,4},{6,5},{7,6},{8,11},{9,8},{10,9... | collective-permute-start | bytes 2359304 | tf_op jit(solution)/shard_map/ppermute | solution.py:31
  139.9 12.0 %all-to-all-start.4 = ((f32[8,2,128]{2,1,0:T(2,128)}), f32[8,2,128]{2,1,0:T(2,128)S(1)}, u32[]{:S(2)}, u32[]{:S(2)}) async-start(f32[8,2,128]{2,1,0:T(2,128)} %shard_map.102), calls=%async_computation.4 | async-start | bytes 16384 | tf_op jit(solution)/shard_map/all_to_all | solution.py:388
  151.9 15.8 %all-to-all-start.2 = ((bf16[4,64,1536]{2,1,0:T(8,128)(2,1)}), bf16[4,64,1536]{2,1,0:T(8,128)(2,1)S(1)}, u32[]{:S(2)}, u32[]{:S(2)}) async-start(bf16[4,64,1536]{2,1,0:T(8,128)(2,1)} %shard_map.101), calls=%async_computation.2 | async-start | bytes 1572864 | tf_op jit(solution)/shard_map/all_to_all | solution.py:399
  156.8 5.8 %collective-permute-start.19 = (bf16[64,1536]{1,0:T(8,128)(2,1)S(1)}, bf16[64,1536]{1,0:T(8,128)(2,1)S(1)}, u32[]{:S(2)}, u32[]{:S(2)}) collective-permute-start(bf16[64,1536]{1,0:T(8,128)(2,1)S(1)} %get-tuple-element.52), channel_id=1, source_target_pairs={{0,192},{64,0},{128,64},{192,128},{1,193},{65,1},{129,65},{193,129... | collective-permute-start | bytes 589832 | tf_op jit(solution)/shard_map/ppermute | solution.py:31
  158.1 8.0 %collective-permute-start.20 = (bf16[64,1536]{1,0:T(8,128)(2,1)S(1)}, bf16[64,1536]{1,0:T(8,128)(2,1)S(1)}, u32[]{:S(2)}, u32[]{:S(2)}) collective-permute-start(bf16[64,1536]{1,0:T(8,128)(2,1)S(1)} %get-tuple-element.53), channel_id=1, source_target_pairs={{0,64},{64,128},{128,192},{192,0},{1,65},{65,129},{129,193},{193,1... | collective-permute-start | bytes 589832 | tf_op jit(solution)/shard_map/ppermute | solution.py:31
  158.4 9.3 %collective-permute-start.21 = (bf16[64,1536]{1,0:T(8,128)(2,1)S(1)}, bf16[64,1536]{1,0:T(8,128)(2,1)S(1)}, u32[]{:S(2)}, u32[]{:S(2)}) collective-permute-start(bf16[64,1536]{1,0:T(8,128)(2,1)S(1)} %get-tuple-element.54), channel_id=1, source_target_pairs={{0,128},{64,192},{128,0},{192,64},{1,129},{65,193},{129,1},{193,65... | collective-permute-start | bytes 589832 | tf_op jit(solution)/shard_map/ppermute | solution.py:31
  168.7 22.2 %all-to-all-start.5 = ((bf16[16,4,3456]{2,1,0:T(4,128)(2,1)}), bf16[16,4,3456]{2,1,0:T(4,128)(2,1)S(1)}, u32[]{:S(2)}, u32[]{:S(2)}) async-start(bf16[16,4,3456]{2,1,0:T(4,128)(2,1)} %reshape.38), calls=%async_computation.5 | async-start | bytes 884736 | tf_op jit(solution)/shard_map/all_to_all | solution.py:405
  (9 other events, 10.3 us)

commit v4 on v3

--- a/solution.py
+++ b/solution.py
@@ -75,6 +75,15 @@
     width = parts.shape[2]
     for i in range(RING):
         (top_out, bot_out)[i // 2][:, (i % 2) * width : (i % 2 + 1) * width] = parts[i]
+
+
+def fetch_body(gate, up, down, gate_out, up_out, down_out, sems):
+    pairs = ((gate, gate_out), (up, up_out), (down, down_out))
+    copies = [pltpu.make_async_copy(a, b, sems.at[i]) for i, (a, b) in enumerate(pairs)]
+    for c in copies:
+        c.start()
+    for c in copies:
+        c.wait()
 
 
 def expert_body(
@@ -356,6 +365,11 @@
     full_dy = ring_gather(d_top, d_bot, "x")
 
     sem = pltpu.SemaphoreType.DMA
+    gate, up, down, _ = lax.optimization_barrier((gate, up, down, d_top))
+    gate, up, down = kernel(
+        fetch_body, tuple(sds(w.shape, BF16) for w in (gate, up, down)), gate, up, down,
+        specs=[HBM] * 3, scratch=[sem((3,))], limit=1,
+    )
     n_shards = 2 * RING * RING
     near = sds((n_rows, quarter), BF16)
     g_near = sds((n_own, RING * quarter), BF16)

time: 193 us -> 188 us (0.974)
  waiting for transfers between devices: 57 us -> 52.6 us
  local copies, waits for them, and re-layouts: 13 us -> 10 us
  starting transfers between devices: 57.1 us -> 59.7 us
    ppermute x26, waiting for transfers between devices: 37.8 us -> 32.8 us  [shift(): return lax.ppermute(a, axis, [(i, (i + n) % RING) for i in range(RING)])]
    unnamed x23 -> x19, local copies, waits for them, and re-layouts: 10.6 us -> 7.68 us
    pallas_call x12 -> x13, Pallas kernels: 21 us -> 21.7 us  [kernel(): pl.pallas_call(body, out_shape=outs, in_specs=list(specs), out_specs=out_...]
  transfers between devices with their start and end apart: 30 -> 30, of which waited for: 16 -> 14; matrix products, arithmetic and copies ran while one was open for 0% -> 0% of each run, Pallas kernels for 5% -> 5%
where the time goes in v4:
time: 188 us; the launch traced here: 187 us
  starting transfers between devices  59.7 us (32%)
  waiting for transfers between devices  52.6 us (28%)
  blocking collectives  40.1 us (21%)
  Pallas kernels  21.7 us (12%)
  local copies, waits for them, and re-layouts  10 us (5%)
    ppermute x26, starting transfers between devices, shift(): return lax.ppermute(a, axis, [(i, (i + n) % RING) for i in range(RING)])  36.8 us
    ppermute x26, waiting for transfers between devices, shift(): return lax.ppermute(a, axis, [(i, (i + n) % RING) for i in range(RING)])  32.8 us
    all_to_all x1, blocking collectives, on_device(): lax.all_to_all(jnp.concatenate([packed, packed], 0), ZAX, 0, 0, tiled=True)  24.7 us
    pallas_call x13, Pallas kernels, kernel(): pl.pallas_call(body, out_shape=outs, in_specs=list(specs), out_specs=out_...  21.7 us
    all_to_all x1, waiting for transfers between devices, on_device(): lax.all_to_all(final.reshape(2 * N_EXP, CAP, -1), ZAX, 0, 0, tiled=True)  15.6 us
    all_to_all x1, blocking collectives, on_device(): gw_all = lax.all_to_all(gw, ('x', 'zh', 'y'), 0, 0, tiled=True)  15.4 us
    all_to_all x1, starting transfers between devices, on_device(): lax.all_to_all(kernel(exchange_body, sds((N_EXP, 2, n_rows // 2), F32), g...  8.83 us
    unnamed x19, local copies, waits for them, and re-layouts  7.68 us
  transfers between devices with their start and end apart: 30, of which 14 were waited for; matrix products, arithmetic and copies ran while one was open for 0% of the time, Pallas kernels for 5%

profile of v4, /device:TPU:1, one launch (start us, length us, event | category | flops | bytes accessed | tf_op | source)
XLA Modules:
  0.0 186.8 jit_solution(4477576656243795349)
XLA Ops:
  3.8 24.7 %all_to_all.30 = bf16[16,4,3200]{2,1,0:T(4,128)(2,1)S(1)} all-to-all(bf16[16,4,3200]{2,1,0:T(4,128)(2,1)S(1)} %pad_maximum_fusion), channel_id=1, replica_groups=mesh['x'=4,'zh'=2,'zl'=4,'c'=2,'y'=4] {'zh','zl','c'}, dimensions={0} | all-to-all | bytes 819200 | tf_op jit(solution)/shard_map/all_to_all | solution.py:337
  29.5 2.7 %collective-permute-start.2 = (bf16[64,1664]{1,0:T(8,128)(2,1)S(1)}, bf16[64,1664]{1,0:T(8,128)(2,1)S(1)}, u32[]{:S(2)}, u32[]{:S(2)}) collective-permute-start(bf16[64,1664]{1,0:T(8,128)(2,1)S(1)} %get-tuple-element.43.own), channel_id=1, source_target_pairs={{0,128},{64,192},{128,0},{192,64},{1,129},{65,193},{129,1},{193,65... | collective-permute-start | bytes 638984 | tf_op jit(solution)/shard_map/ppermute | solution.py:31
  33.8 4.2 %all-to-all-start.1 = ((bf16[4,64,1536]{2,1,0:T(8,128)(2,1)}), bf16[4,64,1536]{2,1,0:T(8,128)(2,1)S(1)}, u32[]{:S(2)}, u32[]{:S(2)}) async-start(bf16[4,64,1536]{2,1,0:T(8,128)(2,1)} %get-tuple-element.46), calls=%async_computation.1 | async-start | bytes 1572864 | tf_op jit(solution)/shard_map/all_to_all | solution.py:348
  37.9 4.7 %collective-permute-done.1.right = bf16[64,1664]{1,0:T(8,128)(2,1)S(1)} collective-permute-done((bf16[64,1664]{1,0:T(8,128)(2,1)S(1)}, bf16[64,1664]{1,0:T(8,128)(2,1)S(1)}, u32[]{:S(2)}, u32[]{:S(2)}) %collective-permute-start.1) | collective-permute-done | bytes 213024 | tf_op jit(solution)/shard_map/ppermute | solution.py:31
  42.7 2.8 %collective-permute-start.5 = (bf16[128,1536]{1,0:T(8,128)(2,1)S(1)}, bf16[128,1536]{1,0:T(8,128)(2,1)S(1)}, u32[]{:S(2)}, u32[]{:S(2)}) collective-permute-start(bf16[128,1536]{1,0:T(8,128)(2,1)S(1)} %get-tuple-element.44.x0t.top), channel_id=1, source_target_pairs={{0,3},{1,0},{2,1},{3,2},{4,7},{5,4},{6,5},{7,6},{8,11},{9,8},{10,9... | collective-permute-start | bytes 1179656 | tf_op jit(solution)/shard_map/ppermute | solution.py:31
  45.5 2.7 %collective-permute-start.6 = (bf16[128,1536]{1,0:T(8,128)(2,1)S(1)}, bf16[128,1536]{1,0:T(8,128)(2,1)S(1)}, u32[]{:S(2)}, u32[]{:S(2)}) collective-permute-start(bf16[128,1536]{1,0:T(8,128)(2,1)S(1)} %get-tuple-element.45.x0b.bot), channel_id=1, source_target_pairs={{0,3},{1,0},{2,1},{3,2},{4,7},{5,4},{6,5},{7,6},{8,11},{9,8},{10,9... | collective-permute-start | bytes 1179656 | tf_op jit(solution)/shard_map/ppermute | solution.py:31
  48.2 1.8 all-to-all-done.1.parts
  50.1 2.1 %collective-permute-start.12 = (bf16[64,3072]{1,0:T(8,128)(2,1)S(1)}, bf16[64,3072]{1,0:T(8,128)(2,1)S(1)}, u32[]{:S(2)}, u32[]{:S(2)}) collective-permute-start(bf16[64,3072]{1,0:T(8,128)(2,1)S(1)} %get-tuple-element.48.d0b), channel_id=1, source_target_pairs={{0,192},{64,0},{128,64},{192,128},{1,193},{65,1},{129,65},{193,129... | collective-permute-start | bytes 1179656 | tf_op jit(solution)/shard_map/ppermute | solution.py:31
  52.3 4.7 %collective-permute-done.5.x2t = bf16[128,1536]{1,0:T(8,128)(2,1)S(1)} collective-permute-done((bf16[128,1536]{1,0:T(8,128)(2,1)S(1)}, bf16[128,1536]{1,0:T(8,128)(2,1)S(1)}, u32[]{:S(2)}, u32[]{:S(2)}) %collective-permute-start.5) | collective-permute-done | bytes 393248 | tf_op jit(solution)/shard_map/ppermute | solution.py:31
  59.1 6.3 %collective-permute-done.6.x2b = bf16[128,1536]{1,0:T(8,128)(2,1)S(1)} collective-permute-done((bf16[128,1536]{1,0:T(8,128)(2,1)S(1)}, bf16[128,1536]{1,0:T(8,128)(2,1)S(1)}, u32[]{:S(2)}, u32[]{:S(2)}) %collective-permute-start.6) | collective-permute-done | bytes 393248 | tf_op jit(solution)/shard_map/ppermute | solution.py:31
  65.4 2.1 %collective-permute-start.11 = (bf16[64,3072]{1,0:T(8,128)(2,1)S(1)}, bf16[64,3072]{1,0:T(8,128)(2,1)S(1)}, u32[]{:S(2)}, u32[]{:S(2)}) collective-permute-start(bf16[64,3072]{1,0:T(8,128)(2,1)S(1)} %get-tuple-element.47.d0t), channel_id=1, source_target_pairs={{0,192},{64,0},{128,64},{192,128},{1,193},{65,1},{129,65},{193,129... | collective-permute-start | bytes 1179656 | tf_op jit(solution)/shard_map/ppermute | solution.py:31
  67.5 1.9 %collective-permute-start.7 = (bf16[128,1536]{1,0:T(8,128)(2,1)S(1)}, bf16[128,1536]{1,0:T(8,128)(2,1)S(1)}, u32[]{:S(2)}, u32[]{:S(2)}) collective-permute-start(bf16[128,1536]{1,0:T(8,128)(2,1)S(1)} %collective-permute-done.3.x1t), channel_id=1, source_target_pairs={{0,1},{1,2},{2,3},{3,0},{4,5},{5,6},{6,7},{7,4},{8,9},{9,10},{10,1... | collective-permute-start | bytes 1179656 | tf_op jit(solution)/shard_map/ppermute | solution.py:31
  72.0 3.4 %collective-permute-done.9.d1t = bf16[64,3072]{1,0:T(8,128)(2,1)S(1)} collective-permute-done((bf16[64,3072]{1,0:T(8,128)(2,1)S(1)}, bf16[64,3072]{1,0:T(8,128)(2,1)S(1)}, u32[]{:S(2)}, u32[]{:S(2)}) %collective-permute-start.9) | collective-permute-done | bytes 393248 | tf_op jit(solution)/shard_map/ppermute | solution.py:31
  75.4 1.9 %copy-done.1 = bf16[1,6144,256]{2,1,0:T(8,128)(2,1)S(1)} copy-done((bf16[1,6144,256]{2,1,0:T(8,128)(2,1)S(1)}, bf16[1,6144,256]{2,1,0:T(8,128)(2,1)}, u32[]{:S(2)}) %copy-start.1) | copy-done | bytes 3145752
  77.3 1.9 %copy-done.2 = bf16[1,6144,256]{2,1,0:T(8,128)(2,1)S(1)} copy-done((bf16[1,6144,256]{2,1,0:T(8,128)(2,1)S(1)}, bf16[1,6144,256]{2,1,0:T(8,128)(2,1)}, u32[]{:S(2)}) %copy-start.2) | copy-done | bytes 3145752
  79.2 1.9 %copy-done.3 = bf16[1,256,6144]{2,1,0:T(8,128)(2,1)S(1)} copy-done((bf16[1,256,6144]{2,1,0:T(8,128)(2,1)S(1)}, bf16[1,256,6144]{2,1,0:T(8,128)(2,1)}, u32[]{:S(2)}) %copy-start.3) | copy-done | bytes 3145752
  86.4 10.1 %shard_map.98 = (bf16[256,1536]{1,0:T(8,128)(2,1)S(1)}, bf16[256,1536]{1,0:T(8,128)(2,1)S(1)}, bf16[256,1536]{1,0:T(8,128)(2,1)S(1)}, bf16[128,1536]{1,0:T(8,128...) custom-call(s32[4]{0:T(128)S(1)} %pad_add_fusion.at, ...), custom_call_target="tpu_custom_call" | custom-call | tf_op jit(solution)/shard_map/pallas_call | solution.py:44
  96.6 2.7 %collective-permute-start.23 = (bf16[64,3072]{1,0:T(8,128)(2,1)S(1)}, bf16[64,3072]{1,0:T(8,128)(2,1)S(1)}, u32[]{:S(2)}, u32[]{:S(2)}) collective-permute-start(bf16[64,3072]{1,0:T(8,128)(2,1)S(1)} %get-tuple-element.71), channel_id=1, source_target_pairs={{0,192},{64,0},{128,64},{192,128},{1,193},{65,1},{129,65},{193,129... | collective-permute-start | bytes 1179656 | tf_op jit(solution)/shard_map/ppermute | solution.py:31
  99.3 3.4 %collective-permute-start.15 = (bf16[128,1536]{1,0:T(8,128)(2,1)S(1)}, bf16[128,1536]{1,0:T(8,128)(2,1)S(1)}, u32[]{:S(2)}, u32[]{:S(2)}) collective-permute-start(bf16[128,1536]{1,0:T(8,128)(2,1)S(1)} %get-tuple-element.58), channel_id=1, source_target_pairs={{0,1},{1,2},{2,3},{3,0},{4,5},{5,6},{6,7},{7,4},{8,9},{9,10},{10,1... | collective-permute-start | bytes 1179656 | tf_op jit(solution)/shard_map/ppermute | solution.py:31
  102.7 2.4 %collective-permute-start.16 = (bf16[128,1536]{1,0:T(8,128)(2,1)S(1)}, bf16[128,1536]{1,0:T(8,128)(2,1)S(1)}, u32[]{:S(2)}, u32[]{:S(2)}) collective-permute-start(bf16[128,1536]{1,0:T(8,128)(2,1)S(1)} %get-tuple-element.60), channel_id=1, source_target_pairs={{0,3},{1,0},{2,1},{3,2},{4,7},{5,4},{6,5},{7,6},{8,11},{9,8},{10,9... | collective-permute-start | bytes 1179656 | tf_op jit(solution)/shard_map/ppermute | solution.py:31
  109.1 2.6 %collective-permute-done.15.up = bf16[128,1536]{1,0:T(8,128)(2,1)S(1)} collective-permute-done((bf16[128,1536]{1,0:T(8,128)(2,1)S(1)}, bf16[128,1536]{1,0:T(8,128)(2,1)S(1)}, u32[]{:S(2)}, u32[]{:S(2)}) %collective-permute-start.15) | collective-permute-done | bytes 393248 | tf_op jit(solution)/shard_map/ppermute | solution.py:31
  114.3 3.0 %collective-permute-start.18 = (bf16[256,1536]{1,0:T(8,128)(2,1)}, bf16[256,1536]{1,0:T(8,128)(2,1)}, u32[]{:S(2)}, u32[]{:S(2)}) collective-permute-start(bf16[256,1536]{1,0:T(8,128)(2,1)} %get-tuple-element.62), channel_id=1, source_target_pairs={{0,3},{1,0},{2,1},{3,2},{4,7},{5,4},{6,5},{7,6},{8,11},{9,8},{10,9... | collective-permute-start | bytes 2359304 | tf_op jit(solution)/shard_map/ppermute | solution.py:31
  117.3 15.4 %all_to_all.31.gw_all = f32[32,2,128]{2,1,0:T(2,128)S(1)} all-to-all(f32[32,2,128]{2,1,0:T(2,128)S(1)} %get-tuple-element.74), channel_id=1, replica_groups=mesh['x'=4,'zh'=2,'zl'=4,'c'=2,'y'=4] {'x','zh','y'}, dimensions={0} | all-to-all | bytes 65536 | tf_op jit(solution)/shard_map/all_to_all | solution.py:401
  133.3 8.8 %all-to-all-start.4 = ((f32[8,2,128]{2,1,0:T(2,128)}), f32[8,2,128]{2,1,0:T(2,128)S(1)}, u32[]{:S(2)}, u32[]{:S(2)}) async-start(f32[8,2,128]{2,1,0:T(2,128)} %shard_map.103), calls=%async_computation.4 | async-start | bytes 16384 | tf_op jit(solution)/shard_map/all_to_all | solution.py:402
  142.2 2.5 %shard_map.102 = bf16[4,64,1536]{2,1,0:T(8,128)(2,1)} custom-call(bf16[64,6144]{1,0:T(8,128)(2,1)S(1)} %get-tuple-element.67.a, bf16[64,6144]{1,0:T(8,128)(2,1)} %collective-permute-done.24.b, bf16[64,6144]{1,0:T(8,128)(2,1)} %collective-permute-done.25.c), custom_call_target="tpu_custom_call" | custom-call | tf_op jit(solution)/shard_map/pallas_call | solution.py:44
  144.7 2.4 %all-to-all-done.4 = f32[8,2,128]{2,1,0:T(2,128)S(1)} async-done(((f32[8,2,128]{2,1,0:T(2,128)}), f32[8,2,128]{2,1,0:T(2,128)S(1)}, u32[]{:S(2)}, u32[]{:S(2)}) %all-to-all-start.4) | async-done | bytes 8224 | tf_op jit(solution)/shard_map/all_to_all | solution.py:402
  147.1 3.5 %all-to-all-start.2 = ((bf16[4,64,1536]{2,1,0:T(8,128)(2,1)}), bf16[4,64,1536]{2,1,0:T(8,128)(2,1)S(1)}, u32[]{:S(2)}, u32[]{:S(2)}) async-start(bf16[4,64,1536]{2,1,0:T(8,128)(2,1)} %shard_map.102), calls=%async_computation.2 | async-start | bytes 1572864 | tf_op jit(solution)/shard_map/all_to_all | solution.py:413
  156.1 1.8 collective-permute-done.19.a1
  157.8 2.9 %collective-permute-done.20.a2 = bf16[64,1536]{1,0:T(8,128)(2,1)S(1)} collective-permute-done((bf16[64,1536]{1,0:T(8,128)(2,1)S(1)}, bf16[64,1536]{1,0:T(8,128)(2,1)S(1)}, u32[]{:S(2)}, u32[]{:S(2)}) %collective-permute-start.20) | collective-permute-done | bytes 196640 | tf_op jit(solution)/shard_map/ppermute | solution.py:31
  160.7 2.0 %collective-permute-done.21.a3 = bf16[64,1536]{1,0:T(8,128)(2,1)S(1)} collective-permute-done((bf16[64,1536]{1,0:T(8,128)(2,1)S(1)}, bf16[64,1536]{1,0:T(8,128)(2,1)S(1)}, u32[]{:S(2)}, u32[]{:S(2)}) %collective-permute-start.21) | collective-permute-done | bytes 196640 | tf_op jit(solution)/shard_map/ppermute | solution.py:31
  163.8 6.3 %all-to-all-start.5 = ((bf16[16,4,3456]{2,1,0:T(4,128)(2,1)}), bf16[16,4,3456]{2,1,0:T(4,128)(2,1)S(1)}, u32[]{:S(2)}, u32[]{:S(2)}) async-start(bf16[16,4,3456]{2,1,0:T(4,128)(2,1)} %reshape.38), calls=%async_computation.5 | async-start | bytes 884736 | tf_op jit(solution)/shard_map/all_to_all | solution.py:419
  170.2 15.6 %all-to-all-done.5 = bf16[16,4,3456]{2,1,0:T(4,128)(2,1)S(1)} async-done(((bf16[16,4,3456]{2,1,0:T(4,128)(2,1)}), bf16[16,4,3456]{2,1,0:T(4,128)(2,1)S(1)}, u32[]{:S(2)}, u32[]{:S(2)}) %all-to-all-start.5) | async-done | bytes 442400 | tf_op jit(solution)/shard_map/all_to_all | solution.py:419
  (83 shorter events, 30.7 us)
Async XLA Ops:
  29.5 8.4 %collective-permute-start.2 = (bf16[64,1664]{1,0:T(8,128)(2,1)S(1)}, bf16[64,1664]{1,0:T(8,128)(2,1)S(1)}, u32[]{:S(2)}, u32[]{:S(2)}) collective-permute-start(bf16[64,1664]{1,0:T(8,128)(2,1)S(1)} %get-tuple-element.43.own), channel_id=1, source_target_pairs={{0,128},{64,192},{128,0},{192,64},{1,129},{65,193},{129,1},{193,65... | collective-permute-start | bytes 638984 | tf_op jit(solution)/shard_map/ppermute | solution.py:31
  32.3 10.4 %collective-permute-start.1 = (bf16[64,1664]{1,0:T(8,128)(2,1)S(1)}, bf16[64,1664]{1,0:T(8,128)(2,1)S(1)}, u32[]{:S(2)}, u32[]{:S(2)}) collective-permute-start(bf16[64,1664]{1,0:T(8,128)(2,1)S(1)} %get-tuple-element.43.own), channel_id=1, source_target_pairs={{0,192},{64,0},{128,64},{192,128},{1,193},{65,1},{129,65},{193,129... | collective-permute-start | bytes 638984 | tf_op jit(solution)/shard_map/ppermute | solution.py:31
  33.1 9.5 %collective-permute-start = (bf16[64,1664]{1,0:T(8,128)(2,1)S(1)}, bf16[64,1664]{1,0:T(8,128)(2,1)S(1)}, u32[]{:S(2)}, u32[]{:S(2)}) collective-permute-start(bf16[64,1664]{1,0:T(8,128)(2,1)S(1)} %get-tuple-element.43.own), channel_id=1, source_target_pairs={{0,64},{64,128},{128,192},{192,0},{1,65},{65,129},{129,193},{193,1... | collective-permute-start | bytes 638984 | tf_op jit(solution)/shard_map/ppermute | solution.py:31
  33.8 16.3 %all-to-all-start.1 = ((bf16[4,64,1536]{2,1,0:T(8,128)(2,1)}), bf16[4,64,1536]{2,1,0:T(8,128)(2,1)S(1)}, u32[]{:S(2)}, u32[]{:S(2)}) async-start(bf16[4,64,1536]{2,1,0:T(8,128)(2,1)} %get-tuple-element.46), calls=%async_computation.1 | async-start | bytes 1572864 | tf_op jit(solution)/shard_map/all_to_all | solution.py:348
  42.7 14.3 %collective-permute-start.5 = (bf16[128,1536]{1,0:T(8,128)(2,1)S(1)}, bf16[128,1536]{1,0:T(8,128)(2,1)S(1)}, u32[]{:S(2)}, u32[]{:S(2)}) collective-permute-start(bf16[128,1536]{1,0:T(8,128)(2,1)S(1)} %get-tuple-element.44.x0t.top), channel_id=1, source_target_pairs={{0,3},{1,0},{2,1},{3,2},{4,7},{5,4},{6,5},{7,6},{8,11},{9,8},{10,9... | collective-permute-start | bytes 1179656 | tf_op jit(solution)/shard_map/ppermute | solution.py:31
  45.5 13.5 %collective-permute-start.3 = (bf16[128,1536]{1,0:T(8,128)(2,1)S(1)}, bf16[128,1536]{1,0:T(8,128)(2,1)S(1)}, u32[]{:S(2)}, u32[]{:S(2)}) collective-permute-start(bf16[128,1536]{1,0:T(8,128)(2,1)S(1)} %get-tuple-element.44.x0t.top), channel_id=1, source_target_pairs={{0,1},{1,2},{2,3},{3,0},{4,5},{5,6},{6,7},{7,4},{8,9},{9,10},{10,1... | collective-permute-start | bytes 1179656 | tf_op jit(solution)/shard_map/ppermute | solution.py:31
  45.5 19.9 %collective-permute-start.6 = (bf16[128,1536]{1,0:T(8,128)(2,1)S(1)}, bf16[128,1536]{1,0:T(8,128)(2,1)S(1)}, u32[]{:S(2)}, u32[]{:S(2)}) collective-permute-start(bf16[128,1536]{1,0:T(8,128)(2,1)S(1)} %get-tuple-element.45.x0b.bot), channel_id=1, source_target_pairs={{0,3},{1,0},{2,1},{3,2},{4,7},{5,4},{6,5},{7,6},{8,11},{9,8},{10,9... | collective-permute-start | bytes 1179656 | tf_op jit(solution)/shard_map/ppermute | solution.py:31
  48.2 19.3 %collective-permute-start.4 = (bf16[128,1536]{1,0:T(8,128)(2,1)S(1)}, bf16[128,1536]{1,0:T(8,128)(2,1)S(1)}, u32[]{:S(2)}, u32[]{:S(2)}) collective-permute-start(bf16[128,1536]{1,0:T(8,128)(2,1)S(1)} %get-tuple-element.45.x0b.bot), channel_id=1, source_target_pairs={{0,1},{1,2},{2,3},{3,0},{4,5},{5,6},{6,7},{7,4},{8,9},{9,10},{10,1... | collective-permute-start | bytes 1179656 | tf_op jit(solution)/shard_map/ppermute | solution.py:31
  50.1 19.3 %collective-permute-start.12 = (bf16[64,3072]{1,0:T(8,128)(2,1)S(1)}, bf16[64,3072]{1,0:T(8,128)(2,1)S(1)}, u32[]{:S(2)}, u32[]{:S(2)}) collective-permute-start(bf16[64,3072]{1,0:T(8,128)(2,1)S(1)} %get-tuple-element.48.d0b), channel_id=1, source_target_pairs={{0,192},{64,0},{128,64},{192,128},{1,193},{65,1},{129,65},{193,129... | collective-permute-start | bytes 1179656 | tf_op jit(solution)/shard_map/ppermute | solution.py:31
  57.0 13.6 %collective-permute-start.10 = (bf16[64,3072]{1,0:T(8,128)(2,1)S(1)}, bf16[64,3072]{1,0:T(8,128)(2,1)S(1)}, u32[]{:S(2)}, u32[]{:S(2)}) collective-permute-start(bf16[64,3072]{1,0:T(8,128)(2,1)S(1)} %get-tuple-element.48.d0b), channel_id=1, source_target_pairs={{0,64},{64,128},{128,192},{192,0},{1,65},{65,129},{129,193},{193,1... | collective-permute-start | bytes 1179656 | tf_op jit(solution)/shard_map/ppermute | solution.py:31
  59.0 16.4 %collective-permute-start.9 = (bf16[64,3072]{1,0:T(8,128)(2,1)S(1)}, bf16[64,3072]{1,0:T(8,128)(2,1)S(1)}, u32[]{:S(2)}, u32[]{:S(2)}) collective-permute-start(bf16[64,3072]{1,0:T(8,128)(2,1)S(1)} %get-tuple-element.47.d0t), channel_id=1, source_target_pairs={{0,64},{64,128},{128,192},{192,0},{1,65},{65,129},{129,193},{193,1... | collective-permute-start | bytes 1179656 | tf_op jit(solution)/shard_map/ppermute | solution.py:31
  65.4 16.3 %copy-start.4 = (bf16[128,1536]{1,0:T(8,128)(2,1)}, bf16[128,1536]{1,0:T(8,128)(2,1)S(1)}, u32[]{:S(2)}) copy-start(bf16[128,1536]{1,0:T(8,128)(2,1)S(1)} %collective-permute-done.6.x2b) | copy-start | bytes 1179652
  65.4 16.3 %collective-permute-start.11 = (bf16[64,3072]{1,0:T(8,128)(2,1)S(1)}, bf16[64,3072]{1,0:T(8,128)(2,1)S(1)}, u32[]{:S(2)}, u32[]{:S(2)}) collective-permute-start(bf16[64,3072]{1,0:T(8,128)(2,1)S(1)} %get-tuple-element.47.d0t), channel_id=1, source_target_pairs={{0,192},{64,0},{128,64},{192,128},{1,193},{65,1},{129,65},{193,129... | collective-permute-start | bytes 1179656 | tf_op jit(solution)/shard_map/ppermute | solution.py:31
  67.5 14.3 %copy-start.6 = (bf16[128,1536]{1,0:T(8,128)(2,1)}, bf16[128,1536]{1,0:T(8,128)(2,1)S(1)}, u32[]{:S(2)}) copy-start(bf16[128,1536]{1,0:T(8,128)(2,1)S(1)} %collective-permute-done.4.x1b) | copy-start | bytes 1179652
  67.5 14.3 %collective-permute-start.7 = (bf16[128,1536]{1,0:T(8,128)(2,1)S(1)}, bf16[128,1536]{1,0:T(8,128)(2,1)S(1)}, u32[]{:S(2)}, u32[]{:S(2)}) collective-permute-start(bf16[128,1536]{1,0:T(8,128)(2,1)S(1)} %collective-permute-done.3.x1t), channel_id=1, source_target_pairs={{0,1},{1,2},{2,3},{3,0},{4,5},{5,6},{6,7},{7,4},{8,9},{9,10},{10,1... | collective-permute-start | bytes 1179656 | tf_op jit(solution)/shard_map/ppermute | solution.py:31
  69.4 12.4 %collective-permute-start.8 = (bf16[128,1536]{1,0:T(8,128)(2,1)S(1)}, bf16[128,1536]{1,0:T(8,128)(2,1)S(1)}, u32[]{:S(2)}, u32[]{:S(2)}) collective-permute-start(bf16[128,1536]{1,0:T(8,128)(2,1)S(1)} %collective-permute-done.6.x2b), channel_id=1, source_target_pairs={{0,3},{1,0},{2,1},{3,2},{4,7},{5,4},{6,5},{7,6},{8,11},{9,8},{10,9... | collective-permute-start | bytes 1179656 | tf_op jit(solution)/shard_map/ppermute | solution.py:31
  70.6 12.7 %collective-permute-start.14 = (bf16[64,3072]{1,0:T(8,128)(2,1)S(1)}, bf16[64,3072]{1,0:T(8,128)(2,1)S(1)}, u32[]{:S(2)}, u32[]{:S(2)}) collective-permute-start(bf16[64,3072]{1,0:T(8,128)(2,1)S(1)} %collective-permute-done.12.d2b), channel_id=1, source_target_pairs={{0,192},{64,0},{128,64},{192,128},{1,193},{65,1},{129,65},{193,129... | collective-permute-start | bytes 1179656 | tf_op jit(solution)/shard_map/ppermute | solution.py:31
  75.4 9.1 %collective-permute-start.13 = (bf16[64,3072]{1,0:T(8,128)(2,1)S(1)}, bf16[64,3072]{1,0:T(8,128)(2,1)S(1)}, u32[]{:S(2)}, u32[]{:S(2)}) collective-permute-start(bf16[64,3072]{1,0:T(8,128)(2,1)S(1)} %collective-permute-done.9.d1t), channel_id=1, source_target_pairs={{0,64},{64,128},{128,192},{192,0},{1,65},{65,129},{129,193},{193,1... | collective-permute-start | bytes 1179656 | tf_op jit(solution)/shard_map/ppermute | solution.py:31
  96.6 8.6 %collective-permute-start.22 = (bf16[64,3072]{1,0:T(8,128)(2,1)S(1)}, bf16[64,3072]{1,0:T(8,128)(2,1)S(1)}, u32[]{:S(2)}, u32[]{:S(2)}) collective-permute-start(bf16[64,3072]{1,0:T(8,128)(2,1)S(1)} %get-tuple-element.69), channel_id=1, source_target_pairs={{0,64},{64,128},{128,192},{192,0},{1,65},{65,129},{129,193},{193,1... | collective-permute-start | bytes 1179656 | tf_op jit(solution)/shard_map/ppermute | solution.py:31
  96.6 8.5 %collective-permute-start.23 = (bf16[64,3072]{1,0:T(8,128)(2,1)S(1)}, bf16[64,3072]{1,0:T(8,128)(2,1)S(1)}, u32[]{:S(2)}, u32[]{:S(2)}) collective-permute-start(bf16[64,3072]{1,0:T(8,128)(2,1)S(1)} %get-tuple-element.71), channel_id=1, source_target_pairs={{0,192},{64,0},{128,64},{192,128},{1,193},{65,1},{129,65},{193,129... | collective-permute-start | bytes 1179656 | tf_op jit(solution)/shard_map/ppermute | solution.py:31
  99.3 12.4 %collective-permute-start.15 = (bf16[128,1536]{1,0:T(8,128)(2,1)S(1)}, bf16[128,1536]{1,0:T(8,128)(2,1)S(1)}, u32[]{:S(2)}, u32[]{:S(2)}) collective-permute-start(bf16[128,1536]{1,0:T(8,128)(2,1)S(1)} %get-tuple-element.58), channel_id=1, source_target_pairs={{0,1},{1,2},{2,3},{3,0},{4,5},{5,6},{6,7},{7,4},{8,9},{9,10},{10,1... | collective-permute-start | bytes 1179656 | tf_op jit(solution)/shard_map/ppermute | solution.py:31
  102.7 8.9 %collective-permute-start.16 = (bf16[128,1536]{1,0:T(8,128)(2,1)S(1)}, bf16[128,1536]{1,0:T(8,128)(2,1)S(1)}, u32[]{:S(2)}, u32[]{:S(2)}) collective-permute-start(bf16[128,1536]{1,0:T(8,128)(2,1)S(1)} %get-tuple-element.60), channel_id=1, source_target_pairs={{0,3},{1,0},{2,1},{3,2},{4,7},{5,4},{6,5},{7,6},{8,11},{9,8},{10,9... | collective-permute-start | bytes 1179656 | tf_op jit(solution)/shard_map/ppermute | solution.py:31
  106.5 35.7 %collective-permute-start.24 = (bf16[64,6144]{1,0:T(8,128)(2,1)}, bf16[64,6144]{1,0:T(8,128)(2,1)}, u32[]{:S(2)}, u32[]{:S(2)}) collective-permute-start(bf16[64,6144]{1,0:T(8,128)(2,1)} %get-tuple-element.72), channel_id=1, source_target_pairs={{0,64},{64,128},{128,192},{192,0},{1,65},{65,129},{129,193},{193,1... | collective-permute-start | bytes 2359304 | tf_op jit(solution)/shard_map/ppermute | solution.py:31
  108.1 34.1 %collective-permute-start.25 = (bf16[64,6144]{1,0:T(8,128)(2,1)}, bf16[64,6144]{1,0:T(8,128)(2,1)}, u32[]{:S(2)}, u32[]{:S(2)}) collective-permute-start(bf16[64,6144]{1,0:T(8,128)(2,1)} %get-tuple-element.73), channel_id=1, source_target_pairs={{0,192},{64,0},{128,64},{192,128},{1,193},{65,1},{129,65},{193,129... | collective-permute-start | bytes 2359304 | tf_op jit(solution)/shard_map/ppermute | solution.py:31
  113.0 37.6 %collective-permute-start.17 = (bf16[256,1536]{1,0:T(8,128)(2,1)}, bf16[256,1536]{1,0:T(8,128)(2,1)S(1)}, u32[]{:S(2)}, u32[]{:S(2)}) collective-permute-start(bf16[256,1536]{1,0:T(8,128)(2,1)} %get-tuple-element.61), channel_id=1, source_target_pairs={{0,1},{1,2},{2,3},{3,0},{4,5},{5,6},{6,7},{7,4},{8,9},{9,10},{10,1... | collective-permute-start | bytes 2359304 | tf_op jit(solution)/shard_map/ppermute | solution.py:31
  114.3 36.3 %collective-permute-start.18 = (bf16[256,1536]{1,0:T(8,128)(2,1)}, bf16[256,1536]{1,0:T(8,128)(2,1)}, u32[]{:S(2)}, u32[]{:S(2)}) collective-permute-start(bf16[256,1536]{1,0:T(8,128)(2,1)} %get-tuple-element.62), channel_id=1, source_target_pairs={{0,3},{1,0},{2,1},{3,2},{4,7},{5,4},{6,5},{7,6},{8,11},{9,8},{10,9... | collective-permute-start | bytes 2359304 | tf_op jit(solution)/shard_map/ppermute | solution.py:31
  133.3 13.8 %all-to-all-start.4 = ((f32[8,2,128]{2,1,0:T(2,128)}), f32[8,2,128]{2,1,0:T(2,128)S(1)}, u32[]{:S(2)}, u32[]{:S(2)}) async-start(f32[8,2,128]{2,1,0:T(2,128)} %shard_map.103), calls=%async_computation.4 | async-start | bytes 16384 | tf_op jit(solution)/shard_map/all_to_all | solution.py:402
  147.1 15.7 %all-to-all-start.2 = ((bf16[4,64,1536]{2,1,0:T(8,128)(2,1)}), bf16[4,64,1536]{2,1,0:T(8,128)(2,1)S(1)}, u32[]{:S(2)}, u32[]{:S(2)}) async-start(bf16[4,64,1536]{2,1,0:T(8,128)(2,1)} %shard_map.102), calls=%async_computation.2 | async-start | bytes 1572864 | tf_op jit(solution)/shard_map/all_to_all | solution.py:413
  152.0 5.8 %collective-permute-start.19 = (bf16[64,1536]{1,0:T(8,128)(2,1)S(1)}, bf16[64,1536]{1,0:T(8,128)(2,1)S(1)}, u32[]{:S(2)}, u32[]{:S(2)}) collective-permute-start(bf16[64,1536]{1,0:T(8,128)(2,1)S(1)} %get-tuple-element.64), channel_id=1, source_target_pairs={{0,192},{64,0},{128,64},{192,128},{1,193},{65,1},{129,65},{193,129... | collective-permute-start | bytes 589832 | tf_op jit(solution)/shard_map/ppermute | solution.py:31
  153.0 7.7 %collective-permute-start.20 = (bf16[64,1536]{1,0:T(8,128)(2,1)S(1)}, bf16[64,1536]{1,0:T(8,128)(2,1)S(1)}, u32[]{:S(2)}, u32[]{:S(2)}) collective-permute-start(bf16[64,1536]{1,0:T(8,128)(2,1)S(1)} %get-tuple-element.65), channel_id=1, source_target_pairs={{0,64},{64,128},{128,192},{192,0},{1,65},{65,129},{129,193},{193,1... | collective-permute-start | bytes 589832 | tf_op jit(solution)/shard_map/ppermute | solution.py:31
  153.6 9.2 %collective-permute-start.21 = (bf16[64,1536]{1,0:T(8,128)(2,1)S(1)}, bf16[64,1536]{1,0:T(8,128)(2,1)S(1)}, u32[]{:S(2)}, u32[]{:S(2)}) collective-permute-start(bf16[64,1536]{1,0:T(8,128)(2,1)S(1)} %get-tuple-element.66), channel_id=1, source_target_pairs={{0,128},{64,192},{128,0},{192,64},{1,129},{65,193},{129,1},{193,65... | collective-permute-start | bytes 589832 | tf_op jit(solution)/shard_map/ppermute | solution.py:31
  163.8 22.0 %all-to-all-start.5 = ((bf16[16,4,3456]{2,1,0:T(4,128)(2,1)}), bf16[16,4,3456]{2,1,0:T(4,128)(2,1)S(1)}, u32[]{:S(2)}, u32[]{:S(2)}) async-start(bf16[16,4,3456]{2,1,0:T(4,128)(2,1)} %reshape.38), calls=%async_computation.5 | async-start | bytes 884736 | tf_op jit(solution)/shard_map/all_to_all | solution.py:419
  (7 other events, 12.6 us)
